TPU v7x, 512 devices: a whole 4x8x8 slice. The times are simulated.
512 devices in a mesh: row: 32 (over y_lo, z), col: 16 (over y_hi, x, core).
Axes of the slice: x: 4, y: 8 (y_hi: 2, y_lo: 4; y = y_hi * 4 + y_lo), z: 8, core: 2. Of those that a mesh axis runs over, the one named last changes fastest.
Arguments:
- a_blocks: bfloat16 [32, 16, 4, 3, 256, 256], P('row', 'col'), may hold values from -0.15625 to 0.15625
- a_columns: int32 [32, 16, 4, 3], P('row', 'col'), may hold values from 0 to 3, as said below
- a_live: int32 [32, 16, 4], P('row', 'col'), may hold values from 1 to 3, as said below
- owner_map: int32 [16, 2], P('col'), may hold values from 0 to 31, as said below
- b_blocks: bfloat16 [32, 16, 4, 256, 512], P('row', 'col'), may hold values from -6 to 6
- b_columns: int32 [32, 16, 4, 2], P('row', 'col'), may hold values from 0 to 3, as said below
Outputs:
- product_window: bfloat16 [32, 16, 4, 256, 1024], P('row', 'col')
Inputs may be any that keep to these rules, and one draw needn't show every extreme that they name: `a_columns`: the 3 inner indices in a block row of an A tile differ. `a_live`: every A tile has a block row with 3 live slots. `owner_map`: the two grid rows named for a grid column differ. `b_columns`: the 2 block columns in a row of a B tile differ.
All inputs are finite; a program needn't handle non-finite values.
Results may differ from a plain program's by a relative error of at most 0.001.
Values may be sent and summed in bfloat16 or wider, within the bound.
No kernel may reach another device: no remote copies, remote signals or barrier semaphores. Data moves between devices by JAX's collectives and lax.ppermute only.
A program may use at most 64 MiB of HBM per device.

v0:
```python
import jax
import jax.numpy as jnp
from jax import lax
from jax.sharding import PartitionSpec as P

NB = 4


def spread(value, axis, root):
    mine = lax.axis_index(axis) == root
    return lax.psum(jnp.where(mine, value, jnp.zeros_like(value)), axis)


def shifted(block, axis, distance):
    devices = range(lax.axis_size(axis))
    route = [((i - distance) % len(devices), i) for i in devices]
    return lax.ppermute(block, axis, route)


def section_term(a_tile, b_tile):
    blocks, columns, live_count = a_tile
    b_rows, b_targets = b_tile
    rows_count = blocks.shape[0]
    slot_count = blocks.shape[1]
    block_width = blocks.shape[2]
    pair_count = b_targets.shape[1]
    block_ids = jnp.arange(NB, dtype=jnp.int32)
    slot_index = jnp.arange(slot_count, dtype=jnp.int32)
    live_mask = slot_index[None, :] < live_count[:, None]
    masked = jnp.where(live_mask[:, :, None, None], blocks, jnp.zeros_like(blocks))
    picked = b_rows[columns]
    partial_products = jnp.einsum(
        "iaxy,iayw->iaxw", masked, picked, preferred_element_type=jnp.float32
    )
    targets = b_targets[columns]
    select = (targets[..., None] == block_ids).astype(jnp.float32)
    shaped = partial_products.reshape(rows_count, slot_count, block_width, pair_count, block_width)
    placed = jnp.einsum("iaxtz,iatj->ixjz", shaped, select, precision=lax.Precision.HIGHEST)
    return placed.reshape(rows_count, block_width, NB * block_width)


def shared_tile(local_a, holder):
    return (
        spread(local_a[0], "row", holder),
        spread(local_a[1], "row", holder),
        spread(local_a[2], "row", holder),
    )


def on_device(a_blocks, a_columns, a_live, owner_map, b_blocks, b_columns):
    local_a = (a_blocks[0, 0], a_columns[0, 0], a_live[0, 0])
    local_b = (b_blocks[0, 0], b_columns[0, 0])
    first_a = shared_tile(local_a, owner_map[0, 0])
    second_a = shared_tile(local_a, owner_map[0, 1])
    next_b = shifted((local_b[0], local_b[1]), "col", -1)
    summed = section_term(first_a, local_b) + section_term(second_a, next_b)
    rows_count = summed.shape[0]
    return summed.astype(jnp.bfloat16).reshape(1, 1, rows_count, summed.shape[1], summed.shape[2])


def solution(mesh):
    placed = (
        P("row", "col", None, None, None, None),
        P("row", "col", None, None),
        P("row", "col", None),
        P("col", None),
        P("row", "col", None, None, None),
        P("row", "col", None, None),
    )
    return jax.shard_map(
        on_device,
        mesh=mesh,
        in_specs=placed,
        out_specs=P("row", "col", None, None, None),
        check_vma=False,
    )
```

profile of v0, /device:TPU:6, one launch (start us, length us, event | category | flops | bytes accessed | tf_op | source)
XLA Modules:
  0.0 406.1 jit_solution(15529518619099587491)
XLA Ops:
  6.5 0.0 all-reduce.4.cloned.1.call-start
  6.5 1.4 fusion.28
  9.2 0.0 copy-start.2
  9.2 0.0 copy-start.1
  9.2 0.0 copy-start.3
  9.2 3.3 select_bitcast_fusion.1
  12.5 0.0 all-reduce.4.cloned.1.call-update
  12.6 2.2 collective-permute-start.1
  14.7 0.0 copy-done.2
  14.8 0.1 copy.18
  14.9 2.6 collective-permute-start
  17.4 0.0 copy-done.1
  17.5 0.1 copy.23
  17.6 0.1 copy.17
  17.6 0.0 copy-done.3
  17.6 26.7 %all-reduce = (s32[4,3]{1,0:T(4,128)S(1)}, s32[4]{0:T(128)S(1)}, s32[4,3]{1,0:T(4,128)S(1)}, s32[4]{0:T(128)S(1)}) all-reduce(s32[4,3]{1,0:T(4,128)S(1)} %bitcast.52, s32[4]{0:T(128)S(1)} %get-tuple-element.16, s32[4,3]{1,0:T(4,128)S(1)} %bitcast.53, s32[4]{0:T(128)S(1)} %get-tuple-element.15), channel_id=1, replica_groups=mesh['row'=32,'col'=16] {'row'}, use_global_device_ids=true, to_apply=%region_3.4 | all-reduce | flops 32 | bytes 256 | tf_op jit(solution)/shard_map/psum | solution.py:11
  44.3 0.1 reshape.97
  44.4 2.0 gather_fusion.1
  46.4 0.6 gather_fusion
  46.9 0.1 reshape.113
  47.0 0.1 copy.19
  47.1 0.1 reshape.96
  47.2 0.1 iota_compare_fusion.2
  47.3 0.1 iota_compare_fusion.3
  47.4 0.0 collective-permute-done
  47.4 0.6 gather_fusion.2
  47.9 0.1 copy.24
  48.0 0.1 reshape.112
  48.1 0.0 collective-permute-done.1
  48.1 3.7 gather_fusion.3
  51.8 288.1 %all-reduce.4.cloned.1.call-done = (bf16[4,3,256,256]{3,2,1,0:T(8,128)(2,1)}, bf16[4,3,256,256]{3,2,1,0:T(8,128)(2,1)}) async-done(((bf16[4,3,256,256]{3,2,1,0:T(8,128)(2,1)}, bf16[4,3,256,256]{3,2,1,0:T(8,128)(2,1)}), (bf16[4,3,256,256]{3,2,1,0:T(8,128)(2,1)}, bf16[4,3,256,256]{3,2,1,0:T(8,128)(2,1)})) %all-reduce.4.cloned.1.call-update) | async-done | bytes 3145744 | tf_op jit(solution)/shard_map/psum | solution.py:11
  339.9 6.0 %fusion.10 = f32[4,3,256,512]{3,2,1,0:T(8,128)} fusion(bf16[4,3,256,512]{3,2,1,0:T(8,128)(2,1)} %bitcast.51, bf16[4,3,256,256]{3,2,1,0:T(8,128)(2,1)} %get-tuple-element.9, pred[4,3]{1,0:T(4,128)(4,1)S(1)} %iota_compare_fusion.2), kind=kOutput, calls=%fused_computation.11 | convolution fusion | flops 806092800 | bytes 11010060 | tf_op jit(solution)/shard_map/iaxy,iayw->iaxw/dot_general | solution.py:32
  345.9 8.2 %reshape.94 = f32[4,3,256,2,256]{4,3,2,1,0:T(2,128)} reshape(f32[4,3,256,512]{3,2,1,0:T(8,128)} %fusion.10) | data formatting | bytes 12582912 | tf_op jit(solution)/shard_map/reshape | solution.py:37
  354.2 5.1 %fusion.12 = f32[4,3,256,512]{3,2,1,0:T(8,128)} fusion(bf16[4,3,256,512]{3,2,1,0:T(8,128)(2,1)S(1)} %bitcast.50, bf16[4,3,256,256]{3,2,1,0:T(8,128)(2,1)} %get-tuple-element.10, pred[4,3]{1,0:T(4,128)(4,1)S(1)} %iota_compare_fusion.3), kind=kOutput, calls=%fused_computation.14 | convolution fusion | flops 806092800 | bytes 11010060 | tf_op jit(solution)/shard_map/iaxy,iayw->iaxw/dot_general | solution.py:32
  359.2 8.2 %reshape.93 = f32[4,3,256,2,256]{4,3,2,1,0:T(2,128)} reshape(f32[4,3,256,512]{3,2,1,0:T(8,128)} %fusion.12) | data formatting | bytes 12582912 | tf_op jit(solution)/shard_map/reshape | solution.py:37
  367.5 0.0 copy-start
  367.5 16.9 %fusion = f32[4,4,256,256,1]{3,1,4,2,0:T(4,128)S(1)} fusion(f32[4,3,256,2,256]{4,3,2,1,0:T(2,128)} %reshape.94, s32[4,3,2]{1,2,0:T(2,128)S(1)} %copy.25), kind=kOutput, calls=%fused_computation.4 | convolution fusion | flops 75497568 | bytes 10485856 | tf_op jit(solution)/shard_map/iaxtz,iatj->ixjz/dot_general | solution.py:38
  384.4 0.0 copy-done
  384.4 12.2 %fusion.7 = bf16[4,256,4,256]{3,2,1,0:T(4,128)(2,1)S(1)} fusion(f32[4,4,256,256,1]{3,1,4,2,0:T(4,128)S(1)} %fusion, f32[4,3,256,2,256]{4,3,2,1,0:T(2,128)S(1)} %copy-done, s32[4,3,2]{1,2,0:T(2,128)S(1)} %copy.20), kind=kOutput, calls=%fused_computation.10 | convolution fusion | flops 77594720 | bytes 12583008 | tf_op jit(solution)/shard_map/iaxtz,iatj->ixjz/dot_general | solution.py:38
  396.6 2.7 convert_element_type.20
  (7 shorter events, 0.0 us)
Async XLA Ops:
  6.5 333.4 %all-reduce.4.cloned.1.call-start = ((), (), s32[]{:S(2)}) async-start(), calls=%async_computation | async-start | bytes 6291456 | tf_op jit(solution)/shard_map/psum | solution.py:11
  9.2 5.6 %copy-start.2 = (s32[1,1,4,2]{2,3,1,0:T(2,128)S(1)}, s32[1,1,4,2]{2,3,1,0:T(2,128)}, u32[]{:S(2)}) copy-start(s32[1,1,4,2]{2,3,1,0:T(2,128)} %param.11) | copy-start | bytes 100
  9.2 8.2 %copy-start.1 = (s32[1,1,4,3]{2,1,3,0:T(1,128)S(1)}, s32[1,1,4,3]{2,1,3,0:T(1,128)}, u32[]{:S(2)}) copy-start(s32[1,1,4,3]{2,1,3,0:T(1,128)} %param.7) | copy-start | bytes 148
  9.2 8.4 %copy-start.3 = (s32[1,1,4]{2,1,0:T(1,128)S(1)}, s32[1,1,4]{2,1,0:T(1,128)}, u32[]{:S(2)}) copy-start(s32[1,1,4]{2,1,0:T(1,128)} %param.8) | copy-start | bytes 52
  12.6 35.6 %collective-permute-start.1 = (bf16[4,256,512]{2,1,0:T(8,128)(2,1)}, bf16[4,256,512]{2,1,0:T(8,128)(2,1)}, u32[]{:S(2)}, u32[]{:S(2)}) collective-permute-start(bf16[4,256,512]{2,1,0:T(8,128)(2,1)} %bitcast.7), channel_id=1, source_target_pairs={{1,0},{2,1},{3,2},{4,3},{5,4},{6,5},{7,6},{8,7},{9,8},{10,9},{11,1... | collective-permute-start | bytes 3145736 | tf_op jit(solution)/shard_map/ppermute | solution.py:17
  14.9 32.5 %collective-permute-start = (s32[4,2]{1,0:T(4,128)S(1)}, s32[4,2]{1,0:T(4,128)S(1)}, u32[]{:S(2)}, u32[]{:S(2)}) collective-permute-start(s32[4,2]{1,0:T(4,128)S(1)} %copy.18), channel_id=1, source_target_pairs={{1,0},{2,1},{3,2},{4,3},{5,4},{6,5},{7,6},{8,7},{9,8},{10,9},{11,1... | collective-permute-start | bytes 104 | tf_op jit(solution)/shard_map/ppermute | solution.py:17
  367.5 16.9 %copy-start = (f32[4,3,256,2,256]{4,3,2,1,0:T(2,128)S(1)}, f32[4,3,256,2,256]{4,3,2,1,0:T(2,128)}, u32[]{:S(2)}) copy-start(f32[4,3,256,2,256]{4,3,2,1,0:T(2,128)} %reshape.93) | copy-start | bytes 18874372
Sparse Core Ops, SparseCore 0:
  12.7 327.1 all-reduce.3
where the time goes:
time: 407 us; the launch traced here: 406 us
  waiting for transfers between devices  288 us (71%)
  matrix products  40.2 us (10%)
  local copies, waits for them, and re-layouts  28.1 us (7%)
  blocking collectives  26.7 us (7%)
  between operations  14.8 us (4%)
  starting transfers between devices  4.75 us (1%)
    psum x1, waiting for transfers between devices, spread(): return lax.psum(jnp.where(mine, value, jnp.zeros_like(value)), axis)  288 us
    dot_general x2, matrix products, section_term(): jnp.einsum('iaxtz,iatj->ixjz', shaped, select, precision=lax.Precision.HI...  29.1 us
    psum x1, blocking collectives, spread(): return lax.psum(jnp.where(mine, value, jnp.zeros_like(value)), axis)  26.7 us
    reshape x2, local copies, waits for them, and re-layouts, section_term(): partial_products.reshape(rows_count, slot_count, block_width, pair_count,...  16.4 us
    dot_general x2, matrix products, section_term(): jnp.einsum('iaxy,iayw->iaxw', masked, picked, preferred_element_type=jnp....  11.1 us
  transfers between devices with their start and end apart: 3, of which 1 were waited for; matrix products, arithmetic and copies ran while one was open for 2% of the time, Pallas kernels for 0%

commit v1 on v0

v1 whole, which is shorter than its diff:
```python
import jax
import jax.numpy as jnp
from jax import lax
from jax.experimental import pallas as pl
from jax.experimental.pallas import tpu as pltpu
from jax.sharding import Mesh, PartitionSpec as P

BS = 256
MB = 4
NZA = 3
KB = 4
NZB = 2
NB = 4
Y_LO = 4
Z = 8
COL = ("y_hi", "x", "core")
ROW = ("y_lo", "z")
PIECES = Y_LO * Z
PIECE = MB * NZA * BS // PIECES
SPAN = Y_LO * PIECE
META = 8


def z_route(distance):
    return [(i, (i + distance) % Z) for i in range(Z)]


def col_route(n):
    return [((i + 1) % n, i) for i in range(n)]


def products(ints, own, f1, b1, f2, b2, f3, b3, f4, b4, b_here, b_next, out, a_s, b_s, acc, sem):
    i = pl.program_id(0)

    @pl.when(i == 0)
    def _():
        z = ints[0]
        copies = []
        for n, (ref, away) in enumerate(((own, 0), (f1, -1), (b1, 1), (f2, -2), (b2, 2), (f3, -3), (b3, 3))):
            start = pl.multiple_of(((z + Z + away) % Z) * SPAN, SPAN)
            copies.append(pltpu.make_async_copy(ref, a_s.at[:, pl.ds(start, SPAN)], sem.at[n]))
        start = pl.multiple_of(((z + 4) % Z) * SPAN, SPAN)
        half = SPAN // 2
        copies.append(pltpu.make_async_copy(f4, a_s.at[:, pl.ds(start, half)], sem.at[7]))
        copies.append(pltpu.make_async_copy(b4, a_s.at[:, pl.ds(pl.multiple_of(start + half, half), half)], sem.at[8]))
        copies.append(pltpu.make_async_copy(b_here, b_s.at[0], sem.at[9]))
        copies.append(pltpu.make_async_copy(b_next, b_s.at[1], sem.at[10]))
        for c in copies:
            c.start()
        for c in copies:
            c.wait()

    acc[...] = jnp.zeros_like(acc)
    for k in range(2):
        for s in range(NZA):
            at = 1 + k * 24 + i * NZA + s
            live = ints[1 + k * 24 + 12 + i]

            @pl.when(s < live)
            def _():
                q = ints[at]
                row = pl.multiple_of((i * NZA + s) * BS, BS)
                product = jnp.dot(a_s[k, pl.ds(row, BS), :], b_s[k, q], preferred_element_type=jnp.float32)
                for t in range(NZB):
                    j = ints[1 + k * 24 + 16 + q * NZB + t]
                    acc[j] += product[:, t * BS : (t + 1) * BS]

    for j in range(NB):
        out[0, :, j * BS : (j + 1) * BS] = acc[j].astype(jnp.bfloat16)


def on_device(a_blocks, a_columns, a_live, owner_map, b_blocks, b_columns):
    tile = a_blocks.reshape(PIECES, PIECE, BS)
    meta = jnp.concatenate([a_columns.reshape(-1), a_live.reshape(-1)]).astype(jnp.bfloat16)
    meta = jnp.pad(meta[None, :], ((0, META - 1), (0, BS - meta.shape[0])))
    sent = jnp.concatenate([tile, jnp.broadcast_to(meta[None], (PIECES, META, BS))], axis=1)
    got = lax.all_to_all(sent, ("z", "y_lo"), 0, 0, tiled=True)
    holder = owner_map[0]
    source = (holder % Z) * Y_LO + holder // Z
    two = jnp.stack([lax.dynamic_index_in_dim(got, source[k], 0, keepdims=False) for k in range(2)])
    mine = two[:, :PIECE]
    own = lax.all_gather(mine, "y_lo", axis=1, tiled=True)

    b_here = b_blocks[0, 0]
    cols = lax.axis_size(COL)
    b_ready, own = lax.optimization_barrier((b_here, own))
    b_next = lax.ppermute(b_ready, COL, col_route(cols))
    bc_next = lax.ppermute(b_columns[0, 0], COL, col_route(cols))

    ahead = [own]
    back = [own]
    for _ in range(3):
        ahead.append(lax.ppermute(ahead[-1], "z", z_route(1)))
        back.append(lax.ppermute(back[-1], "z", z_route(-1)))
    f4 = lax.ppermute(ahead[3][:, : SPAN // 2], "z", z_route(1))
    b4 = lax.ppermute(back[3][:, SPAN // 2 :], "z", z_route(-1))

    pairs = [b_columns[0, 0].reshape(-1), bc_next.reshape(-1)]
    ints = [lax.axis_index("z").astype(jnp.int32)[None]]
    for k in range(2):
        ints += [two[k, PIECE, : MB * NZA + MB].astype(jnp.int32), pairs[k]]
    ints = jnp.concatenate(ints)

    hbm = pl.BlockSpec(memory_space=pl.ANY)
    window = pl.pallas_call(
        products,
        out_shape=jax.ShapeDtypeStruct((MB, BS, NB * BS), jnp.bfloat16),
        grid_spec=pltpu.PrefetchScalarGridSpec(
            num_scalar_prefetch=1,
            grid=(MB,),
            in_specs=[hbm] * 11,
            out_specs=pl.BlockSpec((1, BS, NB * BS), lambda i, ints: (i, 0, 0)),
            scratch_shapes=[
                pltpu.VMEM((2, MB * NZA * BS, BS), jnp.bfloat16),
                pltpu.VMEM((2, KB, BS, NZB * BS), jnp.bfloat16),
                pltpu.VMEM((NB, BS, BS), jnp.float32),
                pltpu.SemaphoreType.DMA((11,)),
            ],
        ),
        compiler_params=pltpu.CompilerParams(vmem_limit_bytes=24 * 1024 * 1024),
    )(ints, own, ahead[1], back[1], ahead[2], back[2], ahead[3], back[3], f4, b4, b_here, b_next)
    return window[None, None]


def solution(mesh):
    fine = Mesh(mesh.devices.reshape(Y_LO, Z, 2, 4, 2), ROW + COL)
    row, col = ROW, COL
    return jax.shard_map(
        on_device,
        mesh=fine,
        in_specs=(
            P(row, col, None, None, None, None),
            P(row, col, None, None),
            P(row, col, None),
            P(col, None),
            P(row, col, None, None, None),
            P(row, col, None, None),
        ),
        out_specs=P(row, col, None, None, None),
        check_vma=False,
    )
```

time: 407 us -> 142 us (0.35)
  the two profiles are of different devices: /device:TPU:6 before, /device:TPU:7 now
where the time goes in v1:
time: 142 us; the launch traced here: 141 us
  starting transfers between devices  53.8 us (38%)
  waiting for transfers between devices  47.2 us (33%)
  blocking collectives  12 us (8%)
  local copies, waits for them, and re-layouts  10 us (7%)
  Pallas kernels  8.93 us (6%)
  other arithmetic  4.87 us (3%)
  between operations  3.95 us (3%)
    all_to_all x1, waiting for transfers between devices, on_device(): got = lax.all_to_all(sent, ('z', 'y_lo'), 0, 0, tiled=True)  36.5 us
    ppermute x3, starting transfers between devices, on_device(): back.append(lax.ppermute(back[-1], 'z', z_route(-1)))  14.8 us
    all_to_all x1, starting transfers between devices, on_device(): got = lax.all_to_all(sent, ('z', 'y_lo'), 0, 0, tiled=True)  13.6 us
    all_gather x1, blocking collectives, on_device(): own = lax.all_gather(mine, 'y_lo', axis=1, tiled=True)  12 us
    pallas_call x1, Pallas kernels, on_device(): pl.pallas_call(products, out_shape=jax.ShapeDtypeStruct((MB, BS, NB * BS)...  8.93 us
    unnamed x25, local copies, waits for them, and re-layouts  7.48 us
    ppermute x1, starting transfers between devices, on_device(): b_next = lax.ppermute(b_ready, COL, col_route(cols))  6.58 us
    ppermute x3, waiting for transfers between devices, on_device(): back.append(lax.ppermute(back[-1], 'z', z_route(-1)))  5.95 us
  transfers between devices with their start and end apart: 11, of which 4 were waited for; matrix products, arithmetic and copies ran while one was open for 2% of the time, Pallas kernels for 0%

profile of v1, /device:TPU:7, one launch (start us, length us, event | category | flops | bytes accessed | tf_op | source)
XLA Modules:
  0.0 140.8 jit_solution(3516381216641011046)
XLA Ops:
  0.0 0.7 convert_bitcast_fusion
  0.7 0.7 convert.10
  1.3 0.1 copy.10
  1.5 0.1 concatenate.21
  1.5 0.1 fusion.5
  1.6 2.7 %pad_maximum_fusion = bf16[32,104,256]{2,1,0:T(8,128)(2,1)} fusion(bf16[32,8,256]{2,1,0:T(8,128)(2,1)S(1)} %broadcast_in_dim.14, bf16[32,96,256]{2,1,0:T(8,128)(2,1)} %bitcast.34), kind=kLoop, calls=%fused_computation | loop fusion | flops 3407872 | bytes 3407872 | tf_op jit(solution)/shard_map/concatenate | solution.py:76
  4.3 13.6 %all-to-all-start = ((bf16[32,104,256]{2,1,0:T(8,128)(2,1)}), bf16[32,104,256]{2,1,0:T(8,128)(2,1)S(1)}, u32[]{:S(2)}, u32[]{:S(2)}) async-start(bf16[32,104,256]{2,1,0:T(8,128)(2,1)} %pad_maximum_fusion), calls=%async_computation | async-start | bytes 3407872 | tf_op jit(solution)/shard_map/all_to_all | solution.py:77
  18.0 0.0 copy-start.10
  18.0 0.6 fusion.12
  22.3 36.5 %all-to-all-done = bf16[32,104,256]{2,1,0:T(8,128)(2,1)S(1)} async-done(((bf16[32,104,256]{2,1,0:T(8,128)(2,1)}), bf16[32,104,256]{2,1,0:T(8,128)(2,1)S(1)}, u32[]{:S(2)}, u32[]{:S(2)}) %all-to-all-start) | async-done | bytes 1703968 | tf_op jit(solution)/shard_map/all_to_all | solution.py:77
  58.8 1.2 copy-done.9
  60.0 12.0 %all_gather.3.own = bf16[2,384,256]{2,1,0:T(8,128)(2,1)S(1)} all-gather(bf16[2,96,256]{2,1,0:T(8,128)(2,1)S(1)} %pad_maximum_fusion.1), channel_id=1, replica_groups=mesh['y_lo'=4,'z'=8,'y_hi'=2,'x'=4,'core'=2] {'y_lo'}, dimensions={1}, use_global_device_ids=true | all-gather | bytes 491520 | tf_op jit(solution)/shard_map/all_gather | solution.py:82
  72.0 5.3 %collective-permute-start.2 = (bf16[2,384,256]{2,1,0:T(8,128)(2,1)S(1)}, bf16[2,384,256]{2,1,0:T(8,128)(2,1)S(1)}, u32[]{:S(2)}, u32[]{:S(2)}) collective-permute-start(bf16[2,384,256]{2,1,0:T(8,128)(2,1)S(1)} %all_gather.3.own), channel_id=1, source_target_pairs={{0,112},{16,0},{32,16},{48,32},{64,48},{80,64},{96,80},{112,96},{1... | collective-permute-start | bytes 1179656 | tf_op jit(solution)/shard_map/ppermute | solution.py:94
  77.3 1.9 %collective-permute-start.1 = (bf16[2,384,256]{2,1,0:T(8,128)(2,1)S(1)}, bf16[2,384,256]{2,1,0:T(8,128)(2,1)S(1)}, u32[]{:S(2)}, u32[]{:S(2)}) collective-permute-start(bf16[2,384,256]{2,1,0:T(8,128)(2,1)S(1)} %all_gather.3.own), channel_id=1, source_target_pairs={{0,16},{16,32},{32,48},{48,64},{64,80},{80,96},{96,112},{112,0},{1... | collective-permute-start | bytes 1179656 | tf_op jit(solution)/shard_map/ppermute | solution.py:93
  79.3 6.6 %collective-permute-start.9 = (bf16[4,256,512]{2,1,0:T(8,128)(2,1)S(1)}, bf16[4,256,512]{2,1,0:T(8,128)(2,1)S(1)}, u32[]{:S(2)}, u32[]{:S(2)}) collective-permute-start(bf16[4,256,512]{2,1,0:T(8,128)(2,1)S(1)} %bitcast.32), channel_id=1, source_target_pairs={{1,0},{2,1},{3,2},{4,3},{5,4},{6,5},{7,6},{8,7},{9,8},{10,9},{11,1... | collective-permute-start | bytes 3145736 | tf_op jit(solution)/shard_map/ppermute | solution.py:87
  85.8 0.0 collective-permute-done.2.b1
  85.9 4.2 %collective-permute-start.4 = (bf16[2,384,256]{2,1,0:T(8,128)(2,1)S(1)}, bf16[2,384,256]{2,1,0:T(8,128)(2,1)S(1)}, u32[]{:S(2)}, u32[]{:S(2)}) collective-permute-start(bf16[2,384,256]{2,1,0:T(8,128)(2,1)S(1)} %collective-permute-done.2.b1), channel_id=1, source_target_pairs={{0,112},{16,0},{32,16},{48,32},{64,48},{80,64},{96,80},{112,96},{1... | collective-permute-start | bytes 1179656 | tf_op jit(solution)/shard_map/ppermute | solution.py:94
  90.0 0.7 copy-done.1
  90.8 0.0 collective-permute-done.1.f1
  90.8 1.9 %collective-permute-start.3 = (bf16[2,384,256]{2,1,0:T(8,128)(2,1)S(1)}, bf16[2,384,256]{2,1,0:T(8,128)(2,1)S(1)}, u32[]{:S(2)}, u32[]{:S(2)}) collective-permute-start(bf16[2,384,256]{2,1,0:T(8,128)(2,1)S(1)} %collective-permute-done.1.f1), channel_id=1, source_target_pairs={{0,16},{16,32},{32,48},{48,64},{64,80},{80,96},{96,112},{112,0},{1... | collective-permute-start | bytes 1179656 | tf_op jit(solution)/shard_map/ppermute | solution.py:93
  92.7 0.7 copy-done.3
  93.4 3.1 %collective-permute-done.4.b2 = bf16[2,384,256]{2,1,0:T(8,128)(2,1)S(1)} collective-permute-done((bf16[2,384,256]{2,1,0:T(8,128)(2,1)S(1)}, bf16[2,384,256]{2,1,0:T(8,128)(2,1)S(1)}, u32[]{:S(2)}, u32[]{:S(2)}) %collective-permute-start.4) | collective-permute-done | bytes 393248 | tf_op jit(solution)/shard_map/ppermute | solution.py:94
  96.5 5.3 %collective-permute-start.6 = (bf16[2,384,256]{2,1,0:T(8,128)(2,1)S(1)}, bf16[2,384,256]{2,1,0:T(8,128)(2,1)S(1)}, u32[]{:S(2)}, u32[]{:S(2)}) collective-permute-start(bf16[2,384,256]{2,1,0:T(8,128)(2,1)S(1)} %collective-permute-done.4.b2), channel_id=1, source_target_pairs={{0,112},{16,0},{32,16},{48,32},{64,48},{80,64},{96,80},{112,96},{1... | collective-permute-start | bytes 1179656 | tf_op jit(solution)/shard_map/ppermute | solution.py:94
  101.8 0.8 copy-done.5
  102.6 0.0 collective-permute-done.3.f2
  102.6 1.9 %collective-permute-start.5 = (bf16[2,384,256]{2,1,0:T(8,128)(2,1)S(1)}, bf16[2,384,256]{2,1,0:T(8,128)(2,1)S(1)}, u32[]{:S(2)}, u32[]{:S(2)}) collective-permute-start(bf16[2,384,256]{2,1,0:T(8,128)(2,1)S(1)} %collective-permute-done.3.f2), channel_id=1, source_target_pairs={{0,16},{16,32},{32,48},{48,64},{64,80},{80,96},{96,112},{112,0},{1... | collective-permute-start | bytes 1179656 | tf_op jit(solution)/shard_map/ppermute | solution.py:93
  104.5 2.9 %collective-permute-done.6.b3 = bf16[2,384,256]{2,1,0:T(8,128)(2,1)S(1)} collective-permute-done((bf16[2,384,256]{2,1,0:T(8,128)(2,1)S(1)}, bf16[2,384,256]{2,1,0:T(8,128)(2,1)S(1)}, u32[]{:S(2)}, u32[]{:S(2)}) %collective-permute-start.6) | collective-permute-done | bytes 393248 | tf_op jit(solution)/shard_map/ppermute | solution.py:94
  107.4 0.7 slice.29
  108.1 5.3 %collective-permute-start.8 = (bf16[2,192,256]{2,1,0:T(8,128)(2,1)}, bf16[2,192,256]{2,1,0:T(8,128)(2,1)S(1)}, u32[]{:S(2)}, u32[]{:S(2)}) collective-permute-start(bf16[2,192,256]{2,1,0:T(8,128)(2,1)} %slice.29), channel_id=1, source_target_pairs={{0,112},{16,0},{32,16},{48,32},{64,48},{80,64},{96,80},{112,96},{1... | collective-permute-start | bytes 589832 | tf_op jit(solution)/shard_map/ppermute | solution.py:96
  113.4 0.0 collective-permute-done.5.f3
  113.4 0.7 slice.28
  114.1 1.9 %collective-permute-start.7 = (bf16[2,192,256]{2,1,0:T(8,128)(2,1)}, bf16[2,192,256]{2,1,0:T(8,128)(2,1)}, u32[]{:S(2)}, u32[]{:S(2)}) collective-permute-start(bf16[2,192,256]{2,1,0:T(8,128)(2,1)} %slice.28), channel_id=1, source_target_pairs={{0,16},{16,32},{32,48},{48,64},{64,80},{80,96},{96,112},{112,0},{1... | collective-permute-start | bytes 589832 | tf_op jit(solution)/shard_map/ppermute | solution.py:95
  116.0 5.9 %collective-permute-start = (s32[4,2]{0,1:T(2,128)S(1)}, s32[4,2]{0,1:T(2,128)S(1)}, u32[]{:S(2)}, u32[]{:S(2)}) collective-permute-start(s32[4,2]{0,1:T(2,128)S(1)} %bitcast.35), channel_id=1, source_target_pairs={{1,0},{2,1},{3,2},{4,3},{5,4},{6,5},{7,6},{8,7},{9,8},{10,9},{11,1... | collective-permute-start | bytes 104 | tf_op jit(solution)/shard_map/ppermute | solution.py:88
  122.0 0.1 copy.11
  122.1 0.1 reshape_squeeze.3
  122.2 4.8 %collective-permute-done = s32[4,2]{0,1:T(2,128)S(1)} collective-permute-done((s32[4,2]{0,1:T(2,128)S(1)}, s32[4,2]{0,1:T(2,128)S(1)}, u32[]{:S(2)}, u32[]{:S(2)}) %collective-permute-start) | collective-permute-done | bytes 64 | tf_op jit(solution)/shard_map/ppermute | solution.py:88
  126.9 0.1 copy.12
  127.0 0.1 reshape.47
  127.1 0.7 fusion.9
  127.8 0.1 concatenate.25.ints
  127.9 0.0 collective-permute-done.9.b_next
  127.9 0.0 collective-permute-done.8.b4
  127.9 0.0 collective-permute-done.7.f4
  127.9 1.0 copy-done.2
  128.9 1.0 copy-done.4
  129.9 1.0 copy-done.6
  130.9 1.0 copy-done.8
  131.9 8.9 %shard_map.64 = bf16[4,256,1024]{2,1,0:T(8,128)(2,1)} custom-call(s32[49]{0:T(128)S(1)} %concatenate.25.ints, bf16[2,384,256]{2,1,0:T(8,128)(2,1)S(1)} %all_gather.3.own, bf16[2,384,256]{2,1,0:T(8,128)(2,1)S(1)} %copy-done.4, bf16[2,384,256]{2,1,0:T(8,128)(2,1)S(1)} %copy-done.2, bf16[2,384,256]{2,1,0:T(8,128)(2,1)S(1)} %copy-done.8, ...), custom_call_target="tpu_custom_call" | custom-call | tf_op jit(solution)/shard_map/pallas_call | solution.py:105
  (19 shorter events, 0.1 us)
Async XLA Ops:
  4.3 13.6 %copy-start.11 = (s32[1,2]{1,0:T(1,128)S(1)}, s32[1,2]{1,0:T(1,128)}, u32[]{:S(2)}) copy-start(s32[1,2]{1,0:T(1,128)} %param.9) | copy-start | bytes 28
  4.3 74.9 %copy-start = (bf16[1,1,4,256,512]{4,3,2,1,0:T(8,128)(2,1)S(1)}, bf16[1,1,4,256,512]{4,3,2,1,0:T(8,128)(2,1)}, u32[]{:S(2)}) copy-start(bf16[1,1,4,256,512]{4,3,2,1,0:T(8,128)(2,1)} %param.10) | copy-start | bytes 3145732
  4.3 54.5 %all-to-all-start = ((bf16[32,104,256]{2,1,0:T(8,128)(2,1)}), bf16[32,104,256]{2,1,0:T(8,128)(2,1)S(1)}, u32[]{:S(2)}, u32[]{:S(2)}) async-start(bf16[32,104,256]{2,1,0:T(8,128)(2,1)} %pad_maximum_fusion), calls=%async_computation | async-start | bytes 3407872 | tf_op jit(solution)/shard_map/all_to_all | solution.py:77
  18.0 98.1 %copy-start.10 = (s32[1,1,4,2]{2,3,1,0:T(2,128)S(1)}, s32[1,1,4,2]{2,3,1,0:T(2,128)}, u32[]{:S(2)}) copy-start(s32[1,1,4,2]{2,3,1,0:T(2,128)} %param.11) | copy-start | bytes 100
  58.8 1.2 copy-start.9
  72.0 13.8 %collective-permute-start.2 = (bf16[2,384,256]{2,1,0:T(8,128)(2,1)S(1)}, bf16[2,384,256]{2,1,0:T(8,128)(2,1)S(1)}, u32[]{:S(2)}, u32[]{:S(2)}) collective-permute-start(bf16[2,384,256]{2,1,0:T(8,128)(2,1)S(1)} %all_gather.3.own), channel_id=1, source_target_pairs={{0,112},{16,0},{32,16},{48,32},{64,48},{80,64},{96,80},{112,96},{1... | collective-permute-start | bytes 1179656 | tf_op jit(solution)/shard_map/ppermute | solution.py:94
  77.3 13.5 %collective-permute-start.1 = (bf16[2,384,256]{2,1,0:T(8,128)(2,1)S(1)}, bf16[2,384,256]{2,1,0:T(8,128)(2,1)S(1)}, u32[]{:S(2)}, u32[]{:S(2)}) collective-permute-start(bf16[2,384,256]{2,1,0:T(8,128)(2,1)S(1)} %all_gather.3.own), channel_id=1, source_target_pairs={{0,16},{16,32},{32,48},{48,64},{64,80},{80,96},{96,112},{112,0},{1... | collective-permute-start | bytes 1179656 | tf_op jit(solution)/shard_map/ppermute | solution.py:93
  79.3 48.7 %collective-permute-start.9 = (bf16[4,256,512]{2,1,0:T(8,128)(2,1)S(1)}, bf16[4,256,512]{2,1,0:T(8,128)(2,1)S(1)}, u32[]{:S(2)}, u32[]{:S(2)}) collective-permute-start(bf16[4,256,512]{2,1,0:T(8,128)(2,1)S(1)} %bitcast.32), channel_id=1, source_target_pairs={{1,0},{2,1},{3,2},{4,3},{5,4},{6,5},{7,6},{8,7},{9,8},{10,9},{11,1... | collective-permute-start | bytes 3145736 | tf_op jit(solution)/shard_map/ppermute | solution.py:87
  85.9 10.7 %collective-permute-start.4 = (bf16[2,384,256]{2,1,0:T(8,128)(2,1)S(1)}, bf16[2,384,256]{2,1,0:T(8,128)(2,1)S(1)}, u32[]{:S(2)}, u32[]{:S(2)}) collective-permute-start(bf16[2,384,256]{2,1,0:T(8,128)(2,1)S(1)} %collective-permute-done.2.b1), channel_id=1, source_target_pairs={{0,112},{16,0},{32,16},{48,32},{64,48},{80,64},{96,80},{112,96},{1... | collective-permute-start | bytes 1179656 | tf_op jit(solution)/shard_map/ppermute | solution.py:94
  90.0 0.7 copy-start.1
  90.8 11.8 %collective-permute-start.3 = (bf16[2,384,256]{2,1,0:T(8,128)(2,1)S(1)}, bf16[2,384,256]{2,1,0:T(8,128)(2,1)S(1)}, u32[]{:S(2)}, u32[]{:S(2)}) collective-permute-start(bf16[2,384,256]{2,1,0:T(8,128)(2,1)S(1)} %collective-permute-done.1.f1), channel_id=1, source_target_pairs={{0,16},{16,32},{32,48},{48,64},{64,80},{80,96},{96,112},{112,0},{1... | collective-permute-start | bytes 1179656 | tf_op jit(solution)/shard_map/ppermute | solution.py:93
  92.7 0.7 copy-start.3
  96.5 10.9 %collective-permute-start.6 = (bf16[2,384,256]{2,1,0:T(8,128)(2,1)S(1)}, bf16[2,384,256]{2,1,0:T(8,128)(2,1)S(1)}, u32[]{:S(2)}, u32[]{:S(2)}) collective-permute-start(bf16[2,384,256]{2,1,0:T(8,128)(2,1)S(1)} %collective-permute-done.4.b2), channel_id=1, source_target_pairs={{0,112},{16,0},{32,16},{48,32},{64,48},{80,64},{96,80},{112,96},{1... | collective-permute-start | bytes 1179656 | tf_op jit(solution)/shard_map/ppermute | solution.py:94
  101.8 0.8 copy-start.5
  102.6 10.8 %copy-start.7 = (bf16[2,384,256]{2,1,0:T(8,128)(2,1)}, bf16[2,384,256]{2,1,0:T(8,128)(2,1)S(1)}, u32[]{:S(2)}) copy-start(bf16[2,384,256]{2,1,0:T(8,128)(2,1)S(1)} %collective-permute-done.3.f2) | copy-start | bytes 1179652
  102.6 10.8 %collective-permute-start.5 = (bf16[2,384,256]{2,1,0:T(8,128)(2,1)S(1)}, bf16[2,384,256]{2,1,0:T(8,128)(2,1)S(1)}, u32[]{:S(2)}, u32[]{:S(2)}) collective-permute-start(bf16[2,384,256]{2,1,0:T(8,128)(2,1)S(1)} %collective-permute-done.3.f2), channel_id=1, source_target_pairs={{0,16},{16,32},{32,48},{48,64},{64,80},{80,96},{96,112},{112,0},{1... | collective-permute-start | bytes 1179656 | tf_op jit(solution)/shard_map/ppermute | solution.py:93
  108.1 19.8 %collective-permute-start.8 = (bf16[2,192,256]{2,1,0:T(8,128)(2,1)}, bf16[2,192,256]{2,1,0:T(8,128)(2,1)S(1)}, u32[]{:S(2)}, u32[]{:S(2)}) collective-permute-start(bf16[2,192,256]{2,1,0:T(8,128)(2,1)} %slice.29), channel_id=1, source_target_pairs={{0,112},{16,0},{32,16},{48,32},{64,48},{80,64},{96,80},{112,96},{1... | collective-permute-start | bytes 589832 | tf_op jit(solution)/shard_map/ppermute | solution.py:96
  114.1 13.8 %collective-permute-start.7 = (bf16[2,192,256]{2,1,0:T(8,128)(2,1)}, bf16[2,192,256]{2,1,0:T(8,128)(2,1)}, u32[]{:S(2)}, u32[]{:S(2)}) collective-permute-start(bf16[2,192,256]{2,1,0:T(8,128)(2,1)} %slice.28), channel_id=1, source_target_pairs={{0,16},{16,32},{32,48},{48,64},{64,80},{80,96},{96,112},{112,0},{1... | collective-permute-start | bytes 589832 | tf_op jit(solution)/shard_map/ppermute | solution.py:95
  116.0 10.9 %collective-permute-start = (s32[4,2]{0,1:T(2,128)S(1)}, s32[4,2]{0,1:T(2,128)S(1)}, u32[]{:S(2)}, u32[]{:S(2)}) collective-permute-start(s32[4,2]{0,1:T(2,128)S(1)} %bitcast.35), channel_id=1, source_target_pairs={{1,0},{2,1},{3,2},{4,3},{5,4},{6,5},{7,6},{8,7},{9,8},{10,9},{11,1... | collective-permute-start | bytes 104 | tf_op jit(solution)/shard_map/ppermute | solution.py:88
  127.9 1.0 copy-start.2
  128.9 1.0 copy-start.4
  129.9 1.0 copy-start.6
  130.9 1.0 copy-start.8

commit v2 on v1

--- a/solution.py
+++ b/solution.py
@@ -18,7 +18,6 @@
 PIECES = Y_LO * Z
 PIECE = MB * NZA * BS // PIECES
 SPAN = Y_LO * PIECE
-META = 8
 
 
 def z_route(distance):
@@ -69,23 +68,41 @@
         out[0, :, j * BS : (j + 1) * BS] = acc[j].astype(jnp.bfloat16)
 
 
+def shared_ints(a_columns, a_live, holder, b_columns, cols):
+    mine = jnp.concatenate([a_columns.reshape(-1), a_live.reshape(-1)])
+    here = lax.axis_index(ROW) == holder
+    table = jnp.where(here[:, None], mine[None, :], 0).reshape(1, -1)
+    table = jnp.pad(table, ((0, 0), (0, 128 - table.shape[1])))
+    for axis, bit in (("y_lo", 1), ("y_lo", 2), ("z", 1), ("z", 2), ("z", 4)):
+        table = table + lax.ppermute(table, axis, [(i, i ^ bit) for i in range(lax.axis_size(axis))])
+    bc_here = b_columns[0, 0]
+    bc_next = lax.ppermute(bc_here, COL, col_route(cols))
+    each = MB * NZA + MB
+    return jnp.concatenate(
+        [
+            lax.axis_index("z").astype(jnp.int32)[None],
+            table[0, :each],
+            bc_here.reshape(-1),
+            table[0, each : 2 * each],
+            bc_next.reshape(-1),
+        ]
+    )
+
+
 def on_device(a_blocks, a_columns, a_live, owner_map, b_blocks, b_columns):
     tile = a_blocks.reshape(PIECES, PIECE, BS)
-    meta = jnp.concatenate([a_columns.reshape(-1), a_live.reshape(-1)]).astype(jnp.bfloat16)
-    meta = jnp.pad(meta[None, :], ((0, META - 1), (0, BS - meta.shape[0])))
-    sent = jnp.concatenate([tile, jnp.broadcast_to(meta[None], (PIECES, META, BS))], axis=1)
-    got = lax.all_to_all(sent, ("z", "y_lo"), 0, 0, tiled=True)
+    cols = lax.axis_size(COL)
+    got = lax.all_to_all(tile, ("z", "y_lo"), 0, 0, tiled=True)
     holder = owner_map[0]
     source = (holder % Z) * Y_LO + holder // Z
-    two = jnp.stack([lax.dynamic_index_in_dim(got, source[k], 0, keepdims=False) for k in range(2)])
-    mine = two[:, :PIECE]
+    ints = shared_ints(a_columns, a_live, holder, b_columns, cols)
+    got, ints = lax.optimization_barrier((got, ints))
+    mine = jnp.stack([lax.dynamic_index_in_dim(got, source[k], 0, keepdims=False) for k in range(2)])
     own = lax.all_gather(mine, "y_lo", axis=1, tiled=True)
 
     b_here = b_blocks[0, 0]
-    cols = lax.axis_size(COL)
     b_ready, own = lax.optimization_barrier((b_here, own))
     b_next = lax.ppermute(b_ready, COL, col_route(cols))
-    bc_next = lax.ppermute(b_columns[0, 0], COL, col_route(cols))
 
     ahead = [own]
     back = [own]
@@ -94,12 +111,6 @@
         back.append(lax.ppermute(back[-1], "z", z_route(-1)))
     f4 = lax.ppermute(ahead[3][:, : SPAN // 2], "z", z_route(1))
     b4 = lax.ppermute(back[3][:, SPAN // 2 :], "z", z_route(-1))
-
-    pairs = [b_columns[0, 0].reshape(-1), bc_next.reshape(-1)]
-    ints = [lax.axis_index("z").astype(jnp.int32)[None]]
-    for k in range(2):
-        ints += [two[k, PIECE, : MB * NZA + MB].astype(jnp.int32), pairs[k]]
-    ints = jnp.concatenate(ints)
 
     hbm = pl.BlockSpec(memory_space=pl.ANY)
     window = pl.pallas_call(

time: 142 us -> 147 us (1.035)
  the two profiles are of different devices: /device:TPU:7 before, /device:TPU:6 now
where the time goes in v2:
time: 147 us; the launch traced here: 146 us
  starting transfers between devices  61.6 us (42%)
  waiting for transfers between devices  55.6 us (38%)
  blocking collectives  15.1 us (10%)
  Pallas kernels  7.87 us (5%)
  between operations  4.21 us (3%)
  local copies, waits for them, and re-layouts  1.5 us (1%)
    ppermute x5, waiting for transfers between devices, shared_ints(): lax.ppermute(table, axis, [(i, i ^ bit) for i in range(lax.axis_size(axis...  37.8 us
    ppermute x3, starting transfers between devices, on_device(): back.append(lax.ppermute(back[-1], 'z', z_route(-1)))  15.6 us
    all_gather x1, blocking collectives, on_device(): own = lax.all_gather(mine, 'y_lo', axis=1, tiled=True)  15.1 us
    ppermute x5, starting transfers between devices, shared_ints(): lax.ppermute(table, axis, [(i, i ^ bit) for i in range(lax.axis_size(axis...  15 us
    all_to_all x1, starting transfers between devices, on_device(): got = lax.all_to_all(tile, ('z', 'y_lo'), 0, 0, tiled=True)  13.9 us
    ppermute x3, waiting for transfers between devices, on_device(): back.append(lax.ppermute(back[-1], 'z', z_route(-1)))  10.9 us
    pallas_call x1, Pallas kernels, on_device(): pl.pallas_call(products, out_shape=jax.ShapeDtypeStruct((MB, BS, NB * BS)...  7.87 us
    ppermute x3, starting transfers between devices, on_device(): ahead.append(lax.ppermute(ahead[-1], 'z', z_route(1)))  5.76 us
  transfers between devices with their start and end apart: 16, of which 10 were waited for; matrix products, arithmetic and copies ran while one was open for 1% of the time, Pallas kernels for 0%

profile of v2, /device:TPU:6, one launch (start us, length us, event | category | flops | bytes accessed | tf_op | source)
XLA Modules:
  0.0 146.1 jit_solution(11950013132450034400)
XLA Ops:
  0.0 0.0 copy-start.2
  0.0 13.9 %all-to-all-start = ((bf16[32,96,256]{2,1,0:T(8,128)(2,1)}), bf16[32,96,256]{2,1,0:T(8,128)(2,1)S(1)}, u32[]{:S(2)}, u32[]{:S(2)}) async-start(bf16[32,96,256]{2,1,0:T(8,128)(2,1)} %bitcast.28), calls=%async_computation | async-start | bytes 3145728 | tf_op jit(solution)/shard_map/all_to_all | solution.py:95
  13.9 0.1 copy.10
  14.0 0.1 reshape.43
  14.1 0.1 pad_add_fusion
  14.2 0.0 copy-done.4
  14.2 0.1 broadcast_select_fusion
  14.3 0.1 select_n.34
  14.4 3.7 %collective-permute-start = (s32[1,128]{1,0:T(1,128)S(1)}, s32[1,128]{1,0:T(1,128)S(1)}, u32[]{:S(2)}, u32[]{:S(2)}) collective-permute-start(s32[1,128]{1,0:T(1,128)S(1)} %pad.4), channel_id=1, source_target_pairs={{0,128},{128,0},{256,384},{384,256},{1,129},{129,1},{257,385},{385... | collective-permute-start | bytes 1544 | tf_op jit(solution)/shard_map/ppermute | solution.py:77
  18.1 28.7 %collective-permute-done = s32[1,128]{1,0:T(1,128)S(1)} collective-permute-done((s32[1,128]{1,0:T(1,128)S(1)}, s32[1,128]{1,0:T(1,128)S(1)}, u32[]{:S(2)}, u32[]{:S(2)}) %collective-permute-start) | collective-permute-done | bytes 544 | tf_op jit(solution)/shard_map/ppermute | solution.py:77
  46.8 1.9 %collective-permute-start.1 = (s32[1,128]{1,0:T(1,128)S(1)}, s32[1,128]{1,0:T(1,128)S(1)}, u32[]{:S(2)}, u32[]{:S(2)}) collective-permute-start(s32[1,128]{1,0:T(1,128)S(1)} %pad_add_fusion.1), channel_id=1, source_target_pairs={{0,256},{128,384},{256,0},{384,128},{1,257},{129,385},{257,1},{385... | collective-permute-start | bytes 1544 | tf_op jit(solution)/shard_map/ppermute | solution.py:77
  48.7 1.9 %collective-permute-start.5 = (s32[4,2]{0,1:T(2,128)S(1)}, s32[4,2]{0,1:T(2,128)S(1)}, u32[]{:S(2)}, u32[]{:S(2)}) collective-permute-start(s32[4,2]{0,1:T(2,128)S(1)} %bitcast.29), channel_id=1, source_target_pairs={{1,0},{2,1},{3,2},{4,3},{5,4},{6,5},{7,6},{8,7},{9,8},{10,9},{11,1... | collective-permute-start | bytes 104 | tf_op jit(solution)/shard_map/ppermute | solution.py:79
  50.6 2.5 %collective-permute-done.1 = s32[1,128]{1,0:T(1,128)S(1)} collective-permute-done((s32[1,128]{1,0:T(1,128)S(1)}, s32[1,128]{1,0:T(1,128)S(1)}, u32[]{:S(2)}, u32[]{:S(2)}) %collective-permute-start.1) | collective-permute-done | bytes 544 | tf_op jit(solution)/shard_map/ppermute | solution.py:77
  53.1 1.9 %collective-permute-start.2 = (s32[1,128]{1,0:T(1,128)S(1)}, s32[1,128]{1,0:T(1,128)S(1)}, u32[]{:S(2)}, u32[]{:S(2)}) collective-permute-start(s32[1,128]{1,0:T(1,128)S(1)} %add.39), channel_id=1, source_target_pairs={{0,16},{16,0},{32,48},{48,32},{64,80},{80,64},{96,112},{112,96},{1... | collective-permute-start | bytes 1544 | tf_op jit(solution)/shard_map/ppermute | solution.py:77
  55.0 3.5 %collective-permute-done.2 = s32[1,128]{1,0:T(1,128)S(1)} collective-permute-done((s32[1,128]{1,0:T(1,128)S(1)}, s32[1,128]{1,0:T(1,128)S(1)}, u32[]{:S(2)}, u32[]{:S(2)}) %collective-permute-start.2) | collective-permute-done | bytes 544 | tf_op jit(solution)/shard_map/ppermute | solution.py:77
  58.5 2.6 %collective-permute-start.3 = (s32[1,128]{1,0:T(1,128)S(1)}, s32[1,128]{1,0:T(1,128)S(1)}, u32[]{:S(2)}, u32[]{:S(2)}) collective-permute-start(s32[1,128]{1,0:T(1,128)S(1)} %add.40), channel_id=1, source_target_pairs={{0,32},{16,48},{32,0},{48,16},{64,96},{80,112},{96,64},{112,80},{1... | collective-permute-start | bytes 1544 | tf_op jit(solution)/shard_map/ppermute | solution.py:77
  61.2 0.7 fusion.2
  63.2 1.6 %collective-permute-done.3 = s32[1,128]{1,0:T(1,128)S(1)} collective-permute-done((s32[1,128]{1,0:T(1,128)S(1)}, s32[1,128]{1,0:T(1,128)S(1)}, u32[]{:S(2)}, u32[]{:S(2)}) %collective-permute-start.3) | collective-permute-done | bytes 544 | tf_op jit(solution)/shard_map/ppermute | solution.py:77
  64.8 4.9 %collective-permute-start.4 = (s32[1,128]{1,0:T(1,128)S(1)}, s32[1,128]{1,0:T(1,128)S(1)}, u32[]{:S(2)}, u32[]{:S(2)}) collective-permute-start(s32[1,128]{1,0:T(1,128)S(1)} %add.41), channel_id=1, source_target_pairs={{0,64},{16,80},{32,96},{48,112},{64,0},{80,16},{96,32},{112,48},{1... | collective-permute-start | bytes 1544 | tf_op jit(solution)/shard_map/ppermute | solution.py:77
  71.0 0.1 copy.11
  71.0 0.1 reshape_squeeze.3
  72.5 0.0 collective-permute-done.5
  72.5 0.1 copy.12
  72.6 0.1 reshape.45
  72.6 1.5 %collective-permute-done.4 = s32[1,128]{1,0:T(1,128)S(1)} collective-permute-done((s32[1,128]{1,0:T(1,128)S(1)}, s32[1,128]{1,0:T(1,128)S(1)}, u32[]{:S(2)}, u32[]{:S(2)}) %collective-permute-start.4) | collective-permute-done | bytes 544 | tf_op jit(solution)/shard_map/ppermute | solution.py:77
  74.2 0.1 slice_bitcast_fusion
  74.2 0.1 concatenate.7.ints
  74.3 0.0 all-to-all-done
  74.4 15.1 %all_gather.3.own = bf16[2,384,256]{2,1,0:T(8,128)(2,1)S(1)} all-gather(bf16[2,96,256]{2,1,0:T(8,128)(2,1)S(1)} %pad_maximum_fusion), channel_id=1, replica_groups=mesh['y_lo'=4,'z'=8,'y_hi'=2,'x'=4,'core'=2] {'y_lo'}, dimensions={1}, use_global_device_ids=true | all-gather | bytes 491520 | tf_op jit(solution)/shard_map/all_gather | solution.py:101
  89.4 4.5 %collective-permute-start.7 = (bf16[2,384,256]{2,1,0:T(8,128)(2,1)S(1)}, bf16[2,384,256]{2,1,0:T(8,128)(2,1)S(1)}, u32[]{:S(2)}, u32[]{:S(2)}) collective-permute-start(bf16[2,384,256]{2,1,0:T(8,128)(2,1)S(1)} %all_gather.3.own), channel_id=1, source_target_pairs={{0,112},{16,0},{32,16},{48,32},{64,48},{80,64},{96,80},{112,96},{1... | collective-permute-start | bytes 1179656 | tf_op jit(solution)/shard_map/ppermute | solution.py:111
  93.9 1.9 %collective-permute-start.6 = (bf16[2,384,256]{2,1,0:T(8,128)(2,1)S(1)}, bf16[2,384,256]{2,1,0:T(8,128)(2,1)S(1)}, u32[]{:S(2)}, u32[]{:S(2)}) collective-permute-start(bf16[2,384,256]{2,1,0:T(8,128)(2,1)S(1)} %all_gather.3.own), channel_id=1, source_target_pairs={{0,16},{16,32},{32,48},{48,64},{64,80},{80,96},{96,112},{112,0},{1... | collective-permute-start | bytes 1179656 | tf_op jit(solution)/shard_map/ppermute | solution.py:110
  95.8 1.9 %collective-permute-start.14 = (bf16[4,256,512]{2,1,0:T(8,128)(2,1)S(1)}, bf16[4,256,512]{2,1,0:T(8,128)(2,1)S(1)}, u32[]{:S(2)}, u32[]{:S(2)}) collective-permute-start(bf16[4,256,512]{2,1,0:T(8,128)(2,1)S(1)} %bitcast.26), channel_id=1, source_target_pairs={{1,0},{2,1},{3,2},{4,3},{5,4},{6,5},{7,6},{8,7},{9,8},{10,9},{11,1... | collective-permute-start | bytes 3145736 | tf_op jit(solution)/shard_map/ppermute | solution.py:105
  97.7 1.4 collective-permute-done.7.b1
  99.2 5.6 %collective-permute-start.9 = (bf16[2,384,256]{2,1,0:T(8,128)(2,1)S(1)}, bf16[2,384,256]{2,1,0:T(8,128)(2,1)S(1)}, u32[]{:S(2)}, u32[]{:S(2)}) collective-permute-start(bf16[2,384,256]{2,1,0:T(8,128)(2,1)S(1)} %collective-permute-done.7.b1), channel_id=1, source_target_pairs={{0,112},{16,0},{32,16},{48,32},{64,48},{80,64},{96,80},{112,96},{1... | collective-permute-start | bytes 1179656 | tf_op jit(solution)/shard_map/ppermute | solution.py:111
  104.7 0.0 collective-permute-done.6.f1
  104.8 1.9 %collective-permute-start.8 = (bf16[2,384,256]{2,1,0:T(8,128)(2,1)S(1)}, bf16[2,384,256]{2,1,0:T(8,128)(2,1)S(1)}, u32[]{:S(2)}, u32[]{:S(2)}) collective-permute-start(bf16[2,384,256]{2,1,0:T(8,128)(2,1)S(1)} %collective-permute-done.6.f1), channel_id=1, source_target_pairs={{0,16},{16,32},{32,48},{48,64},{64,80},{80,96},{96,112},{112,0},{1... | collective-permute-start | bytes 1179656 | tf_op jit(solution)/shard_map/ppermute | solution.py:110
  106.7 5.2 %collective-permute-done.9.b2 = bf16[2,384,256]{2,1,0:T(8,128)(2,1)S(1)} collective-permute-done((bf16[2,384,256]{2,1,0:T(8,128)(2,1)S(1)}, bf16[2,384,256]{2,1,0:T(8,128)(2,1)S(1)}, u32[]{:S(2)}, u32[]{:S(2)}) %collective-permute-start.9) | collective-permute-done | bytes 393248 | tf_op jit(solution)/shard_map/ppermute | solution.py:111
  111.9 5.6 %collective-permute-start.11 = (bf16[2,384,256]{2,1,0:T(8,128)(2,1)S(1)}, bf16[2,384,256]{2,1,0:T(8,128)(2,1)S(1)}, u32[]{:S(2)}, u32[]{:S(2)}) collective-permute-start(bf16[2,384,256]{2,1,0:T(8,128)(2,1)S(1)} %collective-permute-done.9.b2), channel_id=1, source_target_pairs={{0,112},{16,0},{32,16},{48,32},{64,48},{80,64},{96,80},{112,96},{1... | collective-permute-start | bytes 1179656 | tf_op jit(solution)/shard_map/ppermute | solution.py:111
  117.5 0.0 collective-permute-done.8.f2
  117.5 1.9 %collective-permute-start.10 = (bf16[2,384,256]{2,1,0:T(8,128)(2,1)S(1)}, bf16[2,384,256]{2,1,0:T(8,128)(2,1)S(1)}, u32[]{:S(2)}, u32[]{:S(2)}) collective-permute-start(bf16[2,384,256]{2,1,0:T(8,128)(2,1)S(1)} %collective-permute-done.8.f2), channel_id=1, source_target_pairs={{0,16},{16,32},{32,48},{48,64},{64,80},{80,96},{96,112},{112,0},{1... | collective-permute-start | bytes 1179656 | tf_op jit(solution)/shard_map/ppermute | solution.py:110
  119.4 4.3 %collective-permute-done.11.b3 = bf16[2,384,256]{2,1,0:T(8,128)(2,1)S(1)} collective-permute-done((bf16[2,384,256]{2,1,0:T(8,128)(2,1)S(1)}, bf16[2,384,256]{2,1,0:T(8,128)(2,1)S(1)}, u32[]{:S(2)}, u32[]{:S(2)}) %collective-permute-start.11) | collective-permute-done | bytes 393248 | tf_op jit(solution)/shard_map/ppermute | solution.py:111
  123.8 5.6 %collective-permute-start.13 = (bf16[2,192,256]{2,1,0:T(8,128)(2,1)S(1)}, bf16[2,192,256]{2,1,0:T(8,128)(2,1)S(1)}, u32[]{:S(2)}, u32[]{:S(2)}) collective-permute-start(bf16[2,192,256]{2,1,0:T(8,128)(2,1)S(1)} %slice.25), channel_id=1, source_target_pairs={{0,112},{16,0},{32,16},{48,32},{64,48},{80,64},{96,80},{112,96},{1... | collective-permute-start | bytes 589832 | tf_op jit(solution)/shard_map/ppermute | solution.py:113
  129.4 0.0 collective-permute-done.10.f3
  129.4 1.9 %collective-permute-start.12 = (bf16[2,192,256]{2,1,0:T(8,128)(2,1)S(1)}, bf16[2,192,256]{2,1,0:T(8,128)(2,1)S(1)}, u32[]{:S(2)}, u32[]{:S(2)}) collective-permute-start(bf16[2,192,256]{2,1,0:T(8,128)(2,1)S(1)} %slice.24), channel_id=1, source_target_pairs={{0,16},{16,32},{32,48},{48,64},{64,80},{80,96},{96,112},{112,0},{1... | collective-permute-start | bytes 589832 | tf_op jit(solution)/shard_map/ppermute | solution.py:112
  131.3 0.0 collective-permute-done.14.b_next
  131.3 1.2 collective-permute-done.13.b4
  132.5 5.6 %collective-permute-done.12.f4 = bf16[2,192,256]{2,1,0:T(8,128)(2,1)S(1)} collective-permute-done((bf16[2,192,256]{2,1,0:T(8,128)(2,1)S(1)}, bf16[2,192,256]{2,1,0:T(8,128)(2,1)S(1)}, u32[]{:S(2)}, u32[]{:S(2)}) %collective-permute-start.12) | collective-permute-done | bytes 196640 | tf_op jit(solution)/shard_map/ppermute | solution.py:112
  138.2 7.9 %shard_map.64 = bf16[4,256,1024]{2,1,0:T(8,128)(2,1)} custom-call(s32[49]{0:T(128)S(1)} %concatenate.7.ints, bf16[2,384,256]{2,1,0:T(8,128)(2,1)S(1)} %all_gather.3.own, bf16[2,384,256]{2,1,0:T(8,128)(2,1)S(1)} %collective-permute-done.6.f1, bf16[2,384,256]{2,1,0:T(8,128)(2,1)S(1)} %collective-permute-done.7.b1, ...), custom_call_target="tpu_custom_call" | custom-call | tf_op jit(solution)/shard_map/pallas_call | solution.py:116
  (20 shorter events, 0.1 us)
Async XLA Ops:
  0.0 13.9 %copy-start.1 = (s32[1,1,4,3]{2,1,3,0:T(1,128)S(1)}, s32[1,1,4,3]{2,1,3,0:T(1,128)}, u32[]{:S(2)}) copy-start(s32[1,1,4,3]{2,1,3,0:T(1,128)} %param.7) | copy-start | bytes 148
  0.0 14.1 %copy-start.3 = (s32[1,1,4]{2,1,0:T(1,128)S(1)}, s32[1,1,4]{2,1,0:T(1,128)}, u32[]{:S(2)}) copy-start(s32[1,1,4]{2,1,0:T(1,128)} %param.8) | copy-start | bytes 52
  0.0 14.2 %copy-start.4 = (s32[1,2]{1,0:T(1,128)S(1)}, s32[1,2]{1,0:T(1,128)}, u32[]{:S(2)}) copy-start(s32[1,2]{1,0:T(1,128)} %param.9) | copy-start | bytes 28
  0.0 48.7 %copy-start.2 = (s32[1,1,4,2]{2,3,1,0:T(2,128)S(1)}, s32[1,1,4,2]{2,3,1,0:T(2,128)}, u32[]{:S(2)}) copy-start(s32[1,1,4,2]{2,3,1,0:T(2,128)} %param.11) | copy-start | bytes 100
  0.0 95.8 %copy-start = (bf16[1,1,4,256,512]{4,3,2,1,0:T(8,128)(2,1)S(1)}, bf16[1,1,4,256,512]{4,3,2,1,0:T(8,128)(2,1)}, u32[]{:S(2)}) copy-start(bf16[1,1,4,256,512]{4,3,2,1,0:T(8,128)(2,1)} %param.10) | copy-start | bytes 3145732
  0.0 74.3 %all-to-all-start = ((bf16[32,96,256]{2,1,0:T(8,128)(2,1)}), bf16[32,96,256]{2,1,0:T(8,128)(2,1)S(1)}, u32[]{:S(2)}, u32[]{:S(2)}) async-start(bf16[32,96,256]{2,1,0:T(8,128)(2,1)} %bitcast.28), calls=%async_computation | async-start | bytes 3145728 | tf_op jit(solution)/shard_map/all_to_all | solution.py:95
  14.4 32.4 %collective-permute-start = (s32[1,128]{1,0:T(1,128)S(1)}, s32[1,128]{1,0:T(1,128)S(1)}, u32[]{:S(2)}, u32[]{:S(2)}) collective-permute-start(s32[1,128]{1,0:T(1,128)S(1)} %pad.4), channel_id=1, source_target_pairs={{0,128},{128,0},{256,384},{384,256},{1,129},{129,1},{257,385},{385... | collective-permute-start | bytes 1544 | tf_op jit(solution)/shard_map/ppermute | solution.py:77
  46.8 6.3 %collective-permute-start.1 = (s32[1,128]{1,0:T(1,128)S(1)}, s32[1,128]{1,0:T(1,128)S(1)}, u32[]{:S(2)}, u32[]{:S(2)}) collective-permute-start(s32[1,128]{1,0:T(1,128)S(1)} %pad_add_fusion.1), channel_id=1, source_target_pairs={{0,256},{128,384},{256,0},{384,128},{1,257},{129,385},{257,1},{385... | collective-permute-start | bytes 1544 | tf_op jit(solution)/shard_map/ppermute | solution.py:77
  48.7 23.8 %collective-permute-start.5 = (s32[4,2]{0,1:T(2,128)S(1)}, s32[4,2]{0,1:T(2,128)S(1)}, u32[]{:S(2)}, u32[]{:S(2)}) collective-permute-start(s32[4,2]{0,1:T(2,128)S(1)} %bitcast.29), channel_id=1, source_target_pairs={{1,0},{2,1},{3,2},{4,3},{5,4},{6,5},{7,6},{8,7},{9,8},{10,9},{11,1... | collective-permute-start | bytes 104 | tf_op jit(solution)/shard_map/ppermute | solution.py:79
  53.1 5.4 %collective-permute-start.2 = (s32[1,128]{1,0:T(1,128)S(1)}, s32[1,128]{1,0:T(1,128)S(1)}, u32[]{:S(2)}, u32[]{:S(2)}) collective-permute-start(s32[1,128]{1,0:T(1,128)S(1)} %add.39), channel_id=1, source_target_pairs={{0,16},{16,0},{32,48},{48,32},{64,80},{80,64},{96,112},{112,96},{1... | collective-permute-start | bytes 1544 | tf_op jit(solution)/shard_map/ppermute | solution.py:77
  58.5 6.3 %collective-permute-start.3 = (s32[1,128]{1,0:T(1,128)S(1)}, s32[1,128]{1,0:T(1,128)S(1)}, u32[]{:S(2)}, u32[]{:S(2)}) collective-permute-start(s32[1,128]{1,0:T(1,128)S(1)} %add.40), channel_id=1, source_target_pairs={{0,32},{16,48},{32,0},{48,16},{64,96},{80,112},{96,64},{112,80},{1... | collective-permute-start | bytes 1544 | tf_op jit(solution)/shard_map/ppermute | solution.py:77
  64.8 9.3 %collective-permute-start.4 = (s32[1,128]{1,0:T(1,128)S(1)}, s32[1,128]{1,0:T(1,128)S(1)}, u32[]{:S(2)}, u32[]{:S(2)}) collective-permute-start(s32[1,128]{1,0:T(1,128)S(1)} %add.41), channel_id=1, source_target_pairs={{0,64},{16,80},{32,96},{48,112},{64,0},{80,16},{96,32},{112,48},{1... | collective-permute-start | bytes 1544 | tf_op jit(solution)/shard_map/ppermute | solution.py:77
  89.4 9.7 %collective-permute-start.7 = (bf16[2,384,256]{2,1,0:T(8,128)(2,1)S(1)}, bf16[2,384,256]{2,1,0:T(8,128)(2,1)S(1)}, u32[]{:S(2)}, u32[]{:S(2)}) collective-permute-start(bf16[2,384,256]{2,1,0:T(8,128)(2,1)S(1)} %all_gather.3.own), channel_id=1, source_target_pairs={{0,112},{16,0},{32,16},{48,32},{64,48},{80,64},{96,80},{112,96},{1... | collective-permute-start | bytes 1179656 | tf_op jit(solution)/shard_map/ppermute | solution.py:111
  93.9 10.9 %collective-permute-start.6 = (bf16[2,384,256]{2,1,0:T(8,128)(2,1)S(1)}, bf16[2,384,256]{2,1,0:T(8,128)(2,1)S(1)}, u32[]{:S(2)}, u32[]{:S(2)}) collective-permute-start(bf16[2,384,256]{2,1,0:T(8,128)(2,1)S(1)} %all_gather.3.own), channel_id=1, source_target_pairs={{0,16},{16,32},{32,48},{48,64},{64,80},{80,96},{96,112},{112,0},{1... | collective-permute-start | bytes 1179656 | tf_op jit(solution)/shard_map/ppermute | solution.py:110
  95.8 35.5 %collective-permute-start.14 = (bf16[4,256,512]{2,1,0:T(8,128)(2,1)S(1)}, bf16[4,256,512]{2,1,0:T(8,128)(2,1)S(1)}, u32[]{:S(2)}, u32[]{:S(2)}) collective-permute-start(bf16[4,256,512]{2,1,0:T(8,128)(2,1)S(1)} %bitcast.26), channel_id=1, source_target_pairs={{1,0},{2,1},{3,2},{4,3},{5,4},{6,5},{7,6},{8,7},{9,8},{10,9},{11,1... | collective-permute-start | bytes 3145736 | tf_op jit(solution)/shard_map/ppermute | solution.py:105
  99.2 12.8 %collective-permute-start.9 = (bf16[2,384,256]{2,1,0:T(8,128)(2,1)S(1)}, bf16[2,384,256]{2,1,0:T(8,128)(2,1)S(1)}, u32[]{:S(2)}, u32[]{:S(2)}) collective-permute-start(bf16[2,384,256]{2,1,0:T(8,128)(2,1)S(1)} %collective-permute-done.7.b1), channel_id=1, source_target_pairs={{0,112},{16,0},{32,16},{48,32},{64,48},{80,64},{96,80},{112,96},{1... | collective-permute-start | bytes 1179656 | tf_op jit(solution)/shard_map/ppermute | solution.py:111
  104.8 12.8 %collective-permute-start.8 = (bf16[2,384,256]{2,1,0:T(8,128)(2,1)S(1)}, bf16[2,384,256]{2,1,0:T(8,128)(2,1)S(1)}, u32[]{:S(2)}, u32[]{:S(2)}) collective-permute-start(bf16[2,384,256]{2,1,0:T(8,128)(2,1)S(1)} %collective-permute-done.6.f1), channel_id=1, source_target_pairs={{0,16},{16,32},{32,48},{48,64},{64,80},{80,96},{96,112},{112,0},{1... | collective-permute-start | bytes 1179656 | tf_op jit(solution)/shard_map/ppermute | solution.py:110
  111.9 11.8 %collective-permute-start.11 = (bf16[2,384,256]{2,1,0:T(8,128)(2,1)S(1)}, bf16[2,384,256]{2,1,0:T(8,128)(2,1)S(1)}, u32[]{:S(2)}, u32[]{:S(2)}) collective-permute-start(bf16[2,384,256]{2,1,0:T(8,128)(2,1)S(1)} %collective-permute-done.9.b2), channel_id=1, source_target_pairs={{0,112},{16,0},{32,16},{48,32},{64,48},{80,64},{96,80},{112,96},{1... | collective-permute-start | bytes 1179656 | tf_op jit(solution)/shard_map/ppermute | solution.py:111
  117.5 11.9 %collective-permute-start.10 = (bf16[2,384,256]{2,1,0:T(8,128)(2,1)S(1)}, bf16[2,384,256]{2,1,0:T(8,128)(2,1)S(1)}, u32[]{:S(2)}, u32[]{:S(2)}) collective-permute-start(bf16[2,384,256]{2,1,0:T(8,128)(2,1)S(1)} %collective-permute-done.8.f2), channel_id=1, source_target_pairs={{0,16},{16,32},{32,48},{48,64},{64,80},{80,96},{96,112},{112,0},{1... | collective-permute-start | bytes 1179656 | tf_op jit(solution)/shard_map/ppermute | solution.py:110
  123.8 8.8 %collective-permute-start.13 = (bf16[2,192,256]{2,1,0:T(8,128)(2,1)S(1)}, bf16[2,192,256]{2,1,0:T(8,128)(2,1)S(1)}, u32[]{:S(2)}, u32[]{:S(2)}) collective-permute-start(bf16[2,192,256]{2,1,0:T(8,128)(2,1)S(1)} %slice.25), channel_id=1, source_target_pairs={{0,112},{16,0},{32,16},{48,32},{64,48},{80,64},{96,80},{112,96},{1... | collective-permute-start | bytes 589832 | tf_op jit(solution)/shard_map/ppermute | solution.py:113
  129.4 8.8 %collective-permute-start.12 = (bf16[2,192,256]{2,1,0:T(8,128)(2,1)S(1)}, bf16[2,192,256]{2,1,0:T(8,128)(2,1)S(1)}, u32[]{:S(2)}, u32[]{:S(2)}) collective-permute-start(bf16[2,192,256]{2,1,0:T(8,128)(2,1)S(1)} %slice.24), channel_id=1, source_target_pairs={{0,16},{16,32},{32,48},{48,64},{64,80},{80,96},{96,112},{112,0},{1... | collective-permute-start | bytes 589832 | tf_op jit(solution)/shard_map/ppermute | solution.py:112

commit v3 on v2

v3 whole, which is shorter than its diff:
```python
import jax
import jax.numpy as jnp
from jax import lax
from jax.experimental import pallas as pl
from jax.experimental.pallas import tpu as pltpu
from jax.sharding import Mesh, PartitionSpec as P

BS = 256
MB = 4
NZA = 3
KB = 4
NZB = 2
NB = 4
Y_LO = 4
Z = 8
COL = ("y_hi", "x", "core")
ROW = ("y_lo", "z")
PIECES = Y_LO * Z
PIECE = MB * NZA * BS // PIECES
SPAN = Y_LO * PIECE


def z_route(distance):
    return [(i, (i + distance) % Z) for i in range(Z)]


def col_route(n):
    return [((i + 1) % n, i) for i in range(n)]


def block_rows(rounds, ints, refs, b_refs, out, a_s, o_s, acc, sem, osem):
    place, table, rest, b_columns = ints[0], ints[1], ints[2], ints[3:]
    z = place[0]
    copies = []
    for n, (ref, away, start, rows) in enumerate(refs):
        at = pl.multiple_of(((z + Z + away) % Z) * SPAN + start, SPAN // 2)
        copies.append(pltpu.make_async_copy(ref, a_s.at[:, pl.ds(at, rows)], sem.at[n]))
    for c in copies:
        c.start()
    for c in copies:
        c.wait()
    odd = z % 2
    writes = []
    for n, even_row, odd_row in rounds:
        i = ((z + even_row + odd * (odd_row - even_row) + Z) % Z) // 2
        acc[...] = jnp.zeros_like(acc)
        for k in range(2):
            for s in range(NZA):
                base = k * EACH
                live = table[0, base + MB * NZA + i] + rest[0, base + MB * NZA + i]

                @pl.when(s < live)
                def _():
                    at = base + i * NZA + s
                    q = table[0, at] + rest[0, at]
                    row = pl.multiple_of((i * NZA + s) * BS, BS)
                    product = jnp.dot(a_s[k, pl.ds(row, BS), :], b_refs[k][q], preferred_element_type=jnp.float32)
                    for t in range(NZB):
                        j = b_columns[k][q * NZB + t]
                        acc[j] += product[:, t * BS : (t + 1) * BS]

        for j in range(NB):
            o_s[n, :, j * BS : (j + 1) * BS] = acc[j].astype(jnp.bfloat16)
        writes.append(pltpu.make_async_copy(o_s.at[n], out.at[i], osem.at[n]))
        writes[-1].start()
    for w in writes:
        w.wait()


def two_rows(place, table, rest, bc_here, bc_next, own, f1, b1, f2, b2, b_here, b_next, out, *scratch):
    refs = [(own, 0, 0, SPAN), (f1, -1, 0, SPAN), (b1, 1, 0, SPAN), (f2, -2, 0, SPAN), (b2, 2, 0, SPAN)]
    block_rows([(0, 0, 0), (1, -2, 1)], (place, table, rest, bc_here, bc_next), refs, (b_here, b_next), out, *scratch)


def third_row(place, table, rest, bc_here, bc_next, f2, b2, f3, b3, b_here, b_next, before, out, *scratch):
    refs = [(f2, -2, 0, SPAN), (b2, 2, 0, SPAN), (f3, -3, 0, SPAN), (b3, 3, 0, SPAN)]
    block_rows([(0, 2, -3)], (place, table, rest, bc_here, bc_next), refs, (b_here, b_next), out, *scratch)


def last_row(place, table, rest, bc_here, bc_next, f3, b3, f4, b4, b_here, b_next, before, out, *scratch):
    half = SPAN // 2
    refs = [(f3, -3, 0, SPAN), (b3, 3, 0, SPAN), (f4, 4, 0, half), (b4, 4, half, half)]
    block_rows([(0, 4, 3)], (place, table, rest, bc_here, bc_next), refs, (b_here, b_next), out, *scratch)


def call(kernel, rows, ints, pieces, b_pair, before):
    hbm = pl.BlockSpec(memory_space=pl.ANY)
    vmem = pl.BlockSpec(memory_space=pltpu.VMEM)
    ends = [] if before is None else [before]
    return pl.pallas_call(
        kernel,
        out_shape=jax.ShapeDtypeStruct((MB, BS, NB * BS), jnp.bfloat16),
        grid_spec=pltpu.PrefetchScalarGridSpec(
            num_scalar_prefetch=len(ints),
            grid=(),
            in_specs=[hbm] * len(pieces) + [vmem] * 2 + [hbm] * len(ends),
            out_specs=hbm,
            scratch_shapes=[
                pltpu.VMEM((2, MB * NZA * BS, BS), jnp.bfloat16),
                pltpu.VMEM((rows, BS, NB * BS), jnp.bfloat16),
                pltpu.VMEM((NB, BS, BS), jnp.float32),
                pltpu.SemaphoreType.DMA((len(pieces),)),
                pltpu.SemaphoreType.DMA((rows,)),
            ],
        ),
        input_output_aliases={len(ints) + len(pieces) + 2: 0} if ends else {},
        cost_estimate=pl.CostEstimate(flops=rows * 12 * BS**3 * 2, bytes_accessed=rows << 20, transcendentals=0),
        compiler_params=pltpu.CompilerParams(vmem_limit_bytes=12 * 1024 * 1024),
    )(*ints, *pieces, *b_pair, *ends)


EACH = MB * NZA + MB


def masked_ints(a_columns, a_live, holder):
    mine = jnp.concatenate([a_columns.reshape(-1), a_live.reshape(-1)])
    here = lax.axis_index(ROW) == holder
    table = jnp.where(here[:, None], mine[None, :], 0).reshape(1, -1)
    table = jnp.pad(table, ((0, 0), (0, 128 - table.shape[1])))
    total = table
    for distance in range(1, Z):
        total = total + lax.ppermute(table, "z", z_route(distance))
    return total


def on_device(a_blocks, a_columns, a_live, owner_map, b_blocks, b_columns):
    tile = a_blocks.reshape(PIECES, PIECE, BS)
    cols = lax.axis_size(COL)
    got = lax.all_to_all(tile, ("z", "y_lo"), 0, 0, tiled=True)
    holder = owner_map[0]
    source = (holder % Z) * Y_LO + holder // Z
    table = masked_ints(a_columns, a_live, holder)
    bc_here = b_columns[0, 0]
    bc_next = lax.ppermute(bc_here, COL, col_route(cols)).reshape(-1)
    bc_here = bc_here.reshape(-1)
    got, table, bc_here, bc_next = lax.optimization_barrier((got, table, bc_here, bc_next))

    first = lax.ppermute(table, "y_lo", [(i, i ^ 1) for i in range(Y_LO)])
    two = jnp.stack([lax.dynamic_index_in_dim(got, source[k], 0, keepdims=False) for k in range(2)])
    own = lax.all_gather(two, "y_lo", axis=1, tiled=True)
    own, first = lax.optimization_barrier((own, first))
    b_here = b_blocks[0, 0]
    b_ready, own, table = lax.optimization_barrier((b_here, own, table + first))
    b_next = lax.ppermute(b_ready, COL, col_route(cols))
    rest = lax.ppermute(table, "y_lo", [(i, i ^ 2) for i in range(Y_LO)])
    ahead = [own]
    back = [own]
    for step in range(3):
        ahead.append(lax.ppermute(ahead[-1], "z", z_route(1)))
        back.append(lax.ppermute(back[-1], "z", z_route(-1)))
        if step == 1:
            ahead[2], back[2], rest = lax.optimization_barrier((ahead[2], back[2], rest))
    f4 = lax.ppermute(ahead[3][:, : SPAN // 2], "z", z_route(1))
    b4 = lax.ppermute(back[3][:, SPAN // 2 :], "z", z_route(-1))

    b_pair = (b_here, b_next)
    ints = (lax.axis_index("z").astype(jnp.int32)[None], table, rest, bc_here, bc_next)
    window = call(two_rows, 2, ints, (own, ahead[1], back[1], ahead[2], back[2]), b_pair, None)
    window = call(third_row, 1, ints, (ahead[2], back[2], ahead[3], back[3]), b_pair, window)
    window = call(last_row, 1, ints, (ahead[3], back[3], f4, b4), b_pair, window)
    return window[None, None]


def solution(mesh):
    fine = Mesh(mesh.devices.reshape(Y_LO, Z, 2, 4, 2), ROW + COL)
    row, col = ROW, COL
    return jax.shard_map(
        on_device,
        mesh=fine,
        in_specs=(
            P(row, col, None, None, None, None),
            P(row, col, None, None),
            P(row, col, None),
            P(col, None),
            P(row, col, None, None, None),
            P(row, col, None, None),
        ),
        out_specs=P(row, col, None, None, None),
        check_vma=False,
    )
```

time: 147 us -> 143 us (0.973)
  the two profiles are of different devices: /device:TPU:6 before, /device:TPU:8 now
where the time goes in v3:
time: 143 us
  starting transfers between devices  83.6 us (58%)
  waiting for transfers between devices  26.6 us (19%)
  blocking collectives  15.5 us (11%)
  Pallas kernels  11.1 us (8%)
  between operations  4.36 us (3%)
    ppermute x7, starting transfers between devices, masked_ints(): total = total + lax.ppermute(table, 'z', z_route(distance))  27.3 us
    all_gather x1, blocking collectives, on_device(): own = lax.all_gather(two, 'y_lo', axis=1, tiled=True)  15.5 us
    all_to_all x1, starting transfers between devices, on_device(): got = lax.all_to_all(tile, ('z', 'y_lo'), 0, 0, tiled=True)  14.1 us
    ppermute x3, starting transfers between devices, on_device(): back.append(lax.ppermute(back[-1], 'z', z_route(-1)))  14 us
    ppermute x1, waiting for transfers between devices, on_device(): rest = lax.ppermute(table, 'y_lo', [(i, i ^ 2) for i in range(Y_LO)])  13.2 us
    pallas_call x3, Pallas kernels, call(): pl.pallas_call(kernel, out_shape=jax.ShapeDtypeStruct((MB, BS, NB * BS),...  11.1 us
    ppermute x3, starting transfers between devices, on_device(): ahead.append(lax.ppermute(ahead[-1], 'z', z_route(1)))  7.13 us
    ppermute x3, waiting for transfers between devices, on_device(): ahead.append(lax.ppermute(ahead[-1], 'z', z_route(1)))  5.56 us
  transfers between devices with their start and end apart: 20, of which 5 were waited for; matrix products, arithmetic and copies ran while one was open for 1% of the time, Pallas kernels for 6%

profile of v3, /device:TPU:8, one launch (start us, length us, event | category | flops | bytes accessed | tf_op | source)
XLA Modules:
  0.0 142.7 jit_solution(10268542719780531781)
XLA Ops:
  0.0 14.1 %all-to-all-start = ((bf16[32,96,256]{2,1,0:T(8,128)(2,1)}), bf16[32,96,256]{2,1,0:T(8,128)(2,1)S(1)}, u32[]{:S(2)}, u32[]{:S(2)}) async-start(bf16[32,96,256]{2,1,0:T(8,128)(2,1)} %bitcast.26), calls=%async_computation | async-start | bytes 3145728 | tf_op jit(solution)/shard_map/all_to_all | solution.py:129
  14.2 0.1 copy.12
  14.2 0.1 reshape.43
  14.3 0.1 pad_add_fusion
  14.4 0.1 broadcast_select_fusion
  14.5 0.1 select_n.34
  14.6 3.4 %collective-permute-start = (s32[1,128]{1,0:T(1,128)S(1)}, s32[1,128]{1,0:T(1,128)S(1)}, u32[]{:S(2)}, u32[]{:S(2)}) collective-permute-start(s32[1,128]{1,0:T(1,128)S(1)} %pad.4), channel_id=1, source_target_pairs={{0,16},{16,32},{32,48},{48,64},{64,80},{80,96},{96,112},{112,0},{1... | collective-permute-start | bytes 1544 | tf_op jit(solution)/shard_map/ppermute | solution.py:122
  18.0 4.3 %collective-permute-start.1 = (s32[1,128]{1,0:T(1,128)S(1)}, s32[1,128]{1,0:T(1,128)S(1)}, u32[]{:S(2)}, u32[]{:S(2)}) collective-permute-start(s32[1,128]{1,0:T(1,128)S(1)} %pad.4), channel_id=1, source_target_pairs={{0,32},{16,48},{32,64},{48,80},{64,96},{80,112},{96,0},{112,16},{1... | collective-permute-start | bytes 1544 | tf_op jit(solution)/shard_map/ppermute | solution.py:122
  22.2 4.6 %collective-permute-start.2 = (s32[1,128]{1,0:T(1,128)S(1)}, s32[1,128]{1,0:T(1,128)S(1)}, u32[]{:S(2)}, u32[]{:S(2)}) collective-permute-start(s32[1,128]{1,0:T(1,128)S(1)} %pad.4), channel_id=1, source_target_pairs={{0,48},{16,64},{32,80},{48,96},{64,112},{80,0},{96,16},{112,32},{1... | collective-permute-start | bytes 1544 | tf_op jit(solution)/shard_map/ppermute | solution.py:122
  26.9 4.2 %collective-permute-start.3 = (s32[1,128]{1,0:T(1,128)S(1)}, s32[1,128]{1,0:T(1,128)S(1)}, u32[]{:S(2)}, u32[]{:S(2)}) collective-permute-start(s32[1,128]{1,0:T(1,128)S(1)} %pad.4), channel_id=1, source_target_pairs={{0,64},{16,80},{32,96},{48,112},{64,0},{80,16},{96,32},{112,48},{1... | collective-permute-start | bytes 1544 | tf_op jit(solution)/shard_map/ppermute | solution.py:122
  31.1 5.0 %collective-permute-start.7 = (s32[4,2]{0,1:T(2,128)S(1)}, s32[4,2]{0,1:T(2,128)S(1)}, u32[]{:S(2)}, u32[]{:S(2)}) collective-permute-start(s32[4,2]{0,1:T(2,128)S(1)} %bitcast.27), channel_id=1, source_target_pairs={{1,0},{2,1},{3,2},{4,3},{5,4},{6,5},{7,6},{8,7},{9,8},{10,9},{11,1... | collective-permute-start | bytes 104 | tf_op jit(solution)/shard_map/ppermute | solution.py:134
  36.1 0.1 copy.13
  36.2 0.7 fusion.2
  38.9 5.0 %collective-permute-done.7 = s32[4,2]{0,1:T(2,128)S(1)} collective-permute-done((s32[4,2]{0,1:T(2,128)S(1)}, s32[4,2]{0,1:T(2,128)S(1)}, u32[]{:S(2)}, u32[]{:S(2)}) %collective-permute-start.7) | collective-permute-done | bytes 64 | tf_op jit(solution)/shard_map/ppermute | solution.py:134
  43.8 1.9 %collective-permute-start.4 = (s32[1,128]{1,0:T(1,128)S(1)}, s32[1,128]{1,0:T(1,128)S(1)}, u32[]{:S(2)}, u32[]{:S(2)}) collective-permute-start(s32[1,128]{1,0:T(1,128)S(1)} %pad.4), channel_id=1, source_target_pairs={{0,80},{16,96},{32,112},{48,0},{64,16},{80,32},{96,48},{112,64},{1... | collective-permute-start | bytes 1544 | tf_op jit(solution)/shard_map/ppermute | solution.py:122
  45.8 2.8 %collective-permute-done = s32[1,128]{1,0:T(1,128)S(1)} collective-permute-done((s32[1,128]{1,0:T(1,128)S(1)}, s32[1,128]{1,0:T(1,128)S(1)}, u32[]{:S(2)}, u32[]{:S(2)}) %collective-permute-start) | collective-permute-done | bytes 544 | tf_op jit(solution)/shard_map/ppermute | solution.py:122
  48.5 3.2 %collective-permute-start.5 = (s32[1,128]{1,0:T(1,128)S(1)}, s32[1,128]{1,0:T(1,128)S(1)}, u32[]{:S(2)}, u32[]{:S(2)}) collective-permute-start(s32[1,128]{1,0:T(1,128)S(1)} %pad.4), channel_id=1, source_target_pairs={{0,96},{16,112},{32,0},{48,16},{64,32},{80,48},{96,64},{112,80},{1... | collective-permute-start | bytes 1544 | tf_op jit(solution)/shard_map/ppermute | solution.py:122
  51.7 0.0 collective-permute-done.1
  51.7 5.7 %collective-permute-start.6 = (s32[1,128]{1,0:T(1,128)S(1)}, s32[1,128]{1,0:T(1,128)S(1)}, u32[]{:S(2)}, u32[]{:S(2)}) collective-permute-start(s32[1,128]{1,0:T(1,128)S(1)} %pad.4), channel_id=1, source_target_pairs={{0,112},{16,0},{32,16},{48,32},{64,48},{80,64},{96,80},{112,96},{1... | collective-permute-start | bytes 1544 | tf_op jit(solution)/shard_map/ppermute | solution.py:122
  58.2 0.1 reshape_squeeze.3.bc_here
  59.6 0.1 copy.14
  59.7 0.1 reshape.45.bc_next
  59.8 0.0 collective-permute-done.2
  59.8 0.0 collective-permute-done.3
  59.8 0.0 collective-permute-done.4
  59.8 0.0 collective-permute-done.6
  59.8 2.6 %collective-permute-start.8 = (s32[1,128]{1,0:T(1,128)S(1)}, s32[1,128]{1,0:T(1,128)S(1)}, u32[]{:S(2)}, u32[]{:S(2)}) collective-permute-start(s32[1,128]{1,0:T(1,128)S(1)} %add_add_fusion), channel_id=1, source_target_pairs={{0,128},{128,0},{256,384},{384,256},{1,129},{129,1},{257,385},{385... | collective-permute-start | bytes 1544 | tf_op jit(solution)/shard_map/ppermute | solution.py:138
  62.5 15.5 %all_gather.3.own = bf16[2,384,256]{2,1,0:T(8,128)(2,1)S(1)} all-gather(bf16[2,96,256]{2,1,0:T(8,128)(2,1)S(1)} %pad_maximum_fusion), channel_id=1, replica_groups=mesh['y_lo'=4,'z'=8,'y_hi'=2,'x'=4,'core'=2] {'y_lo'}, dimensions={1}, use_global_device_ids=true | all-gather | bytes 491520 | tf_op jit(solution)/shard_map/all_gather | solution.py:140
  78.0 0.0 collective-permute-done.8
  78.0 3.2 %collective-permute-start.9 = (bf16[2,384,256]{2,1,0:T(8,128)(2,1)S(1)}, bf16[2,384,256]{2,1,0:T(8,128)(2,1)S(1)}, u32[]{:S(2)}, u32[]{:S(2)}) collective-permute-start(bf16[2,384,256]{2,1,0:T(8,128)(2,1)S(1)} %all_gather.3.own), channel_id=1, source_target_pairs={{0,16},{16,32},{32,48},{48,64},{64,80},{80,96},{96,112},{112,0},{1... | collective-permute-start | bytes 1179656 | tf_op jit(solution)/shard_map/ppermute | solution.py:149
  81.2 3.8 %collective-permute-start.11 = (bf16[2,384,256]{2,1,0:T(8,128)(2,1)S(1)}, bf16[2,384,256]{2,1,0:T(8,128)(2,1)S(1)}, u32[]{:S(2)}, u32[]{:S(2)}) collective-permute-start(bf16[2,384,256]{2,1,0:T(8,128)(2,1)S(1)} %all_gather.3.own), channel_id=1, source_target_pairs={{0,112},{16,0},{32,16},{48,32},{64,48},{80,64},{96,80},{112,96},{1... | collective-permute-start | bytes 1179656 | tf_op jit(solution)/shard_map/ppermute | solution.py:150
  85.1 2.0 %collective-permute-start.18 = (bf16[4,256,512]{2,1,0:T(8,128)(2,1)S(1)}, bf16[4,256,512]{2,1,0:T(8,128)(2,1)S(1)}, u32[]{:S(2)}, u32[]{:S(2)}) collective-permute-start(bf16[4,256,512]{2,1,0:T(8,128)(2,1)S(1)} %bitcast.22), channel_id=1, source_target_pairs={{1,0},{2,1},{3,2},{4,3},{5,4},{6,5},{7,6},{8,7},{9,8},{10,9},{11,1... | collective-permute-start | bytes 3145736 | tf_op jit(solution)/shard_map/ppermute | solution.py:144
  87.1 1.7 %collective-permute-done.9.f1 = bf16[2,384,256]{2,1,0:T(8,128)(2,1)S(1)} collective-permute-done((bf16[2,384,256]{2,1,0:T(8,128)(2,1)S(1)}, bf16[2,384,256]{2,1,0:T(8,128)(2,1)S(1)}, u32[]{:S(2)}, u32[]{:S(2)}) %collective-permute-start.9) | collective-permute-done | bytes 393248 | tf_op jit(solution)/shard_map/ppermute | solution.py:149
  88.9 2.0 %collective-permute-start.10 = (bf16[2,384,256]{2,1,0:T(8,128)(2,1)S(1)}, bf16[2,384,256]{2,1,0:T(8,128)(2,1)S(1)}, u32[]{:S(2)}, u32[]{:S(2)}) collective-permute-start(bf16[2,384,256]{2,1,0:T(8,128)(2,1)S(1)} %collective-permute-done.9.f1), channel_id=1, source_target_pairs={{0,16},{16,32},{32,48},{48,64},{64,80},{80,96},{96,112},{112,0},{1... | collective-permute-start | bytes 1179656 | tf_op jit(solution)/shard_map/ppermute | solution.py:149
  90.9 0.0 collective-permute-done.11.b1
  90.9 5.0 %collective-permute-start.12 = (bf16[2,384,256]{2,1,0:T(8,128)(2,1)S(1)}, bf16[2,384,256]{2,1,0:T(8,128)(2,1)S(1)}, u32[]{:S(2)}, u32[]{:S(2)}) collective-permute-start(bf16[2,384,256]{2,1,0:T(8,128)(2,1)S(1)} %collective-permute-done.11.b1), channel_id=1, source_target_pairs={{0,112},{16,0},{32,16},{48,32},{64,48},{80,64},{96,80},{112,96},{1... | collective-permute-start | bytes 1179656 | tf_op jit(solution)/shard_map/ppermute | solution.py:150
  96.0 4.4 %collective-permute-start.13 = (s32[1,128]{1,0:T(1,128)S(1)}, s32[1,128]{1,0:T(1,128)S(1)}, u32[]{:S(2)}, u32[]{:S(2)}) collective-permute-start(s32[1,128]{1,0:T(1,128)S(1)} %add.58.table), channel_id=1, source_target_pairs={{0,256},{128,384},{256,0},{384,128},{1,257},{129,385},{257,1},{385... | collective-permute-start | bytes 1544 | tf_op jit(solution)/shard_map/ppermute | solution.py:145
  100.4 13.2 %collective-permute-done.13.rest = s32[1,128]{1,0:T(1,128)S(1)} collective-permute-done((s32[1,128]{1,0:T(1,128)S(1)}, s32[1,128]{1,0:T(1,128)S(1)}, u32[]{:S(2)}, u32[]{:S(2)}) %collective-permute-start.13) | collective-permute-done | bytes 544 | tf_op jit(solution)/shard_map/ppermute | solution.py:145
  113.6 1.9 %collective-permute-start.14 = (bf16[2,384,256]{2,1,0:T(8,128)(2,1)S(1)}, bf16[2,384,256]{2,1,0:T(8,128)(2,1)S(1)}, u32[]{:S(2)}, u32[]{:S(2)}) collective-permute-start(bf16[2,384,256]{2,1,0:T(8,128)(2,1)S(1)} %collective-permute-done.10.f2), channel_id=1, source_target_pairs={{0,16},{16,32},{32,48},{48,64},{64,80},{80,96},{96,112},{112,0},{1... | collective-permute-start | bytes 1179656 | tf_op jit(solution)/shard_map/ppermute | solution.py:149
  115.5 5.1 %collective-permute-start.15 = (bf16[2,384,256]{2,1,0:T(8,128)(2,1)S(1)}, bf16[2,384,256]{2,1,0:T(8,128)(2,1)S(1)}, u32[]{:S(2)}, u32[]{:S(2)}) collective-permute-start(bf16[2,384,256]{2,1,0:T(8,128)(2,1)S(1)} %collective-permute-done.12.b2), channel_id=1, source_target_pairs={{0,112},{16,0},{32,16},{48,32},{64,48},{80,64},{96,80},{112,96},{1... | collective-permute-start | bytes 1179656 | tf_op jit(solution)/shard_map/ppermute | solution.py:150
  120.7 3.8 %collective-permute-done.14.f3 = bf16[2,384,256]{2,1,0:T(8,128)(2,1)S(1)} collective-permute-done((bf16[2,384,256]{2,1,0:T(8,128)(2,1)S(1)}, bf16[2,384,256]{2,1,0:T(8,128)(2,1)S(1)}, u32[]{:S(2)}, u32[]{:S(2)}) %collective-permute-start.14) | collective-permute-done | bytes 393248 | tf_op jit(solution)/shard_map/ppermute | solution.py:149
  124.5 1.9 %collective-permute-start.16 = (bf16[2,192,256]{2,1,0:T(8,128)(2,1)S(1)}, bf16[2,192,256]{2,1,0:T(8,128)(2,1)S(1)}, u32[]{:S(2)}, u32[]{:S(2)}) collective-permute-start(bf16[2,192,256]{2,1,0:T(8,128)(2,1)S(1)} %slice.16), channel_id=1, source_target_pairs={{0,16},{16,32},{32,48},{48,64},{64,80},{80,96},{96,112},{112,0},{1... | collective-permute-start | bytes 589832 | tf_op jit(solution)/shard_map/ppermute | solution.py:153
  126.4 0.0 collective-permute-done.15.b3
  126.5 5.1 %collective-permute-start.17 = (bf16[2,192,256]{2,1,0:T(8,128)(2,1)S(1)}, bf16[2,192,256]{2,1,0:T(8,128)(2,1)S(1)}, u32[]{:S(2)}, u32[]{:S(2)}) collective-permute-start(bf16[2,192,256]{2,1,0:T(8,128)(2,1)S(1)} %slice.17), channel_id=1, source_target_pairs={{0,112},{16,0},{32,16},{48,32},{64,48},{80,64},{96,80},{112,96},{1... | collective-permute-start | bytes 589832 | tf_op jit(solution)/shard_map/ppermute | solution.py:154
  131.6 5.0 %shard_map.64.before = bf16[4,256,1024]{2,1,0:T(8,128)(2,1)} custom-call(s32[1]{0:T(128)} %bitcast.place, s32[1,128]{1,0:T(1,128)S(1)} %add.58.table, s32[1,128]{1,0:T(1,128)S(1)} %collective-permute-done.13.rest, s32[8]{0:T(128)S(1)} %reshape_squeeze.3.bc_here, s32[8]{0:T(128)S(1)} %reshape.45.bc_next, bf16[2,384,256]{2,1,0:T(8,128)(2,1)S(1)} %all_gather.3.own, ...), custom_call_target="tpu_custom_call" | custom-call | flops 805306368 | bytes 2097152 | tf_op jit(solution)/shard_map/pallas_call | solution.py:90
  136.6 3.0 %shard_map.65.before = bf16[4,256,1024]{2,1,0:T(8,128)(2,1)} custom-call(s32[1]{0:T(128)} %bitcast.place, s32[1,128]{1,0:T(1,128)S(1)} %add.58.table, s32[1,128]{1,0:T(1,128)S(1)} %collective-permute-done.13.rest, s32[8]{0:T(128)S(1)} %reshape_squeeze.3.bc_here, s32[8]{0:T(128)S(1)} %reshape.45.bc_next, ...), custom_call_target="tpu_custom_call", output_to_operand_aliasing={{}: (11, {})} | custom-call | flops 402653184 | bytes 1048576 | tf_op jit(solution)/shard_map/pallas_call | solution.py:90
  139.6 0.0 collective-permute-done.16.f4
  139.7 3.0 %shard_map.66 = bf16[4,256,1024]{2,1,0:T(8,128)(2,1)} custom-call(s32[1]{0:T(128)} %bitcast.place, s32[1,128]{1,0:T(1,128)S(1)} %add.58.table, s32[1,128]{1,0:T(1,128)S(1)} %collective-permute-done.13.rest, s32[8]{0:T(128)S(1)} %reshape_squeeze.3.bc_here, s32[8]{0:T(128)S(1)} %reshape.45.bc_next, ...), custom_call_target="tpu_custom_call", output_to_operand_aliasing={{}: (11, {})} | custom-call | flops 402653184 | bytes 1048576 | tf_op jit(solution)/shard_map/pallas_call | solution.py:90
  (25 shorter events, 0.1 us)
Async XLA Ops:
  0.0 14.1 %copy-start.1 = (s32[1,1,4,3]{2,1,3,0:T(1,128)S(1)}, s32[1,1,4,3]{2,1,3,0:T(1,128)}, u32[]{:S(2)}) copy-start(s32[1,1,4,3]{2,1,3,0:T(1,128)} %param.7) | copy-start | bytes 148
  0.0 14.3 %copy-start.3 = (s32[1,1,4]{2,1,0:T(1,128)S(1)}, s32[1,1,4]{2,1,0:T(1,128)}, u32[]{:S(2)}) copy-start(s32[1,1,4]{2,1,0:T(1,128)} %param.8) | copy-start | bytes 52
  0.0 14.4 %copy-start.4 = (s32[1,2]{1,0:T(1,128)S(1)}, s32[1,2]{1,0:T(1,128)}, u32[]{:S(2)}) copy-start(s32[1,2]{1,0:T(1,128)} %param.9) | copy-start | bytes 28
  0.0 31.1 %copy-start.2 = (s32[1,1,4,2]{2,3,1,0:T(2,128)S(1)}, s32[1,1,4,2]{2,3,1,0:T(2,128)}, u32[]{:S(2)}) copy-start(s32[1,1,4,2]{2,3,1,0:T(2,128)} %param.11) | copy-start | bytes 100
  0.0 85.1 %copy-start = (bf16[1,1,4,256,512]{4,3,2,1,0:T(8,128)(2,1)S(1)}, bf16[1,1,4,256,512]{4,3,2,1,0:T(8,128)(2,1)}, u32[]{:S(2)}) copy-start(bf16[1,1,4,256,512]{4,3,2,1,0:T(8,128)(2,1)} %param.10) | copy-start | bytes 3145732
  0.0 59.8 %all-to-all-start = ((bf16[32,96,256]{2,1,0:T(8,128)(2,1)}), bf16[32,96,256]{2,1,0:T(8,128)(2,1)S(1)}, u32[]{:S(2)}, u32[]{:S(2)}) async-start(bf16[32,96,256]{2,1,0:T(8,128)(2,1)} %bitcast.26), calls=%async_computation | async-start | bytes 3145728 | tf_op jit(solution)/shard_map/all_to_all | solution.py:129
  14.6 34.0 %collective-permute-start = (s32[1,128]{1,0:T(1,128)S(1)}, s32[1,128]{1,0:T(1,128)S(1)}, u32[]{:S(2)}, u32[]{:S(2)}) collective-permute-start(s32[1,128]{1,0:T(1,128)S(1)} %pad.4), channel_id=1, source_target_pairs={{0,16},{16,32},{32,48},{48,64},{64,80},{80,96},{96,112},{112,0},{1... | collective-permute-start | bytes 1544 | tf_op jit(solution)/shard_map/ppermute | solution.py:122
  18.0 33.8 %collective-permute-start.1 = (s32[1,128]{1,0:T(1,128)S(1)}, s32[1,128]{1,0:T(1,128)S(1)}, u32[]{:S(2)}, u32[]{:S(2)}) collective-permute-start(s32[1,128]{1,0:T(1,128)S(1)} %pad.4), channel_id=1, source_target_pairs={{0,32},{16,48},{32,64},{48,80},{64,96},{80,112},{96,0},{112,16},{1... | collective-permute-start | bytes 1544 | tf_op jit(solution)/shard_map/ppermute | solution.py:122
  22.2 37.5 %collective-permute-start.2 = (s32[1,128]{1,0:T(1,128)S(1)}, s32[1,128]{1,0:T(1,128)S(1)}, u32[]{:S(2)}, u32[]{:S(2)}) collective-permute-start(s32[1,128]{1,0:T(1,128)S(1)} %pad.4), channel_id=1, source_target_pairs={{0,48},{16,64},{32,80},{48,96},{64,112},{80,0},{96,16},{112,32},{1... | collective-permute-start | bytes 1544 | tf_op jit(solution)/shard_map/ppermute | solution.py:122
  26.9 32.9 %collective-permute-start.3 = (s32[1,128]{1,0:T(1,128)S(1)}, s32[1,128]{1,0:T(1,128)S(1)}, u32[]{:S(2)}, u32[]{:S(2)}) collective-permute-start(s32[1,128]{1,0:T(1,128)S(1)} %pad.4), channel_id=1, source_target_pairs={{0,64},{16,80},{32,96},{48,112},{64,0},{80,16},{96,32},{112,48},{1... | collective-permute-start | bytes 1544 | tf_op jit(solution)/shard_map/ppermute | solution.py:122
  31.1 12.7 %collective-permute-start.7 = (s32[4,2]{0,1:T(2,128)S(1)}, s32[4,2]{0,1:T(2,128)S(1)}, u32[]{:S(2)}, u32[]{:S(2)}) collective-permute-start(s32[4,2]{0,1:T(2,128)S(1)} %bitcast.27), channel_id=1, source_target_pairs={{1,0},{2,1},{3,2},{4,3},{5,4},{6,5},{7,6},{8,7},{9,8},{10,9},{11,1... | collective-permute-start | bytes 104 | tf_op jit(solution)/shard_map/ppermute | solution.py:134
  43.8 15.9 %collective-permute-start.4 = (s32[1,128]{1,0:T(1,128)S(1)}, s32[1,128]{1,0:T(1,128)S(1)}, u32[]{:S(2)}, u32[]{:S(2)}) collective-permute-start(s32[1,128]{1,0:T(1,128)S(1)} %pad.4), channel_id=1, source_target_pairs={{0,80},{16,96},{32,112},{48,0},{64,16},{80,32},{96,48},{112,64},{1... | collective-permute-start | bytes 1544 | tf_op jit(solution)/shard_map/ppermute | solution.py:122
  48.5 11.2 %collective-permute-start.5 = (s32[1,128]{1,0:T(1,128)S(1)}, s32[1,128]{1,0:T(1,128)S(1)}, u32[]{:S(2)}, u32[]{:S(2)}) collective-permute-start(s32[1,128]{1,0:T(1,128)S(1)} %pad.4), channel_id=1, source_target_pairs={{0,96},{16,112},{32,0},{48,16},{64,32},{80,48},{96,64},{112,80},{1... | collective-permute-start | bytes 1544 | tf_op jit(solution)/shard_map/ppermute | solution.py:122
  51.7 8.0 %collective-permute-start.6 = (s32[1,128]{1,0:T(1,128)S(1)}, s32[1,128]{1,0:T(1,128)S(1)}, u32[]{:S(2)}, u32[]{:S(2)}) collective-permute-start(s32[1,128]{1,0:T(1,128)S(1)} %pad.4), channel_id=1, source_target_pairs={{0,112},{16,0},{32,16},{48,32},{64,48},{80,64},{96,80},{112,96},{1... | collective-permute-start | bytes 1544 | tf_op jit(solution)/shard_map/ppermute | solution.py:122
  59.8 18.2 %collective-permute-start.8 = (s32[1,128]{1,0:T(1,128)S(1)}, s32[1,128]{1,0:T(1,128)S(1)}, u32[]{:S(2)}, u32[]{:S(2)}) collective-permute-start(s32[1,128]{1,0:T(1,128)S(1)} %add_add_fusion), channel_id=1, source_target_pairs={{0,128},{128,0},{256,384},{384,256},{1,129},{129,1},{257,385},{385... | collective-permute-start | bytes 1544 | tf_op jit(solution)/shard_map/ppermute | solution.py:138
  78.0 10.9 %collective-permute-start.9 = (bf16[2,384,256]{2,1,0:T(8,128)(2,1)S(1)}, bf16[2,384,256]{2,1,0:T(8,128)(2,1)S(1)}, u32[]{:S(2)}, u32[]{:S(2)}) collective-permute-start(bf16[2,384,256]{2,1,0:T(8,128)(2,1)S(1)} %all_gather.3.own), channel_id=1, source_target_pairs={{0,16},{16,32},{32,48},{48,64},{64,80},{80,96},{96,112},{112,0},{1... | collective-permute-start | bytes 1179656 | tf_op jit(solution)/shard_map/ppermute | solution.py:149
  81.2 9.7 %collective-permute-start.11 = (bf16[2,384,256]{2,1,0:T(8,128)(2,1)S(1)}, bf16[2,384,256]{2,1,0:T(8,128)(2,1)S(1)}, u32[]{:S(2)}, u32[]{:S(2)}) collective-permute-start(bf16[2,384,256]{2,1,0:T(8,128)(2,1)S(1)} %all_gather.3.own), channel_id=1, source_target_pairs={{0,112},{16,0},{32,16},{48,32},{64,48},{80,64},{96,80},{112,96},{1... | collective-permute-start | bytes 1179656 | tf_op jit(solution)/shard_map/ppermute | solution.py:150
  85.1 46.5 %collective-permute-start.18 = (bf16[4,256,512]{2,1,0:T(8,128)(2,1)S(1)}, bf16[4,256,512]{2,1,0:T(8,128)(2,1)S(1)}, u32[]{:S(2)}, u32[]{:S(2)}) collective-permute-start(bf16[4,256,512]{2,1,0:T(8,128)(2,1)S(1)} %bitcast.22), channel_id=1, source_target_pairs={{1,0},{2,1},{3,2},{4,3},{5,4},{6,5},{7,6},{8,7},{9,8},{10,9},{11,1... | collective-permute-start | bytes 3145736 | tf_op jit(solution)/shard_map/ppermute | solution.py:144
  88.9 24.7 %collective-permute-start.10 = (bf16[2,384,256]{2,1,0:T(8,128)(2,1)S(1)}, bf16[2,384,256]{2,1,0:T(8,128)(2,1)S(1)}, u32[]{:S(2)}, u32[]{:S(2)}) collective-permute-start(bf16[2,384,256]{2,1,0:T(8,128)(2,1)S(1)} %collective-permute-done.9.f1), channel_id=1, source_target_pairs={{0,16},{16,32},{32,48},{48,64},{64,80},{80,96},{96,112},{112,0},{1... | collective-permute-start | bytes 1179656 | tf_op jit(solution)/shard_map/ppermute | solution.py:149
  90.9 22.7 %collective-permute-start.12 = (bf16[2,384,256]{2,1,0:T(8,128)(2,1)S(1)}, bf16[2,384,256]{2,1,0:T(8,128)(2,1)S(1)}, u32[]{:S(2)}, u32[]{:S(2)}) collective-permute-start(bf16[2,384,256]{2,1,0:T(8,128)(2,1)S(1)} %collective-permute-done.11.b1), channel_id=1, source_target_pairs={{0,112},{16,0},{32,16},{48,32},{64,48},{80,64},{96,80},{112,96},{1... | collective-permute-start | bytes 1179656 | tf_op jit(solution)/shard_map/ppermute | solution.py:150
  96.0 17.7 %collective-permute-start.13 = (s32[1,128]{1,0:T(1,128)S(1)}, s32[1,128]{1,0:T(1,128)S(1)}, u32[]{:S(2)}, u32[]{:S(2)}) collective-permute-start(s32[1,128]{1,0:T(1,128)S(1)} %add.58.table), channel_id=1, source_target_pairs={{0,256},{128,384},{256,0},{384,128},{1,257},{129,385},{257,1},{385... | collective-permute-start | bytes 1544 | tf_op jit(solution)/shard_map/ppermute | solution.py:145
  113.6 10.9 %collective-permute-start.14 = (bf16[2,384,256]{2,1,0:T(8,128)(2,1)S(1)}, bf16[2,384,256]{2,1,0:T(8,128)(2,1)S(1)}, u32[]{:S(2)}, u32[]{:S(2)}) collective-permute-start(bf16[2,384,256]{2,1,0:T(8,128)(2,1)S(1)} %collective-permute-done.10.f2), channel_id=1, source_target_pairs={{0,16},{16,32},{32,48},{48,64},{64,80},{80,96},{96,112},{112,0},{1... | collective-permute-start | bytes 1179656 | tf_op jit(solution)/shard_map/ppermute | solution.py:149
  115.5 10.9 %collective-permute-start.15 = (bf16[2,384,256]{2,1,0:T(8,128)(2,1)S(1)}, bf16[2,384,256]{2,1,0:T(8,128)(2,1)S(1)}, u32[]{:S(2)}, u32[]{:S(2)}) collective-permute-start(bf16[2,384,256]{2,1,0:T(8,128)(2,1)S(1)} %collective-permute-done.12.b2), channel_id=1, source_target_pairs={{0,112},{16,0},{32,16},{48,32},{64,48},{80,64},{96,80},{112,96},{1... | collective-permute-start | bytes 1179656 | tf_op jit(solution)/shard_map/ppermute | solution.py:150
  124.5 15.1 %collective-permute-start.16 = (bf16[2,192,256]{2,1,0:T(8,128)(2,1)S(1)}, bf16[2,192,256]{2,1,0:T(8,128)(2,1)S(1)}, u32[]{:S(2)}, u32[]{:S(2)}) collective-permute-start(bf16[2,192,256]{2,1,0:T(8,128)(2,1)S(1)} %slice.16), channel_id=1, source_target_pairs={{0,16},{16,32},{32,48},{48,64},{64,80},{80,96},{96,112},{112,0},{1... | collective-permute-start | bytes 589832 | tf_op jit(solution)/shard_map/ppermute | solution.py:153
  126.5 13.2 %collective-permute-start.17 = (bf16[2,192,256]{2,1,0:T(8,128)(2,1)S(1)}, bf16[2,192,256]{2,1,0:T(8,128)(2,1)S(1)}, u32[]{:S(2)}, u32[]{:S(2)}) collective-permute-start(bf16[2,192,256]{2,1,0:T(8,128)(2,1)S(1)} %slice.17), channel_id=1, source_target_pairs={{0,112},{16,0},{32,16},{48,32},{64,48},{80,64},{96,80},{112,96},{1... | collective-permute-start | bytes 589832 | tf_op jit(solution)/shard_map/ppermute | solution.py:154

commit v4 on v3

--- a/solution.py
+++ b/solution.py
@@ -18,6 +18,7 @@
 PIECES = Y_LO * Z
 PIECE = MB * NZA * BS // PIECES
 SPAN = Y_LO * PIECE
+META = 8
 
 
 def z_route(distance):
@@ -29,7 +30,7 @@
 
 
 def block_rows(rounds, ints, refs, b_refs, out, a_s, o_s, acc, sem, osem):
-    place, table, rest, b_columns = ints[0], ints[1], ints[2], ints[3:]
+    place, table, b_columns = ints[0], ints[1], ints[2:]
     z = place[0]
     copies = []
     for n, (ref, away, start, rows) in enumerate(refs):
@@ -47,12 +48,11 @@
         for k in range(2):
             for s in range(NZA):
                 base = k * EACH
-                live = table[0, base + MB * NZA + i] + rest[0, base + MB * NZA + i]
+                live = table[base + MB * NZA + i]
 
                 @pl.when(s < live)
                 def _():
-                    at = base + i * NZA + s
-                    q = table[0, at] + rest[0, at]
+                    q = table[base + i * NZA + s]
                     row = pl.multiple_of((i * NZA + s) * BS, BS)
                     product = jnp.dot(a_s[k, pl.ds(row, BS), :], b_refs[k][q], preferred_element_type=jnp.float32)
                     for t in range(NZB):
@@ -67,20 +67,20 @@
         w.wait()
 
 
-def two_rows(place, table, rest, bc_here, bc_next, own, f1, b1, f2, b2, b_here, b_next, out, *scratch):
+def two_rows(place, table, bc_here, bc_next, own, f1, b1, f2, b2, b_here, b_next, out, *scratch):
     refs = [(own, 0, 0, SPAN), (f1, -1, 0, SPAN), (b1, 1, 0, SPAN), (f2, -2, 0, SPAN), (b2, 2, 0, SPAN)]
-    block_rows([(0, 0, 0), (1, -2, 1)], (place, table, rest, bc_here, bc_next), refs, (b_here, b_next), out, *scratch)
+    block_rows([(0, 0, 0), (1, -2, 1)], (place, table, bc_here, bc_next), refs, (b_here, b_next), out, *scratch)
 
 
-def third_row(place, table, rest, bc_here, bc_next, f2, b2, f3, b3, b_here, b_next, before, out, *scratch):
+def third_row(place, table, bc_here, bc_next, f2, b2, f3, b3, b_here, b_next, before, out, *scratch):
     refs = [(f2, -2, 0, SPAN), (b2, 2, 0, SPAN), (f3, -3, 0, SPAN), (b3, 3, 0, SPAN)]
-    block_rows([(0, 2, -3)], (place, table, rest, bc_here, bc_next), refs, (b_here, b_next), out, *scratch)
+    block_rows([(0, 2, -3)], (place, table, bc_here, bc_next), refs, (b_here, b_next), out, *scratch)
 
 
-def last_row(place, table, rest, bc_here, bc_next, f3, b3, f4, b4, b_here, b_next, before, out, *scratch):
+def last_row(place, table, bc_here, bc_next, f3, b3, f4, b4, b_here, b_next, before, out, *scratch):
     half = SPAN // 2
     refs = [(f3, -3, 0, SPAN), (b3, 3, 0, SPAN), (f4, 4, 0, half), (b4, 4, half, half)]
-    block_rows([(0, 4, 3)], (place, table, rest, bc_here, bc_next), refs, (b_here, b_next), out, *scratch)
+    block_rows([(0, 4, 3)], (place, table, bc_here, bc_next), refs, (b_here, b_next), out, *scratch)
 
 
 def call(kernel, rows, ints, pieces, b_pair, before):
@@ -112,50 +112,69 @@
 EACH = MB * NZA + MB
 
 
-def masked_ints(a_columns, a_live, holder):
-    mine = jnp.concatenate([a_columns.reshape(-1), a_live.reshape(-1)])
-    here = lax.axis_index(ROW) == holder
-    table = jnp.where(here[:, None], mine[None, :], 0).reshape(1, -1)
-    table = jnp.pad(table, ((0, 0), (0, 128 - table.shape[1])))
-    total = table
-    for distance in range(1, Z):
-        total = total + lax.ppermute(table, "z", z_route(distance))
-    return total
+def payload_rows(a_columns, a_live, tile, out, rows, sem):
+    copy = pltpu.make_async_copy(tile, out.at[:, :PIECE], sem.at[0])
+    copy.start()
+    lane = lax.broadcasted_iota(jnp.int32, (META, BS), 1)
+    row = jnp.zeros((META, BS), jnp.int32)
+    for i in range(MB):
+        for s in range(NZA):
+            row = jnp.where(lane == i * NZA + s, a_columns[i, s], row)
+        row = jnp.where(lane == MB * NZA + i, a_live[i], row)
+    rows[...] = jnp.broadcast_to(row.astype(jnp.float32).astype(jnp.bfloat16)[None], rows.shape)
+    below = pltpu.make_async_copy(rows, out.at[:, PIECE:], sem.at[1])
+    below.start()
+    copy.wait()
+    below.wait()
+
+
+def payload(a_columns, a_live, tile):
+    return pl.pallas_call(
+        payload_rows,
+        out_shape=jax.ShapeDtypeStruct((PIECES, PIECE + META, BS), jnp.bfloat16),
+        grid_spec=pltpu.PrefetchScalarGridSpec(
+            num_scalar_prefetch=2,
+            grid=(),
+            in_specs=[pl.BlockSpec(memory_space=pltpu.HBM)],
+            out_specs=pl.BlockSpec(memory_space=pl.ANY),
+            scratch_shapes=[
+                pltpu.VMEM((PIECES, META, BS), jnp.bfloat16),
+                pltpu.SemaphoreType.DMA((2,)),
+            ],
+        ),
+        compiler_params=pltpu.CompilerParams(vmem_limit_bytes=4 * 1024 * 1024),
+    )(a_columns, a_live, tile)
 
 
 def on_device(a_blocks, a_columns, a_live, owner_map, b_blocks, b_columns):
     tile = a_blocks.reshape(PIECES, PIECE, BS)
     cols = lax.axis_size(COL)
-    got = lax.all_to_all(tile, ("z", "y_lo"), 0, 0, tiled=True)
+    got = lax.all_to_all(payload(a_columns[0, 0], a_live[0, 0], tile), ("z", "y_lo"), 0, 0, tiled=True)
     holder = owner_map[0]
     source = (holder % Z) * Y_LO + holder // Z
-    table = masked_ints(a_columns, a_live, holder)
     bc_here = b_columns[0, 0]
     bc_next = lax.ppermute(bc_here, COL, col_route(cols)).reshape(-1)
     bc_here = bc_here.reshape(-1)
-    got, table, bc_here, bc_next = lax.optimization_barrier((got, table, bc_here, bc_next))
+    place = lax.axis_index("z").astype(jnp.int32)[None]
+    got, bc_here, bc_next, place = lax.optimization_barrier((got, bc_here, bc_next, place))
 
-    first = lax.ppermute(table, "y_lo", [(i, i ^ 1) for i in range(Y_LO)])
     two = jnp.stack([lax.dynamic_index_in_dim(got, source[k], 0, keepdims=False) for k in range(2)])
-    own = lax.all_gather(two, "y_lo", axis=1, tiled=True)
-    own, first = lax.optimization_barrier((own, first))
+    table = two[:, PIECE, :EACH].astype(jnp.int32).reshape(-1)
+    own = lax.all_gather(two[:, :PIECE], "y_lo", axis=1, tiled=True)
     b_here = b_blocks[0, 0]
-    b_ready, own, table = lax.optimization_barrier((b_here, own, table + first))
+    b_ready, own, table = lax.optimization_barrier((b_here, own, table))
     b_next = lax.ppermute(b_ready, COL, col_route(cols))
-    rest = lax.ppermute(table, "y_lo", [(i, i ^ 2) for i in range(Y_LO)])
     ahead = [own]
     back = [own]
     for step in range(3):
         ahead.append(lax.ppermute(ahead[-1], "z", z_route(1)))
         back.append(lax.ppermute(back[-1], "z", z_route(-1)))
-        if step == 1:
-            ahead[2], back[2], rest = lax.optimization_barrier((ahead[2], back[2], rest))
+    b_pair = (b_here, b_next)
+    ints = (place, table, bc_here, bc_next)
+    window = call(two_rows, 2, ints, (own, ahead[1], back[1], ahead[2], back[2]), b_pair, None)
+    window, ahead[3], back[3] = lax.optimization_barrier((window, ahead[3], back[3]))
     f4 = lax.ppermute(ahead[3][:, : SPAN // 2], "z", z_route(1))
     b4 = lax.ppermute(back[3][:, SPAN // 2 :], "z", z_route(-1))
-
-    b_pair = (b_here, b_next)
-    ints = (lax.axis_index("z").astype(jnp.int32)[None], table, rest, bc_here, bc_next)
-    window = call(two_rows, 2, ints, (own, ahead[1], back[1], ahead[2], back[2]), b_pair, None)
     window = call(third_row, 1, ints, (ahead[2], back[2], ahead[3], back[3]), b_pair, window)
     window = call(last_row, 1, ints, (ahead[3], back[3], f4, b4), b_pair, window)
     return window[None, None]

time: 143 us -> 133 us (0.930)
  the two profiles are of different devices: /device:TPU:8 before, /device:TPU:7 now
where the time goes in v4:
time: 133 us
  waiting for transfers between devices  49.7 us (37%)
  starting transfers between devices  49.5 us (37%)
  Pallas kernels  13.3 us (10%)
  blocking collectives  12 us (9%)
  between operations  3.96 us (3%)
  local copies, waits for them, and re-layouts  3.92 us (3%)
    ppermute x1, waiting for transfers between devices, on_device(): bc_next = lax.ppermute(bc_here, COL, col_route(cols)).reshape(-1)  27.3 us
    ppermute x3, starting transfers between devices, on_device(): back.append(lax.ppermute(back[-1], 'z', z_route(-1)))  14.8 us
    all_to_all x1, starting transfers between devices, on_device(): lax.all_to_all(payload(a_columns[0, 0], a_live[0, 0], tile), ('z', 'y_lo'...  13.6 us
    all_gather x1, blocking collectives, on_device(): own = lax.all_gather(two[:, :PIECE], 'y_lo', axis=1, tiled=True)  12 us
    pallas_call x3, Pallas kernels, call(): pl.pallas_call(kernel, out_shape=jax.ShapeDtypeStruct((MB, BS, NB * BS),...  11.6 us
    ppermute x1, waiting for transfers between devices, on_device(): b_next = lax.ppermute(b_ready, COL, col_route(cols))  9.46 us
    ppermute x1, starting transfers between devices, on_device(): b_next = lax.ppermute(b_ready, COL, col_route(cols))  6.59 us
    all_to_all x1, waiting for transfers between devices, on_device(): lax.all_to_all(payload(a_columns[0, 0], a_live[0, 0], tile), ('z', 'y_lo'...  6.02 us
  transfers between devices with their start and end apart: 11, of which 5 were waited for; matrix products, arithmetic and copies ran while one was open for 1% of the time, Pallas kernels for 6%

profile of v4, /device:TPU:7, one launch (start us, length us, event | category | flops | bytes accessed | tf_op | source)
XLA Modules:
  0.0 132.5 jit_solution(8596337918972117740)
XLA Ops:
  0.0 0.8 copy.12
  0.8 0.0 copy-start.1
  0.8 1.4 %copy-done.1 = bf16[1,1,4,3,256,256]{5,4,3,2,1,0:T(8,128)(2,1)S(1)} copy-done((bf16[1,1,4,3,256,256]{5,4,3,2,1,0:T(8,128)(2,1)S(1)}, bf16[1,1,4,3,256,256]{5,4,3,2,1,0:T(8,128)(2,1)}, u32[]{:S(2)}) %copy-start.1) | copy-done | bytes 1572888
  2.2 0.0 copy-start.2
  2.2 0.7 copy-done.2
  2.8 1.8 %shard_map.64 = bf16[32,104,256]{2,1,0:T(8,128)(2,1)} custom-call(s32[4,3]{1,0:T(4,128)S(1)} %bitcast.27, s32[4]{0:T(128)S(1)} %bitcast.28, bf16[32,96,256]{2,1,0:T(8,128)(2,1)S(1)} %bitcast.26), custom_call_target="tpu_custom_call" | custom-call | tf_op jit(solution)/shard_map/pallas_call | solution.py:132
  4.6 0.0 copy-start.3
  4.6 0.0 copy-start.4
  4.6 0.0 copy-start
  4.6 13.6 %all-to-all-start = ((bf16[32,104,256]{2,1,0:T(8,128)(2,1)}), bf16[32,104,256]{2,1,0:T(8,128)(2,1)S(1)}, u32[]{:S(2)}, u32[]{:S(2)}) async-start(bf16[32,104,256]{2,1,0:T(8,128)(2,1)} %shard_map.64), calls=%async_computation | async-start | bytes 3407872 | tf_op jit(solution)/shard_map/all_to_all | solution.py:152
  18.2 0.0 copy-done.3
  18.3 2.9 %collective-permute-start = (s32[4,2]{0,1:T(2,128)S(1)}, s32[4,2]{0,1:T(2,128)S(1)}, u32[]{:S(2)}, u32[]{:S(2)}) collective-permute-start(s32[4,2]{0,1:T(2,128)S(1)} %bitcast.29), channel_id=1, source_target_pairs={{1,0},{2,1},{3,2},{4,3},{5,4},{6,5},{7,6},{8,7},{9,8},{10,9},{11,1... | collective-permute-start | bytes 104 | tf_op jit(solution)/shard_map/ppermute | solution.py:156
  21.1 0.0 copy-done.4
  21.2 0.6 fusion.5
  24.2 0.1 copy.13
  24.3 0.1 reshape_squeeze.3.bc_here
  25.6 27.3 %collective-permute-done = s32[4,2]{0,1:T(2,128)S(1)} collective-permute-done((s32[4,2]{0,1:T(2,128)S(1)}, s32[4,2]{0,1:T(2,128)S(1)}, u32[]{:S(2)}, u32[]{:S(2)}) %collective-permute-start) | collective-permute-done | bytes 64 | tf_op jit(solution)/shard_map/ppermute | solution.py:156
  52.9 0.1 copy.14
  53.0 0.1 reshape.11.bc_next
  53.1 6.0 %all-to-all-done = bf16[32,104,256]{2,1,0:T(8,128)(2,1)S(1)} async-done(((bf16[32,104,256]{2,1,0:T(8,128)(2,1)}), bf16[32,104,256]{2,1,0:T(8,128)(2,1)S(1)}, u32[]{:S(2)}, u32[]{:S(2)}) %all-to-all-start) | async-done | bytes 1703968 | tf_op jit(solution)/shard_map/all_to_all | solution.py:152
  59.2 0.1 reshape.12.table
  59.2 12.0 %all_gather.3.own = bf16[2,384,256]{2,1,0:T(8,128)(2,1)S(1)} all-gather(bf16[2,96,256]{2,1,0:T(8,128)(2,1)S(1)} %fusion), channel_id=1, replica_groups=mesh['y_lo'=4,'z'=8,'y_hi'=2,'x'=4,'core'=2] {'y_lo'}, dimensions={1}, use_global_device_ids=true | all-gather | bytes 491520 | tf_op jit(solution)/shard_map/all_gather | solution.py:163
  71.3 5.3 %collective-permute-start.2 = (bf16[2,384,256]{2,1,0:T(8,128)(2,1)S(1)}, bf16[2,384,256]{2,1,0:T(8,128)(2,1)S(1)}, u32[]{:S(2)}, u32[]{:S(2)}) collective-permute-start(bf16[2,384,256]{2,1,0:T(8,128)(2,1)S(1)} %all_gather.3.own), channel_id=1, source_target_pairs={{0,112},{16,0},{32,16},{48,32},{64,48},{80,64},{96,80},{112,96},{1... | collective-permute-start | bytes 1179656 | tf_op jit(solution)/shard_map/ppermute | solution.py:171
  76.5 1.9 %collective-permute-start.1 = (bf16[2,384,256]{2,1,0:T(8,128)(2,1)S(1)}, bf16[2,384,256]{2,1,0:T(8,128)(2,1)S(1)}, u32[]{:S(2)}, u32[]{:S(2)}) collective-permute-start(bf16[2,384,256]{2,1,0:T(8,128)(2,1)S(1)} %all_gather.3.own), channel_id=1, source_target_pairs={{0,16},{16,32},{32,48},{48,64},{64,80},{80,96},{96,112},{112,0},{1... | collective-permute-start | bytes 1179656 | tf_op jit(solution)/shard_map/ppermute | solution.py:170
  78.5 0.0 copy-done
  78.5 6.6 %collective-permute-start.5 = (bf16[4,256,512]{2,1,0:T(8,128)(2,1)S(1)}, bf16[4,256,512]{2,1,0:T(8,128)(2,1)S(1)}, u32[]{:S(2)}, u32[]{:S(2)}) collective-permute-start(bf16[4,256,512]{2,1,0:T(8,128)(2,1)S(1)} %bitcast.22), channel_id=1, source_target_pairs={{1,0},{2,1},{3,2},{4,3},{5,4},{6,5},{7,6},{8,7},{9,8},{10,9},{11,1... | collective-permute-start | bytes 3145736 | tf_op jit(solution)/shard_map/ppermute | solution.py:166
  85.1 0.0 collective-permute-done.2.b1
  85.1 4.2 %collective-permute-start.4 = (bf16[2,384,256]{2,1,0:T(8,128)(2,1)S(1)}, bf16[2,384,256]{2,1,0:T(8,128)(2,1)S(1)}, u32[]{:S(2)}, u32[]{:S(2)}) collective-permute-start(bf16[2,384,256]{2,1,0:T(8,128)(2,1)S(1)} %collective-permute-done.2.b1), channel_id=1, source_target_pairs={{0,112},{16,0},{32,16},{48,32},{64,48},{80,64},{96,80},{112,96},{1... | collective-permute-start | bytes 1179656 | tf_op jit(solution)/shard_map/ppermute | solution.py:171
  89.3 0.0 collective-permute-done.1.f1
  89.3 1.9 %collective-permute-start.3 = (bf16[2,384,256]{2,1,0:T(8,128)(2,1)S(1)}, bf16[2,384,256]{2,1,0:T(8,128)(2,1)S(1)}, u32[]{:S(2)}, u32[]{:S(2)}) collective-permute-start(bf16[2,384,256]{2,1,0:T(8,128)(2,1)S(1)} %collective-permute-done.1.f1), channel_id=1, source_target_pairs={{0,16},{16,32},{32,48},{48,64},{64,80},{80,96},{96,112},{112,0},{1... | collective-permute-start | bytes 1179656 | tf_op jit(solution)/shard_map/ppermute | solution.py:170
  91.2 4.5 %collective-permute-done.4.b2 = bf16[2,384,256]{2,1,0:T(8,128)(2,1)S(1)} collective-permute-done((bf16[2,384,256]{2,1,0:T(8,128)(2,1)S(1)}, bf16[2,384,256]{2,1,0:T(8,128)(2,1)S(1)}, u32[]{:S(2)}, u32[]{:S(2)}) %collective-permute-start.4) | collective-permute-done | bytes 393248 | tf_op jit(solution)/shard_map/ppermute | solution.py:171
  95.8 5.3 %collective-permute-start.7 = (bf16[2,384,256]{2,1,0:T(8,128)(2,1)S(1)}, bf16[2,384,256]{2,1,0:T(8,128)(2,1)S(1)}, u32[]{:S(2)}, u32[]{:S(2)}) collective-permute-start(bf16[2,384,256]{2,1,0:T(8,128)(2,1)S(1)} %collective-permute-done.4.b2), channel_id=1, source_target_pairs={{0,112},{16,0},{32,16},{48,32},{64,48},{80,64},{96,80},{112,96},{1... | collective-permute-start | bytes 1179656 | tf_op jit(solution)/shard_map/ppermute | solution.py:171
  101.1 0.0 collective-permute-done.3.f2
  101.1 1.9 %collective-permute-start.6 = (bf16[2,384,256]{2,1,0:T(8,128)(2,1)S(1)}, bf16[2,384,256]{2,1,0:T(8,128)(2,1)S(1)}, u32[]{:S(2)}, u32[]{:S(2)}) collective-permute-start(bf16[2,384,256]{2,1,0:T(8,128)(2,1)S(1)} %collective-permute-done.3.f2), channel_id=1, source_target_pairs={{0,16},{16,32},{32,48},{48,64},{64,80},{80,96},{96,112},{112,0},{1... | collective-permute-start | bytes 1179656 | tf_op jit(solution)/shard_map/ppermute | solution.py:170
  103.0 9.5 %collective-permute-done.5.b_next = bf16[4,256,512]{2,1,0:T(8,128)(2,1)S(1)} collective-permute-done((bf16[4,256,512]{2,1,0:T(8,128)(2,1)S(1)}, bf16[4,256,512]{2,1,0:T(8,128)(2,1)S(1)}, u32[]{:S(2)}, u32[]{:S(2)}) %collective-permute-start.5) | collective-permute-done | bytes 1048608 | tf_op jit(solution)/shard_map/ppermute | solution.py:166
  112.5 5.0 %shard_map.65.before = bf16[4,256,1024]{2,1,0:T(8,128)(2,1)} custom-call(s32[1]{0:T(128)} %bitcast.4.place, s32[32]{0:T(128)S(1)} %reshape.12.table, s32[8]{0:T(128)S(1)} %reshape_squeeze.3.bc_here, s32[8]{0:T(128)S(1)} %reshape.11.bc_next, bf16[2,384,256]{2,1,0:T(8,128)(2,1)S(1)} %all_gather.3.own, bf16[2,384,256]{2,1,0:T(8,128)(2,1)S(1)} %collective-permute-done.1.f1, ...), custom_call_target="tpu_custom_call" | custom-call | flops 805306368 | bytes 2097152 | tf_op jit(solution)/shard_map/pallas_call | solution.py:90
  117.5 0.0 collective-permute-done.7.b3
  117.5 0.0 collective-permute-done.6.f3
  117.6 4.0 %collective-permute-start.9 = (bf16[2,192,256]{2,1,0:T(8,128)(2,1)S(1)}, bf16[2,192,256]{2,1,0:T(8,128)(2,1)S(1)}, u32[]{:S(2)}, u32[]{:S(2)}) collective-permute-start(bf16[2,192,256]{2,1,0:T(8,128)(2,1)S(1)} %slice.23), channel_id=1, source_target_pairs={{0,112},{16,0},{32,16},{48,32},{64,48},{80,64},{96,80},{112,96},{1... | collective-permute-start | bytes 589832 | tf_op jit(solution)/shard_map/ppermute | solution.py:177
  121.6 1.9 %collective-permute-start.8 = (bf16[2,192,256]{2,1,0:T(8,128)(2,1)S(1)}, bf16[2,192,256]{2,1,0:T(8,128)(2,1)S(1)}, u32[]{:S(2)}, u32[]{:S(2)}) collective-permute-start(bf16[2,192,256]{2,1,0:T(8,128)(2,1)S(1)} %slice.22), channel_id=1, source_target_pairs={{0,16},{16,32},{32,48},{48,64},{64,80},{80,96},{96,112},{112,0},{1... | collective-permute-start | bytes 589832 | tf_op jit(solution)/shard_map/ppermute | solution.py:176
  123.5 3.3 %shard_map.66.before = bf16[4,256,1024]{2,1,0:T(8,128)(2,1)} custom-call(s32[1]{0:T(128)} %bitcast.4.place, s32[32]{0:T(128)S(1)} %reshape.12.table, s32[8]{0:T(128)S(1)} %reshape_squeeze.3.bc_here, s32[8]{0:T(128)S(1)} %reshape.11.bc_next, bf16[2,384,256]{2,1,0:T(8,128)(2,1)S(1)} %collective-permute-done.3.f2, ...), custom_call_target="tpu_custom_call", output_to_operand_aliasing={{}: (10, {})} | custom-call | flops 402653184 | bytes 1048576 | tf_op jit(solution)/shard_map/pallas_call | solution.py:90
  126.8 0.0 collective-permute-done.9.b4
  126.8 2.4 %collective-permute-done.8.f4 = bf16[2,192,256]{2,1,0:T(8,128)(2,1)S(1)} collective-permute-done((bf16[2,192,256]{2,1,0:T(8,128)(2,1)S(1)}, bf16[2,192,256]{2,1,0:T(8,128)(2,1)S(1)}, u32[]{:S(2)}, u32[]{:S(2)}) %collective-permute-start.8) | collective-permute-done | bytes 196640 | tf_op jit(solution)/shard_map/ppermute | solution.py:176
  129.2 3.3 %shard_map.67 = bf16[4,256,1024]{2,1,0:T(8,128)(2,1)} custom-call(s32[1]{0:T(128)} %bitcast.4.place, s32[32]{0:T(128)S(1)} %reshape.12.table, s32[8]{0:T(128)S(1)} %reshape_squeeze.3.bc_here, s32[8]{0:T(128)S(1)} %reshape.11.bc_next, bf16[2,384,256]{2,1,0:T(8,128)(2,1)S(1)} %collective-permute-done.6.f3, ...), custom_call_target="tpu_custom_call", output_to_operand_aliasing={{}: (10, {})} | custom-call | flops 402653184 | bytes 1048576 | tf_op jit(solution)/shard_map/pallas_call | solution.py:90
  (6 shorter events, 0.1 us)
Async XLA Ops:
  0.8 1.4 %copy-start.1 = (bf16[1,1,4,3,256,256]{5,4,3,2,1,0:T(8,128)(2,1)S(1)}, bf16[1,1,4,3,256,256]{5,4,3,2,1,0:T(8,128)(2,1)}, u32[]{:S(2)}) copy-start(bf16[1,1,4,3,256,256]{5,4,3,2,1,0:T(8,128)(2,1)} %param.6) | copy-start | bytes 4718596
  2.2 0.7 copy-start.2
  4.6 13.7 %copy-start.3 = (s32[1,1,4,2]{2,3,1,0:T(2,128)S(1)}, s32[1,1,4,2]{2,3,1,0:T(2,128)}, u32[]{:S(2)}) copy-start(s32[1,1,4,2]{2,3,1,0:T(2,128)} %param.11) | copy-start | bytes 100
  4.6 16.5 %copy-start.4 = (s32[1,2]{1,0:T(1,128)S(1)}, s32[1,2]{1,0:T(1,128)}, u32[]{:S(2)}) copy-start(s32[1,2]{1,0:T(1,128)} %param.9) | copy-start | bytes 28
  4.6 73.9 %copy-start = (bf16[1,1,4,256,512]{4,3,2,1,0:T(8,128)(2,1)S(1)}, bf16[1,1,4,256,512]{4,3,2,1,0:T(8,128)(2,1)}, u32[]{:S(2)}) copy-start(bf16[1,1,4,256,512]{4,3,2,1,0:T(8,128)(2,1)} %param.10) | copy-start | bytes 3145732
  4.6 54.5 %all-to-all-start = ((bf16[32,104,256]{2,1,0:T(8,128)(2,1)}), bf16[32,104,256]{2,1,0:T(8,128)(2,1)S(1)}, u32[]{:S(2)}, u32[]{:S(2)}) async-start(bf16[32,104,256]{2,1,0:T(8,128)(2,1)} %shard_map.64), calls=%async_computation | async-start | bytes 3407872 | tf_op jit(solution)/shard_map/all_to_all | solution.py:152
  18.3 34.6 %collective-permute-start = (s32[4,2]{0,1:T(2,128)S(1)}, s32[4,2]{0,1:T(2,128)S(1)}, u32[]{:S(2)}, u32[]{:S(2)}) collective-permute-start(s32[4,2]{0,1:T(2,128)S(1)} %bitcast.29), channel_id=1, source_target_pairs={{1,0},{2,1},{3,2},{4,3},{5,4},{6,5},{7,6},{8,7},{9,8},{10,9},{11,1... | collective-permute-start | bytes 104 | tf_op jit(solution)/shard_map/ppermute | solution.py:156
  71.3 13.8 %collective-permute-start.2 = (bf16[2,384,256]{2,1,0:T(8,128)(2,1)S(1)}, bf16[2,384,256]{2,1,0:T(8,128)(2,1)S(1)}, u32[]{:S(2)}, u32[]{:S(2)}) collective-permute-start(bf16[2,384,256]{2,1,0:T(8,128)(2,1)S(1)} %all_gather.3.own), channel_id=1, source_target_pairs={{0,112},{16,0},{32,16},{48,32},{64,48},{80,64},{96,80},{112,96},{1... | collective-permute-start | bytes 1179656 | tf_op jit(solution)/shard_map/ppermute | solution.py:171
  76.5 12.7 %collective-permute-start.1 = (bf16[2,384,256]{2,1,0:T(8,128)(2,1)S(1)}, bf16[2,384,256]{2,1,0:T(8,128)(2,1)S(1)}, u32[]{:S(2)}, u32[]{:S(2)}) collective-permute-start(bf16[2,384,256]{2,1,0:T(8,128)(2,1)S(1)} %all_gather.3.own), channel_id=1, source_target_pairs={{0,16},{16,32},{32,48},{48,64},{64,80},{80,96},{96,112},{112,0},{1... | collective-permute-start | bytes 1179656 | tf_op jit(solution)/shard_map/ppermute | solution.py:170
  78.5 34.0 %collective-permute-start.5 = (bf16[4,256,512]{2,1,0:T(8,128)(2,1)S(1)}, bf16[4,256,512]{2,1,0:T(8,128)(2,1)S(1)}, u32[]{:S(2)}, u32[]{:S(2)}) collective-permute-start(bf16[4,256,512]{2,1,0:T(8,128)(2,1)S(1)} %bitcast.22), channel_id=1, source_target_pairs={{1,0},{2,1},{3,2},{4,3},{5,4},{6,5},{7,6},{8,7},{9,8},{10,9},{11,1... | collective-permute-start | bytes 3145736 | tf_op jit(solution)/shard_map/ppermute | solution.py:166
  85.1 10.7 %collective-permute-start.4 = (bf16[2,384,256]{2,1,0:T(8,128)(2,1)S(1)}, bf16[2,384,256]{2,1,0:T(8,128)(2,1)S(1)}, u32[]{:S(2)}, u32[]{:S(2)}) collective-permute-start(bf16[2,384,256]{2,1,0:T(8,128)(2,1)S(1)} %collective-permute-done.2.b1), channel_id=1, source_target_pairs={{0,112},{16,0},{32,16},{48,32},{64,48},{80,64},{96,80},{112,96},{1... | collective-permute-start | bytes 1179656 | tf_op jit(solution)/shard_map/ppermute | solution.py:171
  89.3 11.8 %collective-permute-start.3 = (bf16[2,384,256]{2,1,0:T(8,128)(2,1)S(1)}, bf16[2,384,256]{2,1,0:T(8,128)(2,1)S(1)}, u32[]{:S(2)}, u32[]{:S(2)}) collective-permute-start(bf16[2,384,256]{2,1,0:T(8,128)(2,1)S(1)} %collective-permute-done.1.f1), channel_id=1, source_target_pairs={{0,16},{16,32},{32,48},{48,64},{64,80},{80,96},{96,112},{112,0},{1... | collective-permute-start | bytes 1179656 | tf_op jit(solution)/shard_map/ppermute | solution.py:170
  95.8 21.7 %collective-permute-start.7 = (bf16[2,384,256]{2,1,0:T(8,128)(2,1)S(1)}, bf16[2,384,256]{2,1,0:T(8,128)(2,1)S(1)}, u32[]{:S(2)}, u32[]{:S(2)}) collective-permute-start(bf16[2,384,256]{2,1,0:T(8,128)(2,1)S(1)} %collective-permute-done.4.b2), channel_id=1, source_target_pairs={{0,112},{16,0},{32,16},{48,32},{64,48},{80,64},{96,80},{112,96},{1... | collective-permute-start | bytes 1179656 | tf_op jit(solution)/shard_map/ppermute | solution.py:171
  101.1 16.4 %collective-permute-start.6 = (bf16[2,384,256]{2,1,0:T(8,128)(2,1)S(1)}, bf16[2,384,256]{2,1,0:T(8,128)(2,1)S(1)}, u32[]{:S(2)}, u32[]{:S(2)}) collective-permute-start(bf16[2,384,256]{2,1,0:T(8,128)(2,1)S(1)} %collective-permute-done.3.f2), channel_id=1, source_target_pairs={{0,16},{16,32},{32,48},{48,64},{64,80},{80,96},{96,112},{112,0},{1... | collective-permute-start | bytes 1179656 | tf_op jit(solution)/shard_map/ppermute | solution.py:170
  117.6 9.2 %collective-permute-start.9 = (bf16[2,192,256]{2,1,0:T(8,128)(2,1)S(1)}, bf16[2,192,256]{2,1,0:T(8,128)(2,1)S(1)}, u32[]{:S(2)}, u32[]{:S(2)}) collective-permute-start(bf16[2,192,256]{2,1,0:T(8,128)(2,1)S(1)} %slice.23), channel_id=1, source_target_pairs={{0,112},{16,0},{32,16},{48,32},{64,48},{80,64},{96,80},{112,96},{1... | collective-permute-start | bytes 589832 | tf_op jit(solution)/shard_map/ppermute | solution.py:177
  121.6 7.6 %collective-permute-start.8 = (bf16[2,192,256]{2,1,0:T(8,128)(2,1)S(1)}, bf16[2,192,256]{2,1,0:T(8,128)(2,1)S(1)}, u32[]{:S(2)}, u32[]{:S(2)}) collective-permute-start(bf16[2,192,256]{2,1,0:T(8,128)(2,1)S(1)} %slice.22), channel_id=1, source_target_pairs={{0,16},{16,32},{32,48},{48,64},{64,80},{80,96},{96,112},{112,0},{1... | collective-permute-start | bytes 589832 | tf_op jit(solution)/shard_map/ppermute | solution.py:176

commit v5 on v1

v5 whole, which is shorter than its diff:
```python
import jax
import jax.numpy as jnp
from jax import lax
from jax.experimental import pallas as pl
from jax.experimental.pallas import tpu as pltpu
from jax.sharding import Mesh, PartitionSpec as P

BS = 256
MB = 4
NZA = 3
KB = 4
NZB = 2
NB = 4
Y_LO = 4
Z = 8
COL = ("y_hi", "x", "core")
ROW = ("y_lo", "z")
PIECES = Y_LO * Z
PIECE = MB * NZA * BS // PIECES
SPAN = Y_LO * PIECE
META = 8


def z_route(distance):
    return [(i, (i + distance) % Z) for i in range(Z)]


def col_route(n):
    return [((i + 1) % n, i) for i in range(n)]


EACH = MB * NZA + MB


def strips(parts):
    found = []
    at = 0
    for ref in parts:
        rows = ref.shape[1]
        off = 0
        while off < rows:
            slot = at // BS
            take = min(rows - off, (slot + 1) * BS - at)
            found.append((slot, at - slot * BS, ref, off, take))
            off += take
            at += take
    return found


def add_products(scalars, i, k, parts, b_ref, acc):
    table, pairs = scalars[1], scalars[2 + k]
    live = table[k * EACH + MB * NZA + i]
    for s in range(NZA):

        @pl.when(s < live)
        def _():
            q = table[k * EACH + i * NZA + s]
            b = b_ref[q]
            for slot, row, ref, off, take in strips(parts):
                if slot == s:
                    product = jnp.dot(ref[k, off : off + take, :], b, preferred_element_type=jnp.float32)
                    for t in range(NZB):
                        j = pairs[q * NZB + t]
                        acc[j, row : row + take] += product[:, t * BS : (t + 1) * BS]


def on_parity(scalars, even, odd, sections, b_refs, acc):
    z = scalars[0][0]
    for bit, (away, parts) in enumerate((even, odd)):

        @pl.when(z % 2 == bit)
        def _():
            i = ((z + away + Z) % Z) // 2
            for k in sections:
                add_products(scalars, i, k, parts, b_refs[k], acc)

    return ((z + even[0] + (z % 2) * (odd[0] - even[0]) + Z) % Z) // 2


def write_row(o_s, acc, out, i, sem):
    for j in range(NB):
        o_s[:, j * BS : (j + 1) * BS] = acc[j].astype(jnp.bfloat16)
    copy = pltpu.make_async_copy(o_s, out.at[i], sem)
    copy.start()
    return copy


def first_section(*refs):
    scalars, (own, f1, b1, f2, b2, b_here, part, acc, sem) = refs[:4], refs[4:]
    acc[...] = jnp.zeros_like(acc)
    rows = (((0, (own, b1)), (-1, (f1, own))), ((-2, (f2, f1)), (1, (b1, b2))))
    copies = []
    for n, (even, odd) in enumerate(rows):
        on_parity(scalars, even, odd, (0,), (b_here,), acc.at[n])
        copies.append(pltpu.make_async_copy(acc.at[n], part.at[n], sem.at[n]))
        copies[-1].start()
    for c in copies:
        c.wait()


def three_rows(*refs):
    scalars = refs[:4]
    own, f1, b1, f2, b2, f3, b3, b_here, b_next, part, out, acc, o_s, sem = refs[4:]
    b_refs = (b_here, b_next)
    loads = [pltpu.make_async_copy(part.at[n], acc.at[n], sem.at[n]) for n in range(2)]
    for c in loads:
        c.start()
    acc[2] = jnp.zeros_like(acc[2])
    i = on_parity(scalars, (2, (b2, b3)), (-3, (f3, f2)), (0, 1), b_refs, acc.at[2])
    writes = [write_row(o_s.at[2], acc.at[2], out, i, sem.at[2])]
    rows = (((0, (own, b1)), (-1, (f1, own))), ((-2, (f2, f1)), (1, (b1, b2))))
    for n, (even, odd) in enumerate(rows):
        loads[n].wait()
        i = on_parity(scalars, even, odd, (1,), b_refs, acc.at[n])
        writes.append(write_row(o_s.at[n], acc.at[n], out, i, sem.at[3 + n]))
    for c in writes:
        c.wait()


def last_row(*refs):
    scalars = refs[:4]
    f3, b3, f4, b4, b_here, b_next, before, out, acc, o_s, sem = refs[4:]
    acc[...] = jnp.zeros_like(acc)
    i = on_parity(scalars, (4, (f4, b4, f3)), (3, (b3, f4, b4)), (0, 1), (b_here, b_next), acc)
    write_row(o_s, acc, out, i, sem.at[0]).wait()


def call(kernel, scalars, held, left, out_shape, scratch, products, alias=False):
    hbm = pl.BlockSpec(memory_space=pl.ANY)
    vmem = pl.BlockSpec(memory_space=pltpu.VMEM)
    return pl.pallas_call(
        kernel,
        out_shape=out_shape,
        grid_spec=pltpu.PrefetchScalarGridSpec(
            num_scalar_prefetch=len(scalars),
            grid=(),
            in_specs=[vmem] * len(held) + [hbm] * len(left),
            out_specs=hbm,
            scratch_shapes=scratch,
        ),
        input_output_aliases={len(scalars) + len(held): 0} if alias else {},
        cost_estimate=pl.CostEstimate(flops=products * 4 * BS**3, bytes_accessed=1 << 20, transcendentals=0),
        compiler_params=pltpu.CompilerParams(vmem_limit_bytes=12 * 1024 * 1024),
    )(*scalars, *held, *left)


def payload_rows(a_columns, a_live, tile, out, wide, rows, sem):
    copy = pltpu.make_async_copy(tile, out.at[:, :PIECE], sem.at[0])
    copy.start()
    wide[...] = jnp.zeros_like(wide)
    for i in range(MB):
        wide[:1, i * NZA : (i + 1) * NZA] = a_columns[i : i + 1].astype(jnp.float32)
    wide[:1, MB * NZA : EACH] = a_live[...].astype(jnp.float32)
    rows[...] = jnp.broadcast_to(wide[...].astype(jnp.bfloat16)[None], rows.shape)
    below = pltpu.make_async_copy(rows, out.at[:, PIECE:], sem.at[1])
    below.start()
    copy.wait()
    below.wait()


def payload(a_columns, a_live, tile):
    vmem = pl.BlockSpec(memory_space=pltpu.VMEM)
    return pl.pallas_call(
        payload_rows,
        out_shape=jax.ShapeDtypeStruct((PIECES, PIECE + META, BS), jnp.bfloat16),
        in_specs=[vmem, vmem, pl.BlockSpec(memory_space=pltpu.HBM)],
        out_specs=pl.BlockSpec(memory_space=pl.ANY),
        scratch_shapes=[
            pltpu.VMEM((META, BS), jnp.float32),
            pltpu.VMEM((PIECES, META, BS), jnp.bfloat16),
            pltpu.SemaphoreType.DMA((2,)),
        ],
        compiler_params=pltpu.CompilerParams(vmem_limit_bytes=4 * 1024 * 1024),
    )(a_columns, a_live, pltpu.with_memory_space_constraint(tile, pltpu.HBM))


def on_device(a_blocks, a_columns, a_live, owner_map, b_blocks, b_columns):
    tile = a_blocks.reshape(PIECES, PIECE, BS)
    cols = lax.axis_size(COL)
    got = lax.all_to_all(payload(a_columns[0, 0], a_live[0], tile), ("z", "y_lo"), 0, 0, tiled=True)
    holder = owner_map[0]
    source = (holder % Z) * Y_LO + holder // Z
    bc_here = b_columns[0, 0]
    bc_next = lax.ppermute(bc_here, COL, col_route(cols)).reshape(-1)
    bc_here = bc_here.reshape(-1)
    place = lax.axis_index("z").astype(jnp.int32)[None]
    got, bc_here, bc_next, place = lax.optimization_barrier((got, bc_here, bc_next, place))

    two = jnp.stack([lax.dynamic_index_in_dim(got, source[k], 0, keepdims=False) for k in range(2)])
    table = two[:, PIECE, :EACH].astype(jnp.int32).reshape(-1)
    own = lax.all_gather(two[:, :PIECE], "y_lo", axis=1, tiled=True)
    b_here = b_blocks[0, 0]
    b_ready, own, table = lax.optimization_barrier((b_here, own, table))
    b_next = lax.ppermute(b_ready, COL, col_route(cols))
    ahead = [own]
    back = [own]
    for step in range(3):
        ahead.append(lax.ppermute(ahead[-1], "z", z_route(1)))
        back.append(lax.ppermute(back[-1], "z", z_route(-1)))
    scalars = (place, table, bc_here, bc_next)
    near = (own, ahead[1], back[1], ahead[2], back[2])
    block = (NB, BS, BS)
    shape = jax.ShapeDtypeStruct((MB, BS, NB * BS), jnp.bfloat16)
    part = call(
        first_section,
        scalars,
        near + (b_here,),
        (),
        jax.ShapeDtypeStruct((2,) + block, jnp.float32),
        [pltpu.VMEM((2,) + block, jnp.float32), pltpu.SemaphoreType.DMA((2,))],
        6,
    )
    part, ahead[3], back[3] = lax.optimization_barrier((part, ahead[3], back[3]))
    f4 = lax.ppermute(ahead[3][:, : SPAN // 2], "z", z_route(1))
    b4 = lax.ppermute(back[3][:, SPAN // 2 :], "z", z_route(-1))
    window = call(
        three_rows,
        scalars,
        near + (ahead[3], back[3], b_here, b_next),
        (part,),
        shape,
        [
            pltpu.VMEM((3,) + block, jnp.float32),
            pltpu.VMEM((3, BS, NB * BS), jnp.bfloat16),
            pltpu.SemaphoreType.DMA((5,)),
        ],
        12,
    )
    window = call(
        last_row,
        scalars,
        (ahead[3], back[3], f4, b4, b_here, b_next),
        (window,),
        shape,
        [pltpu.VMEM(block, jnp.float32), pltpu.VMEM((BS, NB * BS), jnp.bfloat16), pltpu.SemaphoreType.DMA((1,))],
        6,
        alias=True,
    )
    return window[None, None]


def solution(mesh):
    fine = Mesh(mesh.devices.reshape(Y_LO, Z, 2, 4, 2), ROW + COL)
    row, col = ROW, COL
    return jax.shard_map(
        on_device,
        mesh=fine,
        in_specs=(
            P(row, col, None, None, None, None),
            P(row, col, None, None),
            P(row, col, None),
            P(col, None),
            P(row, col, None, None, None),
            P(row, col, None, None),
        ),
        out_specs=P(row, col, None, None, None),
        check_vma=False,
    )
```

time: 142 us -> 175 us (1.23)
  the two profiles are of different devices: /device:TPU:7 before, /device:TPU:6 now
where the time goes in v5:
time: 175 us; the launch traced here: 174 us
  Pallas kernels  58.4 us (33%)
  waiting for transfers between devices  51.4 us (29%)
  starting transfers between devices  43.3 us (25%)
  blocking collectives  15 us (9%)
  between operations  3.8 us (2%)
  local copies, waits for them, and re-layouts  2.52 us (1%)
    pallas_call x1, Pallas kernels, payload(): pl.pallas_call(payload_rows, out_shape=jax.ShapeDtypeStruct((PIECES, PIEC...  48.8 us
    all_to_all x1, waiting for transfers between devices, on_device(): lax.all_to_all(payload(a_columns[0, 0], a_live[0], tile), ('z', 'y_lo'),...  36.5 us
    all_gather x1, blocking collectives, on_device(): own = lax.all_gather(two[:, :PIECE], 'y_lo', axis=1, tiled=True)  15 us
    all_to_all x1, starting transfers between devices, on_device(): lax.all_to_all(payload(a_columns[0, 0], a_live[0], tile), ('z', 'y_lo'),...  13.9 us
    ppermute x3, starting transfers between devices, on_device(): back.append(lax.ppermute(back[-1], 'z', z_route(-1)))  13.3 us
    pallas_call x3, Pallas kernels, call(): pl.pallas_call(kernel, out_shape=out_shape, grid_spec=pltpu.PrefetchScala...  9.62 us
    ppermute x3, waiting for transfers between devices, on_device(): back.append(lax.ppermute(back[-1], 'z', z_route(-1)))  8.92 us
    ppermute x3, starting transfers between devices, on_device(): ahead.append(lax.ppermute(ahead[-1], 'z', z_route(1)))  6.44 us
  transfers between devices with their start and end apart: 11, of which 6 were waited for; matrix products, arithmetic and copies ran while one was open for 1% of the time, Pallas kernels for 4%

profile of v5, /device:TPU:6, one launch (start us, length us, event | category | flops | bytes accessed | tf_op | source)
XLA Modules:
  0.0 174.4 jit_solution(5843859796078469297)
XLA Ops:
  0.0 0.8 copy.11
  0.8 0.0 copy-start.1
  0.8 0.7 copy-done.1
  1.4 48.8 %shard_map.64 = bf16[32,104,256]{2,1,0:T(8,128)(2,1)} custom-call(s32[4,3]{1,0:T(4,128)S(1)} %bitcast.26, s32[1,4]{1,0:T(1,128)S(1)} %bitcast.27, bf16[32,96,256]{2,1,0:T(8,128)(2,1)} %bitcast.28), custom_call_target="tpu_custom_call" | custom-call | tf_op jit(solution)/shard_map/pallas_call | solution.py:163
  50.2 0.0 copy-start.2
  50.2 0.0 copy-start.3
  50.2 0.0 copy-start
  50.2 13.9 %all-to-all-start = ((bf16[32,104,256]{2,1,0:T(8,128)(2,1)}), bf16[32,104,256]{2,1,0:T(8,128)(2,1)S(1)}, u32[]{:S(2)}, u32[]{:S(2)}) async-start(bf16[32,104,256]{2,1,0:T(8,128)(2,1)} %shard_map.64), calls=%async_computation | async-start | bytes 3407872 | tf_op jit(solution)/shard_map/all_to_all | solution.py:180
  64.1 0.0 copy-done.2
  64.1 1.9 %collective-permute-start = (s32[4,2]{0,1:T(2,128)S(1)}, s32[4,2]{0,1:T(2,128)S(1)}, u32[]{:S(2)}, u32[]{:S(2)}) collective-permute-start(s32[4,2]{0,1:T(2,128)S(1)} %bitcast.29), channel_id=1, source_target_pairs={{1,0},{2,1},{3,2},{4,3},{5,4},{6,5},{7,6},{8,7},{9,8},{10,9},{11,1... | collective-permute-start | bytes 104 | tf_op jit(solution)/shard_map/ppermute | solution.py:184
  66.1 0.0 copy-done.3
  66.1 0.6 fusion.5
  69.1 0.1 copy.12
  69.2 0.1 reshape_squeeze.3.refs_2_
  70.4 0.0 collective-permute-done
  70.5 0.1 copy.13
  70.5 0.1 reshape.11.refs_3_
  70.6 36.5 %all-to-all-done = bf16[32,104,256]{2,1,0:T(8,128)(2,1)S(1)} async-done(((bf16[32,104,256]{2,1,0:T(8,128)(2,1)}), bf16[32,104,256]{2,1,0:T(8,128)(2,1)S(1)}, u32[]{:S(2)}, u32[]{:S(2)}) %all-to-all-start) | async-done | bytes 1703968 | tf_op jit(solution)/shard_map/all_to_all | solution.py:180
  107.2 0.1 reshape.12.refs_1_
  107.3 15.0 %all_gather.3.refs_4_ = bf16[2,384,256]{2,1,0:T(8,128)(2,1)S(1)} all-gather(bf16[2,96,256]{2,1,0:T(8,128)(2,1)S(1)} %fusion), channel_id=1, replica_groups=mesh['y_lo'=4,'z'=8,'y_hi'=2,'x'=4,'core'=2] {'y_lo'}, dimensions={1}, use_global_device_ids=true | all-gather | bytes 491520 | tf_op jit(solution)/shard_map/all_gather | solution.py:191
  122.2 3.2 %collective-permute-start.2 = (bf16[2,384,256]{2,1,0:T(8,128)(2,1)S(1)}, bf16[2,384,256]{2,1,0:T(8,128)(2,1)S(1)}, u32[]{:S(2)}, u32[]{:S(2)}) collective-permute-start(bf16[2,384,256]{2,1,0:T(8,128)(2,1)S(1)} %all_gather.3.refs_4_), channel_id=1, source_target_pairs={{0,112},{16,0},{32,16},{48,32},{64,48},{80,64},{96,80},{112,96},{1... | collective-permute-start | bytes 1179656 | tf_op jit(solution)/shard_map/ppermute | solution.py:199
  125.5 2.6 %collective-permute-start.1 = (bf16[2,384,256]{2,1,0:T(8,128)(2,1)S(1)}, bf16[2,384,256]{2,1,0:T(8,128)(2,1)S(1)}, u32[]{:S(2)}, u32[]{:S(2)}) collective-permute-start(bf16[2,384,256]{2,1,0:T(8,128)(2,1)S(1)} %all_gather.3.refs_4_), channel_id=1, source_target_pairs={{0,16},{16,32},{32,48},{48,64},{64,80},{80,96},{96,112},{112,0},{1... | collective-permute-start | bytes 1179656 | tf_op jit(solution)/shard_map/ppermute | solution.py:198
  128.1 0.0 copy-done
  128.1 1.9 %collective-permute-start.9 = (bf16[4,256,512]{2,1,0:T(8,128)(2,1)S(1)}, bf16[4,256,512]{2,1,0:T(8,128)(2,1)S(1)}, u32[]{:S(2)}, u32[]{:S(2)}) collective-permute-start(bf16[4,256,512]{2,1,0:T(8,128)(2,1)S(1)} %bitcast.22), channel_id=1, source_target_pairs={{1,0},{2,1},{3,2},{4,3},{5,4},{6,5},{7,6},{8,7},{9,8},{10,9},{11,1... | collective-permute-start | bytes 3145736 | tf_op jit(solution)/shard_map/ppermute | solution.py:194
  130.0 1.9 %collective-permute-done.2.refs_6_ = bf16[2,384,256]{2,1,0:T(8,128)(2,1)S(1)} collective-permute-done((bf16[2,384,256]{2,1,0:T(8,128)(2,1)S(1)}, bf16[2,384,256]{2,1,0:T(8,128)(2,1)S(1)}, u32[]{:S(2)}, u32[]{:S(2)}) %collective-permute-start.2) | collective-permute-done | bytes 393248 | tf_op jit(solution)/shard_map/ppermute | solution.py:199
  131.9 4.5 %collective-permute-start.4 = (bf16[2,384,256]{2,1,0:T(8,128)(2,1)S(1)}, bf16[2,384,256]{2,1,0:T(8,128)(2,1)S(1)}, u32[]{:S(2)}, u32[]{:S(2)}) collective-permute-start(bf16[2,384,256]{2,1,0:T(8,128)(2,1)S(1)} %collective-permute-done.2.refs_6_), channel_id=1, source_target_pairs={{0,112},{16,0},{32,16},{48,32},{64,48},{80,64},{96,80},{112,96},{1... | collective-permute-start | bytes 1179656 | tf_op jit(solution)/shard_map/ppermute | solution.py:199
  136.4 0.0 collective-permute-done.1.refs_5_
  136.4 1.9 %collective-permute-start.3 = (bf16[2,384,256]{2,1,0:T(8,128)(2,1)S(1)}, bf16[2,384,256]{2,1,0:T(8,128)(2,1)S(1)}, u32[]{:S(2)}, u32[]{:S(2)}) collective-permute-start(bf16[2,384,256]{2,1,0:T(8,128)(2,1)S(1)} %collective-permute-done.1.refs_5_), channel_id=1, source_target_pairs={{0,16},{16,32},{32,48},{48,64},{64,80},{80,96},{96,112},{112,0},{1... | collective-permute-start | bytes 1179656 | tf_op jit(solution)/shard_map/ppermute | solution.py:198
  138.3 5.2 %collective-permute-done.4.refs_8_ = bf16[2,384,256]{2,1,0:T(8,128)(2,1)S(1)} collective-permute-done((bf16[2,384,256]{2,1,0:T(8,128)(2,1)S(1)}, bf16[2,384,256]{2,1,0:T(8,128)(2,1)S(1)}, u32[]{:S(2)}, u32[]{:S(2)}) %collective-permute-start.4) | collective-permute-done | bytes 393248 | tf_op jit(solution)/shard_map/ppermute | solution.py:199
  143.5 5.6 %collective-permute-start.6 = (bf16[2,384,256]{2,1,0:T(8,128)(2,1)S(1)}, bf16[2,384,256]{2,1,0:T(8,128)(2,1)S(1)}, u32[]{:S(2)}, u32[]{:S(2)}) collective-permute-start(bf16[2,384,256]{2,1,0:T(8,128)(2,1)S(1)} %collective-permute-done.4.refs_8_), channel_id=1, source_target_pairs={{0,112},{16,0},{32,16},{48,32},{64,48},{80,64},{96,80},{112,96},{1... | collective-permute-start | bytes 1179656 | tf_op jit(solution)/shard_map/ppermute | solution.py:199
  149.1 0.0 collective-permute-done.3.refs_7_
  149.1 1.9 %collective-permute-start.5 = (bf16[2,384,256]{2,1,0:T(8,128)(2,1)S(1)}, bf16[2,384,256]{2,1,0:T(8,128)(2,1)S(1)}, u32[]{:S(2)}, u32[]{:S(2)}) collective-permute-start(bf16[2,384,256]{2,1,0:T(8,128)(2,1)S(1)} %collective-permute-done.3.refs_7_), channel_id=1, source_target_pairs={{0,16},{16,32},{32,48},{48,64},{64,80},{80,96},{96,112},{112,0},{1... | collective-permute-start | bytes 1179656 | tf_op jit(solution)/shard_map/ppermute | solution.py:198
  151.0 2.4 %shard_map.65.refs_13_ = f32[2,4,256,256]{3,2,1,0:T(8,128)S(1)} custom-call(s32[1]{0:T(128)} %bitcast.4.refs_0_, s32[32]{0:T(128)S(1)} %reshape.12.refs_1_, s32[8]{0:T(128)S(1)} %reshape_squeeze.3.refs_2_, s32[8]{0:T(128)S(1)} %reshape.11.refs_3_, bf16[2,384,256]{2,1,0:T(8,128)(2,1)S(1)} %all_gather.3.refs_4_, ...), custom_call_target="tpu_custom_call" | custom-call | flops 402653184 | bytes 1048576 | tf_op jit(solution)/shard_map/pallas_call | solution.py:131
  153.5 1.9 %collective-permute-done.6.refs_10_.refs_5_ = bf16[2,384,256]{2,1,0:T(8,128)(2,1)S(1)} collective-permute-done((bf16[2,384,256]{2,1,0:T(8,128)(2,1)S(1)}, bf16[2,384,256]{2,1,0:T(8,128)(2,1)S(1)}, u32[]{:S(2)}, u32[]{:S(2)}) %collective-permute-start.6) | collective-permute-done | bytes 393248 | tf_op jit(solution)/shard_map/ppermute | solution.py:199
  155.3 5.3 %collective-permute-done.5.refs_9_.refs_4_ = bf16[2,384,256]{2,1,0:T(8,128)(2,1)S(1)} collective-permute-done((bf16[2,384,256]{2,1,0:T(8,128)(2,1)S(1)}, bf16[2,384,256]{2,1,0:T(8,128)(2,1)S(1)}, u32[]{:S(2)}, u32[]{:S(2)}) %collective-permute-start.5) | collective-permute-done | bytes 393248 | tf_op jit(solution)/shard_map/ppermute | solution.py:198
  160.7 1.9 %collective-permute-start.8 = (bf16[2,192,256]{2,1,0:T(8,128)(2,1)S(1)}, bf16[2,192,256]{2,1,0:T(8,128)(2,1)S(1)}, u32[]{:S(2)}, u32[]{:S(2)}) collective-permute-start(bf16[2,192,256]{2,1,0:T(8,128)(2,1)S(1)} %slice.23), channel_id=1, source_target_pairs={{0,112},{16,0},{32,16},{48,32},{64,48},{80,64},{96,80},{112,96},{1... | collective-permute-start | bytes 589832 | tf_op jit(solution)/shard_map/ppermute | solution.py:215
  162.6 3.9 %collective-permute-start.7 = (bf16[2,192,256]{2,1,0:T(8,128)(2,1)S(1)}, bf16[2,192,256]{2,1,0:T(8,128)(2,1)S(1)}, u32[]{:S(2)}, u32[]{:S(2)}) collective-permute-start(bf16[2,192,256]{2,1,0:T(8,128)(2,1)S(1)} %slice.22), channel_id=1, source_target_pairs={{0,16},{16,32},{32,48},{48,64},{64,80},{80,96},{96,112},{112,0},{1... | collective-permute-start | bytes 589832 | tf_op jit(solution)/shard_map/ppermute | solution.py:214
  166.5 0.0 collective-permute-done.9.refs_12_.refs_9_
  166.6 4.2 %shard_map.66.refs_10_ = bf16[4,256,1024]{2,1,0:T(8,128)(2,1)} custom-call(s32[1]{0:T(128)} %bitcast.4.refs_0_, s32[32]{0:T(128)S(1)} %reshape.12.refs_1_, s32[8]{0:T(128)S(1)} %reshape_squeeze.3.refs_2_, s32[8]{0:T(128)S(1)} %reshape.11.refs_3_, bf16[2,384,256]{2,1,0:T(8,128)(2,1)S(1)} %all_gather.3.refs_4_, ...), custom_call_target="tpu_custom_call" | custom-call | flops 805306368 | bytes 1048576 | tf_op jit(solution)/shard_map/pallas_call | solution.py:131
  170.7 0.0 collective-permute-done.8.refs_7_
  170.8 0.6 collective-permute-done.7.refs_6_
  171.4 3.0 %shard_map.67 = bf16[4,256,1024]{2,1,0:T(8,128)(2,1)} custom-call(s32[1]{0:T(128)} %bitcast.4.refs_0_, s32[32]{0:T(128)S(1)} %reshape.12.refs_1_, s32[8]{0:T(128)S(1)} %reshape_squeeze.3.refs_2_, s32[8]{0:T(128)S(1)} %reshape.11.refs_3_, bf16[2,384,256]{2,1,0:T(8,128)(2,1)S(1)} %collective-permute-done.5.refs_9_.refs_4_, ...), custom_call_target="tpu_custom_call", output_to_operand_aliasing={{}: (10, {})} | custom-call | flops 402653184 | bytes 1048576 | tf_op jit(solution)/shard_map/pallas_call | solution.py:131
  (6 shorter events, 0.1 us)
Async XLA Ops:
  0.8 0.7 copy-start.1
  50.2 13.9 %copy-start.2 = (s32[1,1,4,2]{2,3,1,0:T(2,128)S(1)}, s32[1,1,4,2]{2,3,1,0:T(2,128)}, u32[]{:S(2)}) copy-start(s32[1,1,4,2]{2,3,1,0:T(2,128)} %param.11) | copy-start | bytes 100
  50.2 15.9 %copy-start.3 = (s32[1,2]{1,0:T(1,128)S(1)}, s32[1,2]{1,0:T(1,128)}, u32[]{:S(2)}) copy-start(s32[1,2]{1,0:T(1,128)} %param.9) | copy-start | bytes 28
  50.2 77.9 %copy-start = (bf16[1,1,4,256,512]{4,3,2,1,0:T(8,128)(2,1)S(1)}, bf16[1,1,4,256,512]{4,3,2,1,0:T(8,128)(2,1)}, u32[]{:S(2)}) copy-start(bf16[1,1,4,256,512]{4,3,2,1,0:T(8,128)(2,1)} %param.10) | copy-start | bytes 3145732
  50.2 56.9 %all-to-all-start = ((bf16[32,104,256]{2,1,0:T(8,128)(2,1)}), bf16[32,104,256]{2,1,0:T(8,128)(2,1)S(1)}, u32[]{:S(2)}, u32[]{:S(2)}) async-start(bf16[32,104,256]{2,1,0:T(8,128)(2,1)} %shard_map.64), calls=%async_computation | async-start | bytes 3407872 | tf_op jit(solution)/shard_map/all_to_all | solution.py:180
  64.1 6.3 %collective-permute-start = (s32[4,2]{0,1:T(2,128)S(1)}, s32[4,2]{0,1:T(2,128)S(1)}, u32[]{:S(2)}, u32[]{:S(2)}) collective-permute-start(s32[4,2]{0,1:T(2,128)S(1)} %bitcast.29), channel_id=1, source_target_pairs={{1,0},{2,1},{3,2},{4,3},{5,4},{6,5},{7,6},{8,7},{9,8},{10,9},{11,1... | collective-permute-start | bytes 104 | tf_op jit(solution)/shard_map/ppermute | solution.py:184
  122.2 9.7 %collective-permute-start.2 = (bf16[2,384,256]{2,1,0:T(8,128)(2,1)S(1)}, bf16[2,384,256]{2,1,0:T(8,128)(2,1)S(1)}, u32[]{:S(2)}, u32[]{:S(2)}) collective-permute-start(bf16[2,384,256]{2,1,0:T(8,128)(2,1)S(1)} %all_gather.3.refs_4_), channel_id=1, source_target_pairs={{0,112},{16,0},{32,16},{48,32},{64,48},{80,64},{96,80},{112,96},{1... | collective-permute-start | bytes 1179656 | tf_op jit(solution)/shard_map/ppermute | solution.py:199
  125.5 10.9 %collective-permute-start.1 = (bf16[2,384,256]{2,1,0:T(8,128)(2,1)S(1)}, bf16[2,384,256]{2,1,0:T(8,128)(2,1)S(1)}, u32[]{:S(2)}, u32[]{:S(2)}) collective-permute-start(bf16[2,384,256]{2,1,0:T(8,128)(2,1)S(1)} %all_gather.3.refs_4_), channel_id=1, source_target_pairs={{0,16},{16,32},{32,48},{48,64},{64,80},{80,96},{96,112},{112,0},{1... | collective-permute-start | bytes 1179656 | tf_op jit(solution)/shard_map/ppermute | solution.py:198
  128.1 38.5 %collective-permute-start.9 = (bf16[4,256,512]{2,1,0:T(8,128)(2,1)S(1)}, bf16[4,256,512]{2,1,0:T(8,128)(2,1)S(1)}, u32[]{:S(2)}, u32[]{:S(2)}) collective-permute-start(bf16[4,256,512]{2,1,0:T(8,128)(2,1)S(1)} %bitcast.22), channel_id=1, source_target_pairs={{1,0},{2,1},{3,2},{4,3},{5,4},{6,5},{7,6},{8,7},{9,8},{10,9},{11,1... | collective-permute-start | bytes 3145736 | tf_op jit(solution)/shard_map/ppermute | solution.py:194
  131.9 11.6 %collective-permute-start.4 = (bf16[2,384,256]{2,1,0:T(8,128)(2,1)S(1)}, bf16[2,384,256]{2,1,0:T(8,128)(2,1)S(1)}, u32[]{:S(2)}, u32[]{:S(2)}) collective-permute-start(bf16[2,384,256]{2,1,0:T(8,128)(2,1)S(1)} %collective-permute-done.2.refs_6_), channel_id=1, source_target_pairs={{0,112},{16,0},{32,16},{48,32},{64,48},{80,64},{96,80},{112,96},{1... | collective-permute-start | bytes 1179656 | tf_op jit(solution)/shard_map/ppermute | solution.py:199
  136.4 12.7 %collective-permute-start.3 = (bf16[2,384,256]{2,1,0:T(8,128)(2,1)S(1)}, bf16[2,384,256]{2,1,0:T(8,128)(2,1)S(1)}, u32[]{:S(2)}, u32[]{:S(2)}) collective-permute-start(bf16[2,384,256]{2,1,0:T(8,128)(2,1)S(1)} %collective-permute-done.1.refs_5_), channel_id=1, source_target_pairs={{0,16},{16,32},{32,48},{48,64},{64,80},{80,96},{96,112},{112,0},{1... | collective-permute-start | bytes 1179656 | tf_op jit(solution)/shard_map/ppermute | solution.py:198
  143.5 11.8 %collective-permute-start.6 = (bf16[2,384,256]{2,1,0:T(8,128)(2,1)S(1)}, bf16[2,384,256]{2,1,0:T(8,128)(2,1)S(1)}, u32[]{:S(2)}, u32[]{:S(2)}) collective-permute-start(bf16[2,384,256]{2,1,0:T(8,128)(2,1)S(1)} %collective-permute-done.4.refs_8_), channel_id=1, source_target_pairs={{0,112},{16,0},{32,16},{48,32},{64,48},{80,64},{96,80},{112,96},{1... | collective-permute-start | bytes 1179656 | tf_op jit(solution)/shard_map/ppermute | solution.py:199
  149.1 11.5 %collective-permute-start.5 = (bf16[2,384,256]{2,1,0:T(8,128)(2,1)S(1)}, bf16[2,384,256]{2,1,0:T(8,128)(2,1)S(1)}, u32[]{:S(2)}, u32[]{:S(2)}) collective-permute-start(bf16[2,384,256]{2,1,0:T(8,128)(2,1)S(1)} %collective-permute-done.3.refs_7_), channel_id=1, source_target_pairs={{0,16},{16,32},{32,48},{48,64},{64,80},{80,96},{96,112},{112,0},{1... | collective-permute-start | bytes 1179656 | tf_op jit(solution)/shard_map/ppermute | solution.py:198
  160.7 10.1 %collective-permute-start.8 = (bf16[2,192,256]{2,1,0:T(8,128)(2,1)S(1)}, bf16[2,192,256]{2,1,0:T(8,128)(2,1)S(1)}, u32[]{:S(2)}, u32[]{:S(2)}) collective-permute-start(bf16[2,192,256]{2,1,0:T(8,128)(2,1)S(1)} %slice.23), channel_id=1, source_target_pairs={{0,112},{16,0},{32,16},{48,32},{64,48},{80,64},{96,80},{112,96},{1... | collective-permute-start | bytes 589832 | tf_op jit(solution)/shard_map/ppermute | solution.py:215
  162.6 8.8 %collective-permute-start.7 = (bf16[2,192,256]{2,1,0:T(8,128)(2,1)S(1)}, bf16[2,192,256]{2,1,0:T(8,128)(2,1)S(1)}, u32[]{:S(2)}, u32[]{:S(2)}) collective-permute-start(bf16[2,192,256]{2,1,0:T(8,128)(2,1)S(1)} %slice.22), channel_id=1, source_target_pairs={{0,16},{16,32},{32,48},{48,64},{64,80},{80,96},{96,112},{112,0},{1... | collective-permute-start | bytes 589832 | tf_op jit(solution)/shard_map/ppermute | solution.py:214

commit v6 on v5

--- a/solution.py
+++ b/solution.py
@@ -29,6 +29,14 @@
     return [((i + 1) % n, i) for i in range(n)]
 
 
+def within(n):
+    return [(a, b) for a, b in col_route(n) if (b + 1) % (n // 2)]
+
+
+def across(n):
+    return [(a, b) for a, b in col_route(n) if not (b + 1) % (n // 2)]
+
+
 EACH = MB * NZA + MB
 
 
@@ -54,8 +62,8 @@
 
         @pl.when(s < live)
         def _():
-            q = table[k * EACH + i * NZA + s]
-            b = b_ref[q]
+            q = table[k * EACH + s * MB + i]
+            b = b_ref[q] if k == 0 else b_ref[0][q] + b_ref[1][q]
             for slot, row, ref, off, take in strips(parts):
                 if slot == s:
                     product = jnp.dot(ref[k, off : off + take, :], b, preferred_element_type=jnp.float32)
@@ -100,8 +108,8 @@
 
 def three_rows(*refs):
     scalars = refs[:4]
-    own, f1, b1, f2, b2, f3, b3, b_here, b_next, part, out, acc, o_s, sem = refs[4:]
-    b_refs = (b_here, b_next)
+    own, f1, b1, f2, b2, f3, b3, b_here, b_in, b_over, part, out, acc, o_s, sem = refs[4:]
+    b_refs = (b_here, (b_in, b_over))
     loads = [pltpu.make_async_copy(part.at[n], acc.at[n], sem.at[n]) for n in range(2)]
     for c in loads:
         c.start()
@@ -119,9 +127,9 @@
 
 def last_row(*refs):
     scalars = refs[:4]
-    f3, b3, f4, b4, b_here, b_next, before, out, acc, o_s, sem = refs[4:]
+    f3, b3, f4, b4, b_here, b_in, b_over, before, out, acc, o_s, sem = refs[4:]
     acc[...] = jnp.zeros_like(acc)
-    i = on_parity(scalars, (4, (f4, b4, f3)), (3, (b3, f4, b4)), (0, 1), (b_here, b_next), acc)
+    i = on_parity(scalars, (4, (f4, b4, f3)), (3, (b3, f4, b4)), (0, 1), (b_here, (b_in, b_over)), acc)
     write_row(o_s, acc, out, i, sem.at[0]).wait()
 
 
@@ -144,54 +152,75 @@
     )(*scalars, *held, *left)
 
 
-def payload_rows(a_columns, a_live, tile, out, wide, rows, sem):
-    copy = pltpu.make_async_copy(tile, out.at[:, :PIECE], sem.at[0])
-    copy.start()
+CHUNKS = 4
+
+
+def payload_rows(a_columns, a_live, tile, out, columns, live, wide, rows, sem):
+    step = PIECES // CHUNKS
+    small = [
+        pltpu.make_async_copy(a_columns, columns, sem.at[2 * CHUNKS]),
+        pltpu.make_async_copy(a_live, live, sem.at[2 * CHUNKS + 1]),
+    ]
+    reads = []
+    writes = []
+    for c in range(CHUNKS):
+        part = pl.ds(c * step, step)
+        reads.append(pltpu.make_async_copy(tile.at[part], rows.at[part, :PIECE], sem.at[c]))
+        writes.append(pltpu.make_async_copy(rows.at[part], out.at[part], sem.at[CHUNKS + c]))
+    for c in small + reads:
+        c.start()
     wide[...] = jnp.zeros_like(wide)
-    for i in range(MB):
-        wide[:1, i * NZA : (i + 1) * NZA] = a_columns[i : i + 1].astype(jnp.float32)
-    wide[:1, MB * NZA : EACH] = a_live[...].astype(jnp.float32)
-    rows[...] = jnp.broadcast_to(wide[...].astype(jnp.bfloat16)[None], rows.shape)
-    below = pltpu.make_async_copy(rows, out.at[:, PIECE:], sem.at[1])
-    below.start()
-    copy.wait()
-    below.wait()
+    for c in small:
+        c.wait()
+    for s in range(NZA):
+        wide[:1, s * MB : (s + 1) * MB] = columns[s].astype(jnp.float32)
+    wide[:1, MB * NZA : EACH] = live[...].astype(jnp.float32)
+    for p in range(PIECES):
+        rows[p, PIECE:, :] = wide[...].astype(jnp.bfloat16)
+    for r, w in zip(reads, writes):
+        r.wait()
+        w.start()
+    for w in writes:
+        w.wait()
 
 
 def payload(a_columns, a_live, tile):
-    vmem = pl.BlockSpec(memory_space=pltpu.VMEM)
+    hbm = pl.BlockSpec(memory_space=pltpu.HBM)
     return pl.pallas_call(
         payload_rows,
         out_shape=jax.ShapeDtypeStruct((PIECES, PIECE + META, BS), jnp.bfloat16),
-        in_specs=[vmem, vmem, pl.BlockSpec(memory_space=pltpu.HBM)],
-        out_specs=pl.BlockSpec(memory_space=pl.ANY),
+        in_specs=[hbm, hbm, hbm],
+        out_specs=hbm,
         scratch_shapes=[
+            pltpu.VMEM((NZA, 1, MB), jnp.int32),
+            pltpu.VMEM((1, MB), jnp.int32),
             pltpu.VMEM((META, BS), jnp.float32),
-            pltpu.VMEM((PIECES, META, BS), jnp.bfloat16),
-            pltpu.SemaphoreType.DMA((2,)),
+            pltpu.VMEM((PIECES, PIECE + META, BS), jnp.bfloat16),
+            pltpu.SemaphoreType.DMA((2 * CHUNKS + 2,)),
         ],
         compiler_params=pltpu.CompilerParams(vmem_limit_bytes=4 * 1024 * 1024),
-    )(a_columns, a_live, pltpu.with_memory_space_constraint(tile, pltpu.HBM))
+    )(*(pltpu.with_memory_space_constraint(x, pltpu.HBM) for x in (a_columns, a_live, tile)))
 
 
 def on_device(a_blocks, a_columns, a_live, owner_map, b_blocks, b_columns):
     tile = a_blocks.reshape(PIECES, PIECE, BS)
     cols = lax.axis_size(COL)
-    got = lax.all_to_all(payload(a_columns[0, 0], a_live[0], tile), ("z", "y_lo"), 0, 0, tiled=True)
+    got = lax.all_to_all(payload(a_columns[0].transpose(2, 0, 1), a_live[0], tile), ("z", "y_lo"), 0, 0, tiled=True)
     holder = owner_map[0]
     source = (holder % Z) * Y_LO + holder // Z
     bc_here = b_columns[0, 0]
     bc_next = lax.ppermute(bc_here, COL, col_route(cols)).reshape(-1)
     bc_here = bc_here.reshape(-1)
     place = lax.axis_index("z").astype(jnp.int32)[None]
-    got, bc_here, bc_next, place = lax.optimization_barrier((got, bc_here, bc_next, place))
+    b_here = b_blocks[0, 0]
+    b_in = lax.ppermute(b_here, COL, within(cols))
+    got, bc_here, bc_next, place, b_in = lax.optimization_barrier((got, bc_here, bc_next, place, b_in))
 
     two = jnp.stack([lax.dynamic_index_in_dim(got, source[k], 0, keepdims=False) for k in range(2)])
     table = two[:, PIECE, :EACH].astype(jnp.int32).reshape(-1)
     own = lax.all_gather(two[:, :PIECE], "y_lo", axis=1, tiled=True)
-    b_here = b_blocks[0, 0]
     b_ready, own, table = lax.optimization_barrier((b_here, own, table))
-    b_next = lax.ppermute(b_ready, COL, col_route(cols))
+    b_over = lax.ppermute(b_ready, COL, across(cols))
     ahead = [own]
     back = [own]
     for step in range(3):
@@ -216,7 +245,7 @@
     window = call(
         three_rows,
         scalars,
-        near + (ahead[3], back[3], b_here, b_next),
+        near + (ahead[3], back[3], b_here, b_in, b_over),
         (part,),
         shape,
         [
@@ -229,7 +258,7 @@
     window = call(
         last_row,
         scalars,
-        (ahead[3], back[3], f4, b4, b_here, b_next),
+        (ahead[3], back[3], f4, b4, b_here, b_in, b_over),
         (window,),
         shape,
         [pltpu.VMEM(block, jnp.float32), pltpu.VMEM((BS, NB * BS), jnp.bfloat16), pltpu.SemaphoreType.DMA((1,))],

time: 175 us -> 126 us (0.72)
  Pallas kernels: 58.4 us -> 11.4 us
    pallas_call x1, Pallas kernels: 48.8 us -> 2.29 us  [payload(): pl.pallas_call(payload_rows, out_shape=jax.ShapeDtypeStruct((PIECES, PIEC...]
    all_to_all x1, waiting for transfers between devices: 36.5 us -> 28.5 us  [on_device(): lax.all_to_all(payload(a_columns[0].transpose(2, 0, 1), a_live[0], tile),...]
    ppermute x1, waiting for transfers between devices: 0.01 us -> 4.89 us  [on_device(): bc_next = lax.ppermute(bc_here, COL, col_route(cols)).reshape(-1)]
    ppermute x3, starting transfers between devices: 13.3 us -> 9.54 us  [on_device(): back.append(lax.ppermute(back[-1], 'z', z_route(-1)))]
    ppermute x3, waiting for transfers between devices: 8.92 us -> 11.6 us  [on_device(): back.append(lax.ppermute(back[-1], 'z', z_route(-1)))]
  transfers between devices with their start and end apart: 11 -> 12, of which waited for: 6 -> 8; matrix products, arithmetic and copies ran while one was open for 1% -> 1% of each run, Pallas kernels for 4% -> 5%
where the time goes in v6:
time: 126 us; the launch traced here: 125 us
  waiting for transfers between devices  50.1 us (40%)
  starting transfers between devices  42.5 us (34%)
  blocking collectives  15 us (12%)
  Pallas kernels  11.4 us (9%)
  between operations  3.93 us (3%)
  local copies, waits for them, and re-layouts  1.97 us (2%)
    all_to_all x1, waiting for transfers between devices, on_device(): lax.all_to_all(payload(a_columns[0].transpose(2, 0, 1), a_live[0], tile),...  28.5 us
    all_gather x1, blocking collectives, on_device(): own = lax.all_gather(two[:, :PIECE], 'y_lo', axis=1, tiled=True)  15 us
    all_to_all x1, starting transfers between devices, on_device(): lax.all_to_all(payload(a_columns[0].transpose(2, 0, 1), a_live[0], tile),...  14 us
    ppermute x3, waiting for transfers between devices, on_device(): back.append(lax.ppermute(back[-1], 'z', z_route(-1)))  11.6 us
    ppermute x3, starting transfers between devices, on_device(): back.append(lax.ppermute(back[-1], 'z', z_route(-1)))  9.54 us
    pallas_call x3, Pallas kernels, call(): pl.pallas_call(kernel, out_shape=out_shape, grid_spec=pltpu.PrefetchScala...  9.14 us
    ppermute x3, starting transfers between devices, on_device(): ahead.append(lax.ppermute(ahead[-1], 'z', z_route(1)))  7.66 us
    ppermute x1, waiting for transfers between devices, on_device(): bc_next = lax.ppermute(bc_here, COL, col_route(cols)).reshape(-1)  4.89 us
  transfers between devices with their start and end apart: 12, of which 8 were waited for; matrix products, arithmetic and copies ran while one was open for 1% of the time, Pallas kernels for 5%

profile of v6, /device:TPU:6, one launch (start us, length us, event | category | flops | bytes accessed | tf_op | source)
XLA Modules:
  0.0 125.0 jit_solution(8969551933618901083)
XLA Ops:
  0.0 2.3 %shard_map.64 = bf16[32,104,256]{2,1,0:T(8,128)(2,1)} custom-call(s32[3,1,4]{2,1,0:T(1,128)} %bitcast.30, s32[1,4]{1,0:T(1,128)} %bitcast.32, bf16[32,96,256]{2,1,0:T(8,128)(2,1)} %bitcast.29), custom_call_target="tpu_custom_call" | custom-call | tf_op jit(solution)/shard_map/pallas_call | solution.py:189
  2.3 0.0 copy-start
  2.3 0.0 copy-start.1
  2.3 0.0 copy-start.2
  2.3 14.0 %all-to-all-start = ((bf16[32,104,256]{2,1,0:T(8,128)(2,1)}), bf16[32,104,256]{2,1,0:T(8,128)(2,1)}, u32[]{:S(2)}, u32[]{:S(2)}) async-start(bf16[32,104,256]{2,1,0:T(8,128)(2,1)} %shard_map.64), calls=%async_computation | async-start | bytes 3407872 | tf_op jit(solution)/shard_map/all_to_all | solution.py:208
  16.3 0.0 copy-done
  16.4 1.9 %collective-permute-start.1 = (bf16[4,256,512]{2,1,0:T(8,128)(2,1)S(1)}, bf16[4,256,512]{2,1,0:T(8,128)(2,1)S(1)}, u32[]{:S(2)}, u32[]{:S(2)}) collective-permute-start(bf16[4,256,512]{2,1,0:T(8,128)(2,1)S(1)} %bitcast.24), channel_id=1, source_target_pairs={{1,0},{2,1},{3,2},{4,3},{5,4},{6,5},{7,6},{9,8},{10,9},{11,10},{12... | collective-permute-start | bytes 3145736 | tf_op jit(solution)/shard_map/ppermute | solution.py:216
  18.3 0.0 copy-done.1
  18.3 2.8 %collective-permute-start = (s32[4,2]{0,1:T(2,128)S(1)}, s32[4,2]{0,1:T(2,128)S(1)}, u32[]{:S(2)}, u32[]{:S(2)}) collective-permute-start(s32[4,2]{0,1:T(2,128)S(1)} %bitcast.31), channel_id=1, source_target_pairs={{1,0},{2,1},{3,2},{4,3},{5,4},{6,5},{7,6},{8,7},{9,8},{10,9},{11,1... | collective-permute-start | bytes 104 | tf_op jit(solution)/shard_map/ppermute | solution.py:212
  21.1 0.0 copy-done.2
  21.2 0.6 fusion.5
  24.3 0.1 copy.10
  24.4 0.1 reshape_squeeze.3.refs_2_
  25.7 4.9 %collective-permute-done = s32[4,2]{0,1:T(2,128)S(1)} collective-permute-done((s32[4,2]{0,1:T(2,128)S(1)}, s32[4,2]{0,1:T(2,128)S(1)}, u32[]{:S(2)}, u32[]{:S(2)}) %collective-permute-start) | collective-permute-done | bytes 64 | tf_op jit(solution)/shard_map/ppermute | solution.py:212
  30.6 0.1 copy.11
  30.7 0.1 reshape.11.refs_3_
  30.8 0.0 collective-permute-done.1.refs_12_.refs_9_
  30.8 28.5 %all-to-all-done = bf16[32,104,256]{2,1,0:T(8,128)(2,1)} async-done(((bf16[32,104,256]{2,1,0:T(8,128)(2,1)}), bf16[32,104,256]{2,1,0:T(8,128)(2,1)}, u32[]{:S(2)}, u32[]{:S(2)}) %all-to-all-start) | async-done | bytes 1703968 | tf_op jit(solution)/shard_map/all_to_all | solution.py:208
  59.3 0.8 constant_dynamic-slice_fusion
  60.2 0.1 reshape.12.refs_1_
  60.3 15.0 %all_gather.3.refs_4_ = bf16[2,384,256]{2,1,0:T(8,128)(2,1)S(1)} all-gather(bf16[2,96,256]{2,1,0:T(8,128)(2,1)S(1)} %fusion), channel_id=1, replica_groups=mesh['y_lo'=4,'z'=8,'y_hi'=2,'x'=4,'core'=2] {'y_lo'}, dimensions={1}, use_global_device_ids=true | all-gather | bytes 491520 | tf_op jit(solution)/shard_map/all_gather | solution.py:221
  75.3 3.2 %collective-permute-start.3 = (bf16[2,384,256]{2,1,0:T(8,128)(2,1)S(1)}, bf16[2,384,256]{2,1,0:T(8,128)(2,1)S(1)}, u32[]{:S(2)}, u32[]{:S(2)}) collective-permute-start(bf16[2,384,256]{2,1,0:T(8,128)(2,1)S(1)} %all_gather.3.refs_4_), channel_id=1, source_target_pairs={{0,112},{16,0},{32,16},{48,32},{64,48},{80,64},{96,80},{112,96},{1... | collective-permute-start | bytes 1179656 | tf_op jit(solution)/shard_map/ppermute | solution.py:228
  78.5 2.6 %collective-permute-start.2 = (bf16[2,384,256]{2,1,0:T(8,128)(2,1)S(1)}, bf16[2,384,256]{2,1,0:T(8,128)(2,1)S(1)}, u32[]{:S(2)}, u32[]{:S(2)}) collective-permute-start(bf16[2,384,256]{2,1,0:T(8,128)(2,1)S(1)} %all_gather.3.refs_4_), channel_id=1, source_target_pairs={{0,16},{16,32},{32,48},{48,64},{64,80},{80,96},{96,112},{112,0},{1... | collective-permute-start | bytes 1179656 | tf_op jit(solution)/shard_map/ppermute | solution.py:227
  81.1 0.7 collective-permute-start.10
  81.9 4.1 %collective-permute-done.3.refs_6_ = bf16[2,384,256]{2,1,0:T(8,128)(2,1)S(1)} collective-permute-done((bf16[2,384,256]{2,1,0:T(8,128)(2,1)S(1)}, bf16[2,384,256]{2,1,0:T(8,128)(2,1)S(1)}, u32[]{:S(2)}, u32[]{:S(2)}) %collective-permute-start.3) | collective-permute-done | bytes 393248 | tf_op jit(solution)/shard_map/ppermute | solution.py:228
  86.0 3.4 %collective-permute-start.5 = (bf16[2,384,256]{2,1,0:T(8,128)(2,1)S(1)}, bf16[2,384,256]{2,1,0:T(8,128)(2,1)S(1)}, u32[]{:S(2)}, u32[]{:S(2)}) collective-permute-start(bf16[2,384,256]{2,1,0:T(8,128)(2,1)S(1)} %collective-permute-done.3.refs_6_), channel_id=1, source_target_pairs={{0,112},{16,0},{32,16},{48,32},{64,48},{80,64},{96,80},{112,96},{1... | collective-permute-start | bytes 1179656 | tf_op jit(solution)/shard_map/ppermute | solution.py:228
  89.4 0.0 collective-permute-done.2.refs_5_
  89.4 2.4 %collective-permute-start.4 = (bf16[2,384,256]{2,1,0:T(8,128)(2,1)S(1)}, bf16[2,384,256]{2,1,0:T(8,128)(2,1)S(1)}, u32[]{:S(2)}, u32[]{:S(2)}) collective-permute-start(bf16[2,384,256]{2,1,0:T(8,128)(2,1)S(1)} %collective-permute-done.2.refs_5_), channel_id=1, source_target_pairs={{0,16},{16,32},{32,48},{48,64},{64,80},{80,96},{96,112},{112,0},{1... | collective-permute-start | bytes 1179656 | tf_op jit(solution)/shard_map/ppermute | solution.py:227
  91.8 5.6 %collective-permute-done.5.refs_8_ = bf16[2,384,256]{2,1,0:T(8,128)(2,1)S(1)} collective-permute-done((bf16[2,384,256]{2,1,0:T(8,128)(2,1)S(1)}, bf16[2,384,256]{2,1,0:T(8,128)(2,1)S(1)}, u32[]{:S(2)}, u32[]{:S(2)}) %collective-permute-start.5) | collective-permute-done | bytes 393248 | tf_op jit(solution)/shard_map/ppermute | solution.py:228
  97.4 2.9 %collective-permute-start.7 = (bf16[2,384,256]{2,1,0:T(8,128)(2,1)S(1)}, bf16[2,384,256]{2,1,0:T(8,128)(2,1)S(1)}, u32[]{:S(2)}, u32[]{:S(2)}) collective-permute-start(bf16[2,384,256]{2,1,0:T(8,128)(2,1)S(1)} %collective-permute-done.5.refs_8_), channel_id=1, source_target_pairs={{0,112},{16,0},{32,16},{48,32},{64,48},{80,64},{96,80},{112,96},{1... | collective-permute-start | bytes 1179656 | tf_op jit(solution)/shard_map/ppermute | solution.py:228
  100.3 0.3 collective-permute-done.4.refs_7_
  100.7 2.6 %collective-permute-start.6 = (bf16[2,384,256]{2,1,0:T(8,128)(2,1)S(1)}, bf16[2,384,256]{2,1,0:T(8,128)(2,1)S(1)}, u32[]{:S(2)}, u32[]{:S(2)}) collective-permute-start(bf16[2,384,256]{2,1,0:T(8,128)(2,1)S(1)} %collective-permute-done.4.refs_7_), channel_id=1, source_target_pairs={{0,16},{16,32},{32,48},{48,64},{64,80},{80,96},{96,112},{112,0},{1... | collective-permute-start | bytes 1179656 | tf_op jit(solution)/shard_map/ppermute | solution.py:227
  103.3 1.9 %shard_map.65.refs_14_ = f32[2,4,256,256]{3,2,1,0:T(8,128)S(1)} custom-call(s32[1]{0:T(128)} %bitcast.5.refs_0_, s32[32]{0:T(128)S(1)} %reshape.12.refs_1_, s32[8]{0:T(128)S(1)} %reshape_squeeze.3.refs_2_, s32[8]{0:T(128)S(1)} %reshape.11.refs_3_, bf16[2,384,256]{2,1,0:T(8,128)(2,1)S(1)} %all_gather.3.refs_4_, ...), custom_call_target="tpu_custom_call" | custom-call | flops 402653184 | bytes 1048576 | tf_op jit(solution)/shard_map/pallas_call | solution.py:139
  105.2 1.9 %collective-permute-done.7.refs_10_.refs_5_ = bf16[2,384,256]{2,1,0:T(8,128)(2,1)S(1)} collective-permute-done((bf16[2,384,256]{2,1,0:T(8,128)(2,1)S(1)}, bf16[2,384,256]{2,1,0:T(8,128)(2,1)S(1)}, u32[]{:S(2)}, u32[]{:S(2)}) %collective-permute-start.7) | collective-permute-done | bytes 393248 | tf_op jit(solution)/shard_map/ppermute | solution.py:228
  107.1 4.4 %collective-permute-done.6.refs_9_.refs_4_ = bf16[2,384,256]{2,1,0:T(8,128)(2,1)S(1)} collective-permute-done((bf16[2,384,256]{2,1,0:T(8,128)(2,1)S(1)}, bf16[2,384,256]{2,1,0:T(8,128)(2,1)S(1)}, u32[]{:S(2)}, u32[]{:S(2)}) %collective-permute-start.6) | collective-permute-done | bytes 393248 | tf_op jit(solution)/shard_map/ppermute | solution.py:227
  111.6 1.9 %collective-permute-start.9 = (bf16[2,192,256]{2,1,0:T(8,128)(2,1)S(1)}, bf16[2,192,256]{2,1,0:T(8,128)(2,1)S(1)}, u32[]{:S(2)}, u32[]{:S(2)}) collective-permute-start(bf16[2,192,256]{2,1,0:T(8,128)(2,1)S(1)} %slice.23), channel_id=1, source_target_pairs={{0,112},{16,0},{32,16},{48,32},{64,48},{80,64},{96,80},{112,96},{1... | collective-permute-start | bytes 589832 | tf_op jit(solution)/shard_map/ppermute | solution.py:244
  113.5 3.9 %collective-permute-start.8 = (bf16[2,192,256]{2,1,0:T(8,128)(2,1)S(1)}, bf16[2,192,256]{2,1,0:T(8,128)(2,1)S(1)}, u32[]{:S(2)}, u32[]{:S(2)}) collective-permute-start(bf16[2,192,256]{2,1,0:T(8,128)(2,1)S(1)} %slice.22), channel_id=1, source_target_pairs={{0,16},{16,32},{32,48},{48,64},{64,80},{80,96},{96,112},{112,0},{1... | collective-permute-start | bytes 589832 | tf_op jit(solution)/shard_map/ppermute | solution.py:243
  117.4 0.0 collective-permute-done.10.refs_13_.refs_10_
  117.4 4.4 %shard_map.66.refs_11_ = bf16[4,256,1024]{2,1,0:T(8,128)(2,1)} custom-call(s32[1]{0:T(128)} %bitcast.5.refs_0_, s32[32]{0:T(128)S(1)} %reshape.12.refs_1_, s32[8]{0:T(128)S(1)} %reshape_squeeze.3.refs_2_, s32[8]{0:T(128)S(1)} %reshape.11.refs_3_, bf16[2,384,256]{2,1,0:T(8,128)(2,1)S(1)} %all_gather.3.refs_4_, ...), custom_call_target="tpu_custom_call" | custom-call | flops 805306368 | bytes 1048576 | tf_op jit(solution)/shard_map/pallas_call | solution.py:139
  121.9 0.0 collective-permute-done.9.refs_7_
  121.9 0.4 collective-permute-done.8.refs_6_
  122.3 2.8 %shard_map.67 = bf16[4,256,1024]{2,1,0:T(8,128)(2,1)} custom-call(s32[1]{0:T(128)} %bitcast.5.refs_0_, s32[32]{0:T(128)S(1)} %reshape.12.refs_1_, s32[8]{0:T(128)S(1)} %reshape_squeeze.3.refs_2_, s32[8]{0:T(128)S(1)} %reshape.11.refs_3_, bf16[2,384,256]{2,1,0:T(8,128)(2,1)S(1)} %collective-permute-done.6.refs_9_.refs_4_, ...), custom_call_target="tpu_custom_call", output_to_operand_aliasing={{}: (11, {})} | custom-call | flops 402653184 | bytes 1048576 | tf_op jit(solution)/shard_map/pallas_call | solution.py:139
  (5 shorter events, 0.1 us)
Async XLA Ops:
  2.3 14.0 %copy-start = (bf16[1,1,4,256,512]{4,3,2,1,0:T(8,128)(2,1)S(1)}, bf16[1,1,4,256,512]{4,3,2,1,0:T(8,128)(2,1)}, u32[]{:S(2)}) copy-start(bf16[1,1,4,256,512]{4,3,2,1,0:T(8,128)(2,1)} %param.10) | copy-start | bytes 3145732
  2.3 16.0 %copy-start.1 = (s32[1,1,4,2]{2,3,1,0:T(2,128)S(1)}, s32[1,1,4,2]{2,3,1,0:T(2,128)}, u32[]{:S(2)}) copy-start(s32[1,1,4,2]{2,3,1,0:T(2,128)} %param.11) | copy-start | bytes 100
  2.3 18.8 %copy-start.2 = (s32[1,2]{1,0:T(1,128)S(1)}, s32[1,2]{1,0:T(1,128)}, u32[]{:S(2)}) copy-start(s32[1,2]{1,0:T(1,128)} %param.9) | copy-start | bytes 28
  2.3 57.0 %all-to-all-start = ((bf16[32,104,256]{2,1,0:T(8,128)(2,1)}), bf16[32,104,256]{2,1,0:T(8,128)(2,1)}, u32[]{:S(2)}, u32[]{:S(2)}) async-start(bf16[32,104,256]{2,1,0:T(8,128)(2,1)} %shard_map.64), calls=%async_computation | async-start | bytes 3407872 | tf_op jit(solution)/shard_map/all_to_all | solution.py:208
  16.4 14.4 %collective-permute-start.1 = (bf16[4,256,512]{2,1,0:T(8,128)(2,1)S(1)}, bf16[4,256,512]{2,1,0:T(8,128)(2,1)S(1)}, u32[]{:S(2)}, u32[]{:S(2)}) collective-permute-start(bf16[4,256,512]{2,1,0:T(8,128)(2,1)S(1)} %bitcast.24), channel_id=1, source_target_pairs={{1,0},{2,1},{3,2},{4,3},{5,4},{6,5},{7,6},{9,8},{10,9},{11,10},{12... | collective-permute-start | bytes 3145736 | tf_op jit(solution)/shard_map/ppermute | solution.py:216
  18.3 12.3 %collective-permute-start = (s32[4,2]{0,1:T(2,128)S(1)}, s32[4,2]{0,1:T(2,128)S(1)}, u32[]{:S(2)}, u32[]{:S(2)}) collective-permute-start(s32[4,2]{0,1:T(2,128)S(1)} %bitcast.31), channel_id=1, source_target_pairs={{1,0},{2,1},{3,2},{4,3},{5,4},{6,5},{7,6},{8,7},{9,8},{10,9},{11,1... | collective-permute-start | bytes 104 | tf_op jit(solution)/shard_map/ppermute | solution.py:212
  75.3 10.7 %collective-permute-start.3 = (bf16[2,384,256]{2,1,0:T(8,128)(2,1)S(1)}, bf16[2,384,256]{2,1,0:T(8,128)(2,1)S(1)}, u32[]{:S(2)}, u32[]{:S(2)}) collective-permute-start(bf16[2,384,256]{2,1,0:T(8,128)(2,1)S(1)} %all_gather.3.refs_4_), channel_id=1, source_target_pairs={{0,112},{16,0},{32,16},{48,32},{64,48},{80,64},{96,80},{112,96},{1... | collective-permute-start | bytes 1179656 | tf_op jit(solution)/shard_map/ppermute | solution.py:228
  78.5 10.9 %collective-permute-start.2 = (bf16[2,384,256]{2,1,0:T(8,128)(2,1)S(1)}, bf16[2,384,256]{2,1,0:T(8,128)(2,1)S(1)}, u32[]{:S(2)}, u32[]{:S(2)}) collective-permute-start(bf16[2,384,256]{2,1,0:T(8,128)(2,1)S(1)} %all_gather.3.refs_4_), channel_id=1, source_target_pairs={{0,16},{16,32},{32,48},{48,64},{64,80},{80,96},{96,112},{112,0},{1... | collective-permute-start | bytes 1179656 | tf_op jit(solution)/shard_map/ppermute | solution.py:227
  81.1 36.3 %collective-permute-start.10 = (bf16[4,256,512]{2,1,0:T(8,128)(2,1)S(1)}, bf16[4,256,512]{2,1,0:T(8,128)(2,1)S(1)}, u32[]{:S(2)}, u32[]{:S(2)}) collective-permute-start(bf16[4,256,512]{2,1,0:T(8,128)(2,1)S(1)} %bitcast.25), channel_id=1, source_target_pairs={{8,7},{0,15},{24,23},{16,31},{40,39},{32,47},{56,55},{48,63},{72,7... | collective-permute-start | bytes 3145736 | tf_op jit(solution)/shard_map/ppermute | solution.py:223
  86.0 11.5 %collective-permute-start.5 = (bf16[2,384,256]{2,1,0:T(8,128)(2,1)S(1)}, bf16[2,384,256]{2,1,0:T(8,128)(2,1)S(1)}, u32[]{:S(2)}, u32[]{:S(2)}) collective-permute-start(bf16[2,384,256]{2,1,0:T(8,128)(2,1)S(1)} %collective-permute-done.3.refs_6_), channel_id=1, source_target_pairs={{0,112},{16,0},{32,16},{48,32},{64,48},{80,64},{96,80},{112,96},{1... | collective-permute-start | bytes 1179656 | tf_op jit(solution)/shard_map/ppermute | solution.py:228
  89.4 11.3 %collective-permute-start.4 = (bf16[2,384,256]{2,1,0:T(8,128)(2,1)S(1)}, bf16[2,384,256]{2,1,0:T(8,128)(2,1)S(1)}, u32[]{:S(2)}, u32[]{:S(2)}) collective-permute-start(bf16[2,384,256]{2,1,0:T(8,128)(2,1)S(1)} %collective-permute-done.2.refs_5_), channel_id=1, source_target_pairs={{0,16},{16,32},{32,48},{48,64},{64,80},{80,96},{96,112},{112,0},{1... | collective-permute-start | bytes 1179656 | tf_op jit(solution)/shard_map/ppermute | solution.py:227
  97.4 9.7 %collective-permute-start.7 = (bf16[2,384,256]{2,1,0:T(8,128)(2,1)S(1)}, bf16[2,384,256]{2,1,0:T(8,128)(2,1)S(1)}, u32[]{:S(2)}, u32[]{:S(2)}) collective-permute-start(bf16[2,384,256]{2,1,0:T(8,128)(2,1)S(1)} %collective-permute-done.5.refs_8_), channel_id=1, source_target_pairs={{0,112},{16,0},{32,16},{48,32},{64,48},{80,64},{96,80},{112,96},{1... | collective-permute-start | bytes 1179656 | tf_op jit(solution)/shard_map/ppermute | solution.py:228
  100.7 10.9 %collective-permute-start.6 = (bf16[2,384,256]{2,1,0:T(8,128)(2,1)S(1)}, bf16[2,384,256]{2,1,0:T(8,128)(2,1)S(1)}, u32[]{:S(2)}, u32[]{:S(2)}) collective-permute-start(bf16[2,384,256]{2,1,0:T(8,128)(2,1)S(1)} %collective-permute-done.4.refs_7_), channel_id=1, source_target_pairs={{0,16},{16,32},{32,48},{48,64},{64,80},{80,96},{96,112},{112,0},{1... | collective-permute-start | bytes 1179656 | tf_op jit(solution)/shard_map/ppermute | solution.py:227
  111.6 10.3 %collective-permute-start.9 = (bf16[2,192,256]{2,1,0:T(8,128)(2,1)S(1)}, bf16[2,192,256]{2,1,0:T(8,128)(2,1)S(1)}, u32[]{:S(2)}, u32[]{:S(2)}) collective-permute-start(bf16[2,192,256]{2,1,0:T(8,128)(2,1)S(1)} %slice.23), channel_id=1, source_target_pairs={{0,112},{16,0},{32,16},{48,32},{64,48},{80,64},{96,80},{112,96},{1... | collective-permute-start | bytes 589832 | tf_op jit(solution)/shard_map/ppermute | solution.py:244
  113.5 8.8 %collective-permute-start.8 = (bf16[2,192,256]{2,1,0:T(8,128)(2,1)S(1)}, bf16[2,192,256]{2,1,0:T(8,128)(2,1)S(1)}, u32[]{:S(2)}, u32[]{:S(2)}) collective-permute-start(bf16[2,192,256]{2,1,0:T(8,128)(2,1)S(1)} %slice.22), channel_id=1, source_target_pairs={{0,16},{16,32},{32,48},{48,64},{64,80},{80,96},{96,112},{112,0},{1... | collective-permute-start | bytes 589832 | tf_op jit(solution)/shard_map/ppermute | solution.py:243

commit v7 on v6

--- a/solution.py
+++ b/solution.py
@@ -21,8 +21,17 @@
 META = 8
 
 
-def z_route(distance):
-    return [(i, (i + distance) % Z) for i in range(Z)]
+def swap_route(toward):
+    pairs = []
+    for z in range(Z):
+        for core in range(2):
+            side = toward if (z + core) % 2 == 0 else -toward
+            pairs.append((z * 2 + core, ((z + side) % Z) * 2 + core))
+    return pairs
+
+
+def swapped(value, toward):
+    return lax.ppermute(value, ("z", "core"), swap_route(toward))
 
 
 def col_route(n):
@@ -43,13 +52,12 @@
 def strips(parts):
     found = []
     at = 0
-    for ref in parts:
-        rows = ref.shape[1]
+    for ref, base in parts:
         off = 0
-        while off < rows:
+        while off < SPAN:
             slot = at // BS
-            take = min(rows - off, (slot + 1) * BS - at)
-            found.append((slot, at - slot * BS, ref, off, take))
+            take = min(SPAN - off, (slot + 1) * BS - at)
+            found.append((slot, at - slot * BS, ref, base + off, take))
             off += take
             at += take
     return found
@@ -93,12 +101,17 @@
     return copy
 
 
+def near_rows(own, r1, r2):
+    here = ((0, ((own, 0), (r1, 0))), (-1, ((r1, 0), (own, 0))))
+    next_to = ((-2, ((r2, SPAN), (r2, 0))), (1, ((r2, 0), (r2, SPAN))))
+    return here, next_to
+
+
 def first_section(*refs):
-    scalars, (own, f1, b1, f2, b2, b_here, part, acc, sem) = refs[:4], refs[4:]
+    scalars, (own, r1, r2, b_here, part, acc, sem) = refs[:4], refs[4:]
     acc[...] = jnp.zeros_like(acc)
-    rows = (((0, (own, b1)), (-1, (f1, own))), ((-2, (f2, f1)), (1, (b1, b2))))
     copies = []
-    for n, (even, odd) in enumerate(rows):
+    for n, (even, odd) in enumerate(near_rows(own, r1, r2)):
         on_parity(scalars, even, odd, (0,), (b_here,), acc.at[n])
         copies.append(pltpu.make_async_copy(acc.at[n], part.at[n], sem.at[n]))
         copies[-1].start()
@@ -108,16 +121,16 @@
 
 def three_rows(*refs):
     scalars = refs[:4]
-    own, f1, b1, f2, b2, f3, b3, b_here, b_in, b_over, part, out, acc, o_s, sem = refs[4:]
+    own, r1, r2, r3, b_here, b_in, b_over, part, out, acc, o_s, sem = refs[4:]
     b_refs = (b_here, (b_in, b_over))
     loads = [pltpu.make_async_copy(part.at[n], acc.at[n], sem.at[n]) for n in range(2)]
     for c in loads:
         c.start()
     acc[2] = jnp.zeros_like(acc[2])
-    i = on_parity(scalars, (2, (b2, b3)), (-3, (f3, f2)), (0, 1), b_refs, acc.at[2])
+    even, odd = (2, ((r3, 0), (r3, SPAN))), (-3, ((r3, SPAN), (r3, 0)))
+    i = on_parity(scalars, even, odd, (0, 1), b_refs, acc.at[2])
     writes = [write_row(o_s.at[2], acc.at[2], out, i, sem.at[2])]
-    rows = (((0, (own, b1)), (-1, (f1, own))), ((-2, (f2, f1)), (1, (b1, b2))))
-    for n, (even, odd) in enumerate(rows):
+    for n, (even, odd) in enumerate(near_rows(own, r1, r2)):
         loads[n].wait()
         i = on_parity(scalars, even, odd, (1,), b_refs, acc.at[n])
         writes.append(write_row(o_s.at[n], acc.at[n], out, i, sem.at[3 + n]))
@@ -127,9 +140,10 @@
 
 def last_row(*refs):
     scalars = refs[:4]
-    f3, b3, f4, b4, b_here, b_in, b_over, before, out, acc, o_s, sem = refs[4:]
+    r4, b_here, b_in, b_over, before, out, acc, o_s, sem = refs[4:]
     acc[...] = jnp.zeros_like(acc)
-    i = on_parity(scalars, (4, (f4, b4, f3)), (3, (b3, f4, b4)), (0, 1), (b_here, (b_in, b_over)), acc)
+    even, odd = (-4, ((r4, SPAN), (r4, 0))), (3, ((r4, 0), (r4, SPAN)))
+    i = on_parity(scalars, even, odd, (0, 1), (b_here, (b_in, b_over)), acc)
     write_row(o_s, acc, out, i, sem.at[0]).wait()
 
 
@@ -152,21 +166,18 @@
     )(*scalars, *held, *left)
 
 
-CHUNKS = 4
-
-
-def payload_rows(a_columns, a_live, tile, out, columns, live, wide, rows, sem):
-    step = PIECES // CHUNKS
+def payload_rows(shift, a_columns, a_live, tile, out, columns, live, wide, rows, sem):
     small = [
-        pltpu.make_async_copy(a_columns, columns, sem.at[2 * CHUNKS]),
-        pltpu.make_async_copy(a_live, live, sem.at[2 * CHUNKS + 1]),
+        pltpu.make_async_copy(a_columns, columns, sem.at[2 * Z]),
+        pltpu.make_async_copy(a_live, live, sem.at[2 * Z + 1]),
     ]
     reads = []
     writes = []
-    for c in range(CHUNKS):
-        part = pl.ds(c * step, step)
-        reads.append(pltpu.make_async_copy(tile.at[part], rows.at[part, :PIECE], sem.at[c]))
-        writes.append(pltpu.make_async_copy(rows.at[part], out.at[part], sem.at[CHUNKS + c]))
+    for c in range(Z):
+        part = pl.ds(c * Y_LO, Y_LO)
+        first = ((c + Z - shift[0]) % Z) * Y_LO
+        reads.append(pltpu.make_async_copy(tile.at[pl.ds(first, Y_LO)], rows.at[part, :PIECE], sem.at[c]))
+        writes.append(pltpu.make_async_copy(rows.at[part], out.at[part], sem.at[Z + c]))
     for c in small + reads:
         c.start()
     wide[...] = jnp.zeros_like(wide)
@@ -184,34 +195,40 @@
         w.wait()
 
 
-def payload(a_columns, a_live, tile):
+def payload(core, a_columns, a_live, tile):
     hbm = pl.BlockSpec(memory_space=pltpu.HBM)
     return pl.pallas_call(
         payload_rows,
         out_shape=jax.ShapeDtypeStruct((PIECES, PIECE + META, BS), jnp.bfloat16),
-        in_specs=[hbm, hbm, hbm],
-        out_specs=hbm,
-        scratch_shapes=[
-            pltpu.VMEM((NZA, 1, MB), jnp.int32),
-            pltpu.VMEM((1, MB), jnp.int32),
-            pltpu.VMEM((META, BS), jnp.float32),
-            pltpu.VMEM((PIECES, PIECE + META, BS), jnp.bfloat16),
-            pltpu.SemaphoreType.DMA((2 * CHUNKS + 2,)),
-        ],
+        grid_spec=pltpu.PrefetchScalarGridSpec(
+            num_scalar_prefetch=1,
+            grid=(),
+            in_specs=[hbm, hbm, hbm],
+            out_specs=hbm,
+            scratch_shapes=[
+                pltpu.VMEM((NZA, 1, MB), jnp.int32),
+                pltpu.VMEM((1, MB), jnp.int32),
+                pltpu.VMEM((META, BS), jnp.float32),
+                pltpu.VMEM((PIECES, PIECE + META, BS), jnp.bfloat16),
+                pltpu.SemaphoreType.DMA((2 * Z + 2,)),
+            ],
+        ),
         compiler_params=pltpu.CompilerParams(vmem_limit_bytes=4 * 1024 * 1024),
-    )(*(pltpu.with_memory_space_constraint(x, pltpu.HBM) for x in (a_columns, a_live, tile)))
+    )(core[None], *(pltpu.with_memory_space_constraint(x, pltpu.HBM) for x in (a_columns, a_live, tile)))
 
 
 def on_device(a_blocks, a_columns, a_live, owner_map, b_blocks, b_columns):
     tile = a_blocks.reshape(PIECES, PIECE, BS)
     cols = lax.axis_size(COL)
-    got = lax.all_to_all(payload(a_columns[0].transpose(2, 0, 1), a_live[0], tile), ("z", "y_lo"), 0, 0, tiled=True)
+    core = lax.axis_index("core").astype(jnp.int32)
+    sent = payload(core, a_columns[0].transpose(2, 0, 1), a_live[0], tile)
+    got = lax.all_to_all(sent, ("z", "y_lo"), 0, 0, tiled=True)
     holder = owner_map[0]
     source = (holder % Z) * Y_LO + holder // Z
     bc_here = b_columns[0, 0]
     bc_next = lax.ppermute(bc_here, COL, col_route(cols)).reshape(-1)
     bc_here = bc_here.reshape(-1)
-    place = lax.axis_index("z").astype(jnp.int32)[None]
+    place = ((lax.axis_index("z").astype(jnp.int32) + Z - core) % Z)[None]
     b_here = b_blocks[0, 0]
     b_in = lax.ppermute(b_here, COL, within(cols))
     got, bc_here, bc_next, place, b_in = lax.optimization_barrier((got, bc_here, bc_next, place, b_in))
@@ -221,13 +238,11 @@
     own = lax.all_gather(two[:, :PIECE], "y_lo", axis=1, tiled=True)
     b_ready, own, table = lax.optimization_barrier((b_here, own, table))
     b_over = lax.ppermute(b_ready, COL, across(cols))
-    ahead = [own]
-    back = [own]
-    for step in range(3):
-        ahead.append(lax.ppermute(ahead[-1], "z", z_route(1)))
-        back.append(lax.ppermute(back[-1], "z", z_route(-1)))
+    r1 = swapped(own, 1)
+    r2 = swapped(jnp.concatenate([own, r1], axis=1), -1)
+    r3 = swapped(r2, 1)
     scalars = (place, table, bc_here, bc_next)
-    near = (own, ahead[1], back[1], ahead[2], back[2])
+    near = (own, r1, r2)
     block = (NB, BS, BS)
     shape = jax.ShapeDtypeStruct((MB, BS, NB * BS), jnp.bfloat16)
     part = call(
@@ -239,13 +254,12 @@
         [pltpu.VMEM((2,) + block, jnp.float32), pltpu.SemaphoreType.DMA((2,))],
         6,
     )
-    part, ahead[3], back[3] = lax.optimization_barrier((part, ahead[3], back[3]))
-    f4 = lax.ppermute(ahead[3][:, : SPAN // 2], "z", z_route(1))
-    b4 = lax.ppermute(back[3][:, SPAN // 2 :], "z", z_route(-1))
+    part, r3, b_over = lax.optimization_barrier((part, r3, b_over))
+    r4 = swapped(r3, -1)
     window = call(
         three_rows,
         scalars,
-        near + (ahead[3], back[3], b_here, b_in, b_over),
+        near + (r3, b_here, b_in, b_over),
         (part,),
         shape,
         [
@@ -258,7 +272,7 @@
     window = call(
         last_row,
         scalars,
-        (ahead[3], back[3], f4, b4, b_here, b_in, b_over),
+        (r4, b_here, b_in, b_over),
         (window,),
         shape,
         [pltpu.VMEM(block, jnp.float32), pltpu.VMEM((BS, NB * BS), jnp.bfloat16), pltpu.SemaphoreType.DMA((1,))],

time: 126 us -> 137 us (1.087)
  the two profiles are of different devices: /device:TPU:6 before, /device:TPU:2 now
where the time goes in v7:
time: 137 us; the launch traced here: 136 us
  waiting for transfers between devices  76.5 us (56%)
  starting transfers between devices  28.3 us (21%)
  blocking collectives  15 us (11%)
  Pallas kernels  11 us (8%)
  between operations  3.67 us (3%)
  local copies, waits for them, and re-layouts  1.85 us (1%)
    ppermute x4, waiting for transfers between devices, swapped(): return lax.ppermute(value, ('z', 'core'), swap_route(toward))  42.5 us
    all_to_all x1, waiting for transfers between devices, on_device(): got = lax.all_to_all(sent, ('z', 'y_lo'), 0, 0, tiled=True)  28.5 us
    all_gather x1, blocking collectives, on_device(): own = lax.all_gather(two[:, :PIECE], 'y_lo', axis=1, tiled=True)  15 us
    all_to_all x1, starting transfers between devices, on_device(): got = lax.all_to_all(sent, ('z', 'y_lo'), 0, 0, tiled=True)  14 us
    ppermute x4, starting transfers between devices, swapped(): return lax.ppermute(value, ('z', 'core'), swap_route(toward))  9.09 us
    pallas_call x3, Pallas kernels, call(): pl.pallas_call(kernel, out_shape=out_shape, grid_spec=pltpu.PrefetchScala...  8.67 us
    ppermute x1, waiting for transfers between devices, on_device(): bc_next = lax.ppermute(bc_here, COL, col_route(cols)).reshape(-1)  5.5 us
  transfers between devices with their start and end apart: 8, of which 6 were waited for; matrix products, arithmetic and copies ran while one was open for 1% of the time, Pallas kernels for 4%

profile of v7, /device:TPU:2, one launch (start us, length us, event | category | flops | bytes accessed | tf_op | source)
XLA Modules:
  0.0 136.4 jit_solution(251857796889541488)
XLA Ops:
  0.0 2.4 %shard_map.64 = bf16[32,104,256]{2,1,0:T(8,128)(2,1)} custom-call(s32[1]{0:T(128)} %bitcast.shift, s32[3,1,4]{2,1,0:T(1,128)} %bitcast.31, s32[1,4]{1,0:T(1,128)} %bitcast.33, bf16[32,96,256]{2,1,0:T(8,128)(2,1)} %bitcast.30), custom_call_target="tpu_custom_call" | custom-call | tf_op jit(solution)/shard_map/pallas_call | solution.py:200
  2.4 0.0 copy-start
  2.4 0.0 copy-start.1
  2.4 0.0 copy-start.2
  2.4 14.0 %all-to-all-start = ((bf16[32,104,256]{2,1,0:T(8,128)(2,1)}), bf16[32,104,256]{2,1,0:T(8,128)(2,1)}, u32[]{:S(2)}, u32[]{:S(2)}) async-start(bf16[32,104,256]{2,1,0:T(8,128)(2,1)} %shard_map.64), calls=%async_computation | async-start | bytes 3407872 | tf_op jit(solution)/shard_map/all_to_all | solution.py:225
  16.4 0.0 copy-done
  16.4 1.9 %collective-permute-start.1 = (bf16[4,256,512]{2,1,0:T(8,128)(2,1)S(1)}, bf16[4,256,512]{2,1,0:T(8,128)(2,1)S(1)}, u32[]{:S(2)}, u32[]{:S(2)}) collective-permute-start(bf16[4,256,512]{2,1,0:T(8,128)(2,1)S(1)} %bitcast.25), channel_id=1, source_target_pairs={{1,0},{2,1},{3,2},{4,3},{5,4},{6,5},{7,6},{9,8},{10,9},{11,10},{12... | collective-permute-start | bytes 3145736 | tf_op jit(solution)/shard_map/ppermute | solution.py:233
  18.4 0.0 copy-done.1
  18.4 2.5 %collective-permute-start = (s32[4,2]{0,1:T(2,128)S(1)}, s32[4,2]{0,1:T(2,128)S(1)}, u32[]{:S(2)}, u32[]{:S(2)}) collective-permute-start(s32[4,2]{0,1:T(2,128)S(1)} %bitcast.32), channel_id=1, source_target_pairs={{1,0},{2,1},{3,2},{4,3},{5,4},{6,5},{7,6},{8,7},{9,8},{10,9},{11,1... | collective-permute-start | bytes 104 | tf_op jit(solution)/shard_map/ppermute | solution.py:229
  20.9 0.0 copy-done.2
  21.0 0.6 fusion.5
  23.8 0.1 copy.10
  23.9 0.1 reshape_squeeze.3.refs_2_
  25.2 5.5 %collective-permute-done = s32[4,2]{0,1:T(2,128)S(1)} collective-permute-done((s32[4,2]{0,1:T(2,128)S(1)}, s32[4,2]{0,1:T(2,128)S(1)}, u32[]{:S(2)}, u32[]{:S(2)}) %collective-permute-start) | collective-permute-done | bytes 64 | tf_op jit(solution)/shard_map/ppermute | solution.py:229
  30.7 0.1 copy.11
  30.8 0.1 reshape.11.refs_3_
  30.9 0.0 collective-permute-done.1.refs_9_.refs_6_
  30.9 28.5 %all-to-all-done = bf16[32,104,256]{2,1,0:T(8,128)(2,1)} async-done(((bf16[32,104,256]{2,1,0:T(8,128)(2,1)}), bf16[32,104,256]{2,1,0:T(8,128)(2,1)}, u32[]{:S(2)}, u32[]{:S(2)}) %all-to-all-start) | async-done | bytes 1703968 | tf_op jit(solution)/shard_map/all_to_all | solution.py:225
  59.4 0.8 constant_dynamic-slice_fusion
  60.3 0.1 reshape.12.refs_1_
  60.4 15.0 %all_gather.3.refs_4_ = bf16[2,384,256]{2,1,0:T(8,128)(2,1)S(1)} all-gather(bf16[2,96,256]{2,1,0:T(8,128)(2,1)S(1)} %fusion), channel_id=1, replica_groups=mesh['y_lo'=4,'z'=8,'y_hi'=2,'x'=4,'core'=2] {'y_lo'}, dimensions={1}, use_global_device_ids=true | all-gather | bytes 491520 | tf_op jit(solution)/shard_map/all_gather | solution.py:238
  75.4 2.5 %collective-permute-start.2 = (bf16[2,384,256]{2,1,0:T(8,128)(2,1)S(1)}, bf16[2,384,256]{2,1,0:T(8,128)(2,1)S(1)}, u32[]{:S(2)}, u32[]{:S(2)}) collective-permute-start(bf16[2,384,256]{2,1,0:T(8,128)(2,1)S(1)} %all_gather.3.refs_4_), channel_id=1, source_target_pairs={{0,16},{1,113},{16,0},{17,33},{32,48},{33,17},{48,32},{49,65},{64,... | collective-permute-start | bytes 1179656 | tf_op jit(solution)/shard_map/ppermute | solution.py:34
  77.9 7.6 %collective-permute-done.2.refs_5_ = bf16[2,384,256]{2,1,0:T(8,128)(2,1)S(1)} collective-permute-done((bf16[2,384,256]{2,1,0:T(8,128)(2,1)S(1)}, bf16[2,384,256]{2,1,0:T(8,128)(2,1)S(1)}, u32[]{:S(2)}, u32[]{:S(2)}) %collective-permute-start.2) | collective-permute-done | bytes 393248 | tf_op jit(solution)/shard_map/ppermute | solution.py:34
  85.5 0.1 pad_maximum_fusion
  85.6 2.7 %collective-permute-start.3 = (bf16[2,768,256]{2,1,0:T(8,128)(2,1)S(1)}, bf16[2,768,256]{2,1,0:T(8,128)(2,1)S(1)}, u32[]{:S(2)}, u32[]{:S(2)}) collective-permute-start(bf16[2,768,256]{2,1,0:T(8,128)(2,1)S(1)} %pad_maximum_fusion), channel_id=1, source_target_pairs={{0,112},{1,17},{16,32},{17,1},{32,16},{33,49},{48,64},{49,33},{64,... | collective-permute-start | bytes 2359304 | tf_op jit(solution)/shard_map/ppermute | solution.py:34
  88.3 0.7 collective-permute-start.5
  89.0 13.0 %collective-permute-done.3.refs_6_ = bf16[2,768,256]{2,1,0:T(8,128)(2,1)S(1)} collective-permute-done((bf16[2,768,256]{2,1,0:T(8,128)(2,1)S(1)}, bf16[2,768,256]{2,1,0:T(8,128)(2,1)S(1)}, u32[]{:S(2)}, u32[]{:S(2)}) %collective-permute-start.3) | collective-permute-done | bytes 786464 | tf_op jit(solution)/shard_map/ppermute | solution.py:34
  102.0 1.9 %collective-permute-start.4 = (bf16[2,768,256]{2,1,0:T(8,128)(2,1)S(1)}, bf16[2,768,256]{2,1,0:T(8,128)(2,1)S(1)}, u32[]{:S(2)}, u32[]{:S(2)}) collective-permute-start(bf16[2,768,256]{2,1,0:T(8,128)(2,1)S(1)} %collective-permute-done.3.refs_6_), channel_id=1, source_target_pairs={{0,16},{1,113},{16,0},{17,33},{32,48},{33,17},{48,32},{49,65},{64,... | collective-permute-start | bytes 2359304 | tf_op jit(solution)/shard_map/ppermute | solution.py:34
  103.9 2.2 %shard_map.65.refs_11_ = f32[2,4,256,256]{3,2,1,0:T(8,128)S(1)} custom-call(s32[1]{0:T(128)} %bitcast.6.refs_0_, s32[32]{0:T(128)S(1)} %reshape.12.refs_1_, s32[8]{0:T(128)S(1)} %reshape_squeeze.3.refs_2_, s32[8]{0:T(128)S(1)} %reshape.11.refs_3_, bf16[2,384,256]{2,1,0:T(8,128)(2,1)S(1)} %all_gather.3.refs_4_, ...), custom_call_target="tpu_custom_call" | custom-call | flops 402653184 | bytes 1048576 | tf_op jit(solution)/shard_map/pallas_call | solution.py:153
  106.1 0.0 collective-permute-done.5.refs_10_.refs_7_
  106.1 12.2 %collective-permute-done.4.refs_7_ = bf16[2,768,256]{2,1,0:T(8,128)(2,1)S(1)} collective-permute-done((bf16[2,768,256]{2,1,0:T(8,128)(2,1)S(1)}, bf16[2,768,256]{2,1,0:T(8,128)(2,1)S(1)}, u32[]{:S(2)}, u32[]{:S(2)}) %collective-permute-start.4) | collective-permute-done | bytes 786464 | tf_op jit(solution)/shard_map/ppermute | solution.py:34
  118.3 1.9 %collective-permute-start.6 = (bf16[2,768,256]{2,1,0:T(8,128)(2,1)S(1)}, bf16[2,768,256]{2,1,0:T(8,128)(2,1)S(1)}, u32[]{:S(2)}, u32[]{:S(2)}) collective-permute-start(bf16[2,768,256]{2,1,0:T(8,128)(2,1)S(1)} %collective-permute-done.4.refs_7_), channel_id=1, source_target_pairs={{0,112},{1,17},{16,32},{17,1},{32,16},{33,49},{48,64},{49,33},{64,... | collective-permute-start | bytes 2359304 | tf_op jit(solution)/shard_map/ppermute | solution.py:34
  120.2 3.5 %shard_map.66.refs_8_ = bf16[4,256,1024]{2,1,0:T(8,128)(2,1)} custom-call(s32[1]{0:T(128)} %bitcast.6.refs_0_, s32[32]{0:T(128)S(1)} %reshape.12.refs_1_, s32[8]{0:T(128)S(1)} %reshape_squeeze.3.refs_2_, s32[8]{0:T(128)S(1)} %reshape.11.refs_3_, bf16[2,384,256]{2,1,0:T(8,128)(2,1)S(1)} %all_gather.3.refs_4_, ...), custom_call_target="tpu_custom_call" | custom-call | flops 805306368 | bytes 1048576 | tf_op jit(solution)/shard_map/pallas_call | solution.py:153
  123.7 9.7 %collective-permute-done.6.refs_4_ = bf16[2,768,256]{2,1,0:T(8,128)(2,1)S(1)} collective-permute-done((bf16[2,768,256]{2,1,0:T(8,128)(2,1)S(1)}, bf16[2,768,256]{2,1,0:T(8,128)(2,1)S(1)}, u32[]{:S(2)}, u32[]{:S(2)}) %collective-permute-start.6) | collective-permute-done | bytes 786464 | tf_op jit(solution)/shard_map/ppermute | solution.py:34
  133.4 3.0 %shard_map.67 = bf16[4,256,1024]{2,1,0:T(8,128)(2,1)} custom-call(s32[1]{0:T(128)} %bitcast.6.refs_0_, s32[32]{0:T(128)S(1)} %reshape.12.refs_1_, s32[8]{0:T(128)S(1)} %reshape_squeeze.3.refs_2_, s32[8]{0:T(128)S(1)} %reshape.11.refs_3_, bf16[2,768,256]{2,1,0:T(8,128)(2,1)S(1)} %collective-permute-done.6.refs_4_, ...), custom_call_target="tpu_custom_call", output_to_operand_aliasing={{}: (8, {})} | custom-call | flops 402653184 | bytes 1048576 | tf_op jit(solution)/shard_map/pallas_call | solution.py:153
  (3 shorter events, 0.0 us)
Async XLA Ops:
  2.4 14.0 %copy-start = (bf16[1,1,4,256,512]{4,3,2,1,0:T(8,128)(2,1)S(1)}, bf16[1,1,4,256,512]{4,3,2,1,0:T(8,128)(2,1)}, u32[]{:S(2)}) copy-start(bf16[1,1,4,256,512]{4,3,2,1,0:T(8,128)(2,1)} %param.10) | copy-start | bytes 3145732
  2.4 16.0 %copy-start.1 = (s32[1,1,4,2]{2,3,1,0:T(2,128)S(1)}, s32[1,1,4,2]{2,3,1,0:T(2,128)}, u32[]{:S(2)}) copy-start(s32[1,1,4,2]{2,3,1,0:T(2,128)} %param.11) | copy-start | bytes 100
  2.4 18.5 %copy-start.2 = (s32[1,2]{1,0:T(1,128)S(1)}, s32[1,2]{1,0:T(1,128)}, u32[]{:S(2)}) copy-start(s32[1,2]{1,0:T(1,128)} %param.9) | copy-start | bytes 28
  2.4 57.0 %all-to-all-start = ((bf16[32,104,256]{2,1,0:T(8,128)(2,1)}), bf16[32,104,256]{2,1,0:T(8,128)(2,1)}, u32[]{:S(2)}, u32[]{:S(2)}) async-start(bf16[32,104,256]{2,1,0:T(8,128)(2,1)} %shard_map.64), calls=%async_computation | async-start | bytes 3407872 | tf_op jit(solution)/shard_map/all_to_all | solution.py:225
  16.4 14.4 %collective-permute-start.1 = (bf16[4,256,512]{2,1,0:T(8,128)(2,1)S(1)}, bf16[4,256,512]{2,1,0:T(8,128)(2,1)S(1)}, u32[]{:S(2)}, u32[]{:S(2)}) collective-permute-start(bf16[4,256,512]{2,1,0:T(8,128)(2,1)S(1)} %bitcast.25), channel_id=1, source_target_pairs={{1,0},{2,1},{3,2},{4,3},{5,4},{6,5},{7,6},{9,8},{10,9},{11,10},{12... | collective-permute-start | bytes 3145736 | tf_op jit(solution)/shard_map/ppermute | solution.py:233
  18.4 12.3 %collective-permute-start = (s32[4,2]{0,1:T(2,128)S(1)}, s32[4,2]{0,1:T(2,128)S(1)}, u32[]{:S(2)}, u32[]{:S(2)}) collective-permute-start(s32[4,2]{0,1:T(2,128)S(1)} %bitcast.32), channel_id=1, source_target_pairs={{1,0},{2,1},{3,2},{4,3},{5,4},{6,5},{7,6},{8,7},{9,8},{10,9},{11,1... | collective-permute-start | bytes 104 | tf_op jit(solution)/shard_map/ppermute | solution.py:229
  75.4 10.2 %collective-permute-start.2 = (bf16[2,384,256]{2,1,0:T(8,128)(2,1)S(1)}, bf16[2,384,256]{2,1,0:T(8,128)(2,1)S(1)}, u32[]{:S(2)}, u32[]{:S(2)}) collective-permute-start(bf16[2,384,256]{2,1,0:T(8,128)(2,1)S(1)} %all_gather.3.refs_4_), channel_id=1, source_target_pairs={{0,16},{1,113},{16,0},{17,33},{32,48},{33,17},{48,32},{49,65},{64,... | collective-permute-start | bytes 1179656 | tf_op jit(solution)/shard_map/ppermute | solution.py:34
  85.6 16.4 %collective-permute-start.3 = (bf16[2,768,256]{2,1,0:T(8,128)(2,1)S(1)}, bf16[2,768,256]{2,1,0:T(8,128)(2,1)S(1)}, u32[]{:S(2)}, u32[]{:S(2)}) collective-permute-start(bf16[2,768,256]{2,1,0:T(8,128)(2,1)S(1)} %pad_maximum_fusion), channel_id=1, source_target_pairs={{0,112},{1,17},{16,32},{17,1},{32,16},{33,49},{48,64},{49,33},{64,... | collective-permute-start | bytes 2359304 | tf_op jit(solution)/shard_map/ppermute | solution.py:34
  88.3 17.8 %collective-permute-start.5 = (bf16[4,256,512]{2,1,0:T(8,128)(2,1)S(1)}, bf16[4,256,512]{2,1,0:T(8,128)(2,1)S(1)}, u32[]{:S(2)}, u32[]{:S(2)}) collective-permute-start(bf16[4,256,512]{2,1,0:T(8,128)(2,1)S(1)} %bitcast.26), channel_id=1, source_target_pairs={{8,7},{0,15},{24,23},{16,31},{40,39},{32,47},{56,55},{48,63},{72,7... | collective-permute-start | bytes 3145736 | tf_op jit(solution)/shard_map/ppermute | solution.py:240
  102.0 16.3 %collective-permute-start.4 = (bf16[2,768,256]{2,1,0:T(8,128)(2,1)S(1)}, bf16[2,768,256]{2,1,0:T(8,128)(2,1)S(1)}, u32[]{:S(2)}, u32[]{:S(2)}) collective-permute-start(bf16[2,768,256]{2,1,0:T(8,128)(2,1)S(1)} %collective-permute-done.3.refs_6_), channel_id=1, source_target_pairs={{0,16},{1,113},{16,0},{17,33},{32,48},{33,17},{48,32},{49,65},{64,... | collective-permute-start | bytes 2359304 | tf_op jit(solution)/shard_map/ppermute | solution.py:34
  118.3 15.1 %collective-permute-start.6 = (bf16[2,768,256]{2,1,0:T(8,128)(2,1)S(1)}, bf16[2,768,256]{2,1,0:T(8,128)(2,1)S(1)}, u32[]{:S(2)}, u32[]{:S(2)}) collective-permute-start(bf16[2,768,256]{2,1,0:T(8,128)(2,1)S(1)} %collective-permute-done.4.refs_7_), channel_id=1, source_target_pairs={{0,112},{1,17},{16,32},{17,1},{32,16},{33,49},{48,64},{49,33},{64,... | collective-permute-start | bytes 2359304 | tf_op jit(solution)/shard_map/ppermute | solution.py:34

commit v8 on v6

--- a/solution.py
+++ b/solution.py
@@ -93,34 +93,20 @@
     return copy
 
 
-def first_section(*refs):
-    scalars, (own, f1, b1, f2, b2, b_here, part, acc, sem) = refs[:4], refs[4:]
-    acc[...] = jnp.zeros_like(acc)
-    rows = (((0, (own, b1)), (-1, (f1, own))), ((-2, (f2, f1)), (1, (b1, b2))))
-    copies = []
-    for n, (even, odd) in enumerate(rows):
-        on_parity(scalars, even, odd, (0,), (b_here,), acc.at[n])
-        copies.append(pltpu.make_async_copy(acc.at[n], part.at[n], sem.at[n]))
-        copies[-1].start()
-    for c in copies:
-        c.wait()
-
-
 def three_rows(*refs):
     scalars = refs[:4]
-    own, f1, b1, f2, b2, f3, b3, b_here, b_in, b_over, part, out, acc, o_s, sem = refs[4:]
+    own, f1, b1, f2, b2, f3, b3, b_here, b_in, b_over, out, acc, o_s, sem = refs[4:]
     b_refs = (b_here, (b_in, b_over))
-    loads = [pltpu.make_async_copy(part.at[n], acc.at[n], sem.at[n]) for n in range(2)]
-    for c in loads:
-        c.start()
-    acc[2] = jnp.zeros_like(acc[2])
-    i = on_parity(scalars, (2, (b2, b3)), (-3, (f3, f2)), (0, 1), b_refs, acc.at[2])
-    writes = [write_row(o_s.at[2], acc.at[2], out, i, sem.at[2])]
-    rows = (((0, (own, b1)), (-1, (f1, own))), ((-2, (f2, f1)), (1, (b1, b2))))
+    rows = (
+        ((0, (own, b1)), (-1, (f1, own))),
+        ((-2, (f2, f1)), (1, (b1, b2))),
+        ((2, (b2, b3)), (-3, (f3, f2))),
+    )
+    acc[...] = jnp.zeros_like(acc)
+    writes = []
     for n, (even, odd) in enumerate(rows):
-        loads[n].wait()
-        i = on_parity(scalars, even, odd, (1,), b_refs, acc.at[n])
-        writes.append(write_row(o_s.at[n], acc.at[n], out, i, sem.at[3 + n]))
+        i = on_parity(scalars, even, odd, (0, 1), b_refs, acc.at[n])
+        writes.append(write_row(o_s.at[n], acc.at[n], out, i, sem.at[n]))
     for c in writes:
         c.wait()
 
@@ -230,30 +216,20 @@
     near = (own, ahead[1], back[1], ahead[2], back[2])
     block = (NB, BS, BS)
     shape = jax.ShapeDtypeStruct((MB, BS, NB * BS), jnp.bfloat16)
-    part = call(
-        first_section,
-        scalars,
-        near + (b_here,),
-        (),
-        jax.ShapeDtypeStruct((2,) + block, jnp.float32),
-        [pltpu.VMEM((2,) + block, jnp.float32), pltpu.SemaphoreType.DMA((2,))],
-        6,
-    )
-    part, ahead[3], back[3] = lax.optimization_barrier((part, ahead[3], back[3]))
-    f4 = lax.ppermute(ahead[3][:, : SPAN // 2], "z", z_route(1))
-    b4 = lax.ppermute(back[3][:, SPAN // 2 :], "z", z_route(-1))
+    f4 = lax.ppermute(ahead[2][:, : SPAN // 2], "z", z_route(2))
+    b4 = lax.ppermute(back[2][:, SPAN // 2 :], "z", z_route(-2))
     window = call(
         three_rows,
         scalars,
         near + (ahead[3], back[3], b_here, b_in, b_over),
-        (part,),
+        (),
         shape,
         [
             pltpu.VMEM((3,) + block, jnp.float32),
             pltpu.VMEM((3, BS, NB * BS), jnp.bfloat16),
-            pltpu.SemaphoreType.DMA((5,)),
+            pltpu.SemaphoreType.DMA((3,)),
         ],
-        12,
+        18,
     )
     window = call(
         last_row,

time: 126 us -> 125 us (level)
  Pallas kernels: 11.4 us -> 9.73 us
    pallas_call x3 -> x2, Pallas kernels: 9.14 us -> 7.44 us  [call(): pl.pallas_call(kernel, out_shape=out_shape, grid_spec=pltpu.PrefetchScala...]
  transfers between devices with their start and end apart: 12 -> 12, of which waited for: 8 -> 7; matrix products, arithmetic and copies ran while one was open for 1% -> 1% of each run, Pallas kernels for 5% -> 4%
where the time goes in v8:
time: 125 us
  waiting for transfers between devices  50.4 us (40%)
  starting transfers between devices  43.4 us (35%)
  blocking collectives  15 us (12%)
  Pallas kernels  9.73 us (8%)
  between operations  3.94 us (3%)
  local copies, waits for them, and re-layouts  1.98 us (2%)
    all_to_all x1, waiting for transfers between devices, on_device(): lax.all_to_all(payload(a_columns[0].transpose(2, 0, 1), a_live[0], tile),...  28.5 us
    all_gather x1, blocking collectives, on_device(): own = lax.all_gather(two[:, :PIECE], 'y_lo', axis=1, tiled=True)  15 us
    all_to_all x1, starting transfers between devices, on_device(): lax.all_to_all(payload(a_columns[0].transpose(2, 0, 1), a_live[0], tile),...  14 us
    ppermute x3, waiting for transfers between devices, on_device(): back.append(lax.ppermute(back[-1], 'z', z_route(-1)))  11.6 us
    ppermute x3, starting transfers between devices, on_device(): back.append(lax.ppermute(back[-1], 'z', z_route(-1)))  9.54 us
    ppermute x3, starting transfers between devices, on_device(): ahead.append(lax.ppermute(ahead[-1], 'z', z_route(1)))  7.66 us
    pallas_call x2, Pallas kernels, call(): pl.pallas_call(kernel, out_shape=out_shape, grid_spec=pltpu.PrefetchScala...  7.44 us
    ppermute x3, waiting for transfers between devices, on_device(): ahead.append(lax.ppermute(ahead[-1], 'z', z_route(1)))  5.34 us
  transfers between devices with their start and end apart: 12, of which 7 were waited for; matrix products, arithmetic and copies ran while one was open for 1% of the time, Pallas kernels for 4%

profile of v8, /device:TPU:6, one launch (start us, length us, event | category | flops | bytes accessed | tf_op | source)
XLA Modules:
  0.0 124.5 jit_solution(8695095856745769280)
XLA Ops:
  0.0 2.3 %shard_map.64 = bf16[32,104,256]{2,1,0:T(8,128)(2,1)} custom-call(s32[3,1,4]{2,1,0:T(1,128)} %bitcast.29, s32[1,4]{1,0:T(1,128)} %bitcast.31, bf16[32,96,256]{2,1,0:T(8,128)(2,1)} %bitcast.28), custom_call_target="tpu_custom_call" | custom-call | tf_op jit(solution)/shard_map/pallas_call | solution.py:175
  2.3 0.0 copy-start
  2.3 0.0 copy-start.1
  2.3 0.0 copy-start.2
  2.3 14.0 %all-to-all-start = ((bf16[32,104,256]{2,1,0:T(8,128)(2,1)}), bf16[32,104,256]{2,1,0:T(8,128)(2,1)}, u32[]{:S(2)}, u32[]{:S(2)}) async-start(bf16[32,104,256]{2,1,0:T(8,128)(2,1)} %shard_map.64), calls=%async_computation | async-start | bytes 3407872 | tf_op jit(solution)/shard_map/all_to_all | solution.py:194
  16.3 0.0 copy-done
  16.4 1.9 %collective-permute-start.1 = (bf16[4,256,512]{2,1,0:T(8,128)(2,1)S(1)}, bf16[4,256,512]{2,1,0:T(8,128)(2,1)S(1)}, u32[]{:S(2)}, u32[]{:S(2)}) collective-permute-start(bf16[4,256,512]{2,1,0:T(8,128)(2,1)S(1)} %bitcast.24), channel_id=1, source_target_pairs={{1,0},{2,1},{3,2},{4,3},{5,4},{6,5},{7,6},{9,8},{10,9},{11,10},{12... | collective-permute-start | bytes 3145736 | tf_op jit(solution)/shard_map/ppermute | solution.py:202
  18.3 0.0 copy-done.1
  18.3 2.8 %collective-permute-start = (s32[4,2]{0,1:T(2,128)S(1)}, s32[4,2]{0,1:T(2,128)S(1)}, u32[]{:S(2)}, u32[]{:S(2)}) collective-permute-start(s32[4,2]{0,1:T(2,128)S(1)} %bitcast.30), channel_id=1, source_target_pairs={{1,0},{2,1},{3,2},{4,3},{5,4},{6,5},{7,6},{8,7},{9,8},{10,9},{11,1... | collective-permute-start | bytes 104 | tf_op jit(solution)/shard_map/ppermute | solution.py:198
  21.1 0.0 copy-done.2
  21.2 0.6 fusion.5
  24.3 0.1 copy.10
  24.4 0.1 reshape_squeeze.3.refs_2_
  25.7 4.9 %collective-permute-done = s32[4,2]{0,1:T(2,128)S(1)} collective-permute-done((s32[4,2]{0,1:T(2,128)S(1)}, s32[4,2]{0,1:T(2,128)S(1)}, u32[]{:S(2)}, u32[]{:S(2)}) %collective-permute-start) | collective-permute-done | bytes 64 | tf_op jit(solution)/shard_map/ppermute | solution.py:198
  30.6 0.1 copy.11
  30.7 0.1 reshape.11.refs_3_
  30.8 0.0 collective-permute-done.1.refs_12_.refs_9_
  30.8 28.5 %all-to-all-done = bf16[32,104,256]{2,1,0:T(8,128)(2,1)} async-done(((bf16[32,104,256]{2,1,0:T(8,128)(2,1)}), bf16[32,104,256]{2,1,0:T(8,128)(2,1)}, u32[]{:S(2)}, u32[]{:S(2)}) %all-to-all-start) | async-done | bytes 1703968 | tf_op jit(solution)/shard_map/all_to_all | solution.py:194
  59.3 0.8 constant_dynamic-slice_fusion
  60.2 0.1 reshape.12.refs_1_
  60.3 15.0 %all_gather.3.refs_4_ = bf16[2,384,256]{2,1,0:T(8,128)(2,1)S(1)} all-gather(bf16[2,96,256]{2,1,0:T(8,128)(2,1)S(1)} %fusion), channel_id=1, replica_groups=mesh['y_lo'=4,'z'=8,'y_hi'=2,'x'=4,'core'=2] {'y_lo'}, dimensions={1}, use_global_device_ids=true | all-gather | bytes 491520 | tf_op jit(solution)/shard_map/all_gather | solution.py:207
  75.3 3.2 %collective-permute-start.5 = (bf16[2,384,256]{2,1,0:T(8,128)(2,1)S(1)}, bf16[2,384,256]{2,1,0:T(8,128)(2,1)S(1)}, u32[]{:S(2)}, u32[]{:S(2)}) collective-permute-start(bf16[2,384,256]{2,1,0:T(8,128)(2,1)S(1)} %all_gather.3.refs_4_), channel_id=1, source_target_pairs={{0,112},{16,0},{32,16},{48,32},{64,48},{80,64},{96,80},{112,96},{1... | collective-permute-start | bytes 1179656 | tf_op jit(solution)/shard_map/ppermute | solution.py:214
  78.5 2.6 %collective-permute-start.2 = (bf16[2,384,256]{2,1,0:T(8,128)(2,1)S(1)}, bf16[2,384,256]{2,1,0:T(8,128)(2,1)S(1)}, u32[]{:S(2)}, u32[]{:S(2)}) collective-permute-start(bf16[2,384,256]{2,1,0:T(8,128)(2,1)S(1)} %all_gather.3.refs_4_), channel_id=1, source_target_pairs={{0,16},{16,32},{32,48},{48,64},{64,80},{80,96},{96,112},{112,0},{1... | collective-permute-start | bytes 1179656 | tf_op jit(solution)/shard_map/ppermute | solution.py:213
  81.1 0.7 collective-permute-start.10
  81.9 4.1 %collective-permute-done.5.refs_6_ = bf16[2,384,256]{2,1,0:T(8,128)(2,1)S(1)} collective-permute-done((bf16[2,384,256]{2,1,0:T(8,128)(2,1)S(1)}, bf16[2,384,256]{2,1,0:T(8,128)(2,1)S(1)}, u32[]{:S(2)}, u32[]{:S(2)}) %collective-permute-start.5) | collective-permute-done | bytes 393248 | tf_op jit(solution)/shard_map/ppermute | solution.py:214
  86.0 3.4 %collective-permute-start.6 = (bf16[2,384,256]{2,1,0:T(8,128)(2,1)S(1)}, bf16[2,384,256]{2,1,0:T(8,128)(2,1)S(1)}, u32[]{:S(2)}, u32[]{:S(2)}) collective-permute-start(bf16[2,384,256]{2,1,0:T(8,128)(2,1)S(1)} %collective-permute-done.5.refs_6_), channel_id=1, source_target_pairs={{0,112},{16,0},{32,16},{48,32},{64,48},{80,64},{96,80},{112,96},{1... | collective-permute-start | bytes 1179656 | tf_op jit(solution)/shard_map/ppermute | solution.py:214
  89.4 0.0 collective-permute-done.2.refs_5_
  89.4 2.4 %collective-permute-start.3 = (bf16[2,384,256]{2,1,0:T(8,128)(2,1)S(1)}, bf16[2,384,256]{2,1,0:T(8,128)(2,1)S(1)}, u32[]{:S(2)}, u32[]{:S(2)}) collective-permute-start(bf16[2,384,256]{2,1,0:T(8,128)(2,1)S(1)} %collective-permute-done.2.refs_5_), channel_id=1, source_target_pairs={{0,16},{16,32},{32,48},{48,64},{64,80},{80,96},{96,112},{112,0},{1... | collective-permute-start | bytes 1179656 | tf_op jit(solution)/shard_map/ppermute | solution.py:213
  91.8 5.6 %collective-permute-done.6.refs_8_ = bf16[2,384,256]{2,1,0:T(8,128)(2,1)S(1)} collective-permute-done((bf16[2,384,256]{2,1,0:T(8,128)(2,1)S(1)}, bf16[2,384,256]{2,1,0:T(8,128)(2,1)S(1)}, u32[]{:S(2)}, u32[]{:S(2)}) %collective-permute-start.6) | collective-permute-done | bytes 393248 | tf_op jit(solution)/shard_map/ppermute | solution.py:214
  97.4 2.9 %collective-permute-start.7 = (bf16[2,384,256]{2,1,0:T(8,128)(2,1)S(1)}, bf16[2,384,256]{2,1,0:T(8,128)(2,1)S(1)}, u32[]{:S(2)}, u32[]{:S(2)}) collective-permute-start(bf16[2,384,256]{2,1,0:T(8,128)(2,1)S(1)} %collective-permute-done.6.refs_8_), channel_id=1, source_target_pairs={{0,112},{16,0},{32,16},{48,32},{64,48},{80,64},{96,80},{112,96},{1... | collective-permute-start | bytes 1179656 | tf_op jit(solution)/shard_map/ppermute | solution.py:214
  100.3 0.3 collective-permute-done.3.refs_7_
  100.7 2.6 %collective-permute-start.4 = (bf16[2,384,256]{2,1,0:T(8,128)(2,1)S(1)}, bf16[2,384,256]{2,1,0:T(8,128)(2,1)S(1)}, u32[]{:S(2)}, u32[]{:S(2)}) collective-permute-start(bf16[2,384,256]{2,1,0:T(8,128)(2,1)S(1)} %collective-permute-done.3.refs_7_), channel_id=1, source_target_pairs={{0,16},{16,32},{32,48},{48,64},{64,80},{80,96},{96,112},{112,0},{1... | collective-permute-start | bytes 1179656 | tf_op jit(solution)/shard_map/ppermute | solution.py:213
  103.3 2.4 %collective-permute-start.9 = (bf16[2,192,256]{2,1,0:T(8,128)(2,1)S(1)}, bf16[2,192,256]{2,1,0:T(8,128)(2,1)S(1)}, u32[]{:S(2)}, u32[]{:S(2)}) collective-permute-start(bf16[2,192,256]{2,1,0:T(8,128)(2,1)S(1)} %slice.27), channel_id=1, source_target_pairs={{0,96},{16,112},{32,0},{48,16},{64,32},{80,48},{96,64},{112,80},{1... | collective-permute-start | bytes 589832 | tf_op jit(solution)/shard_map/ppermute | solution.py:220
  105.7 4.4 %collective-permute-start.8 = (bf16[2,192,256]{2,1,0:T(8,128)(2,1)S(1)}, bf16[2,192,256]{2,1,0:T(8,128)(2,1)S(1)}, u32[]{:S(2)}, u32[]{:S(2)}) collective-permute-start(bf16[2,192,256]{2,1,0:T(8,128)(2,1)S(1)} %slice.26), channel_id=1, source_target_pairs={{0,32},{16,48},{32,64},{48,80},{64,96},{80,112},{96,0},{112,16},{1... | collective-permute-start | bytes 589832 | tf_op jit(solution)/shard_map/ppermute | solution.py:219
  110.1 0.0 collective-permute-done.10.refs_13_.refs_10_
  110.1 1.9 %collective-permute-done.7.refs_10_.refs_5_ = bf16[2,384,256]{2,1,0:T(8,128)(2,1)S(1)} collective-permute-done((bf16[2,384,256]{2,1,0:T(8,128)(2,1)S(1)}, bf16[2,384,256]{2,1,0:T(8,128)(2,1)S(1)}, u32[]{:S(2)}, u32[]{:S(2)}) %collective-permute-start.7) | collective-permute-done | bytes 393248 | tf_op jit(solution)/shard_map/ppermute | solution.py:214
  112.0 5.0 %collective-permute-done.4.refs_9_.refs_4_ = bf16[2,384,256]{2,1,0:T(8,128)(2,1)S(1)} collective-permute-done((bf16[2,384,256]{2,1,0:T(8,128)(2,1)S(1)}, bf16[2,384,256]{2,1,0:T(8,128)(2,1)S(1)}, u32[]{:S(2)}, u32[]{:S(2)}) %collective-permute-start.4) | collective-permute-done | bytes 393248 | tf_op jit(solution)/shard_map/ppermute | solution.py:213
  117.0 5.4 %shard_map.65.refs_11_ = bf16[4,256,1024]{2,1,0:T(8,128)(2,1)} custom-call(s32[1]{0:T(128)} %bitcast.5.refs_0_, s32[32]{0:T(128)S(1)} %reshape.12.refs_1_, s32[8]{0:T(128)S(1)} %reshape_squeeze.3.refs_2_, s32[8]{0:T(128)S(1)} %reshape.11.refs_3_, bf16[2,384,256]{2,1,0:T(8,128)(2,1)S(1)} %all_gather.3.refs_4_, ...), custom_call_target="tpu_custom_call" | custom-call | flops 1207959552 | bytes 1048576 | tf_op jit(solution)/shard_map/pallas_call | solution.py:125
  122.4 0.0 collective-permute-done.9.refs_7_
  122.5 0.0 collective-permute-done.8.refs_6_
  122.5 2.0 %shard_map.66 = bf16[4,256,1024]{2,1,0:T(8,128)(2,1)} custom-call(s32[1]{0:T(128)} %bitcast.5.refs_0_, s32[32]{0:T(128)S(1)} %reshape.12.refs_1_, s32[8]{0:T(128)S(1)} %reshape_squeeze.3.refs_2_, s32[8]{0:T(128)S(1)} %reshape.11.refs_3_, bf16[2,384,256]{2,1,0:T(8,128)(2,1)S(1)} %collective-permute-done.4.refs_9_.refs_4_, ...), custom_call_target="tpu_custom_call", output_to_operand_aliasing={{}: (11, {})} | custom-call | flops 402653184 | bytes 1048576 | tf_op jit(solution)/shard_map/pallas_call | solution.py:125
  (5 shorter events, 0.1 us)
Async XLA Ops:
  2.3 14.0 %copy-start = (bf16[1,1,4,256,512]{4,3,2,1,0:T(8,128)(2,1)S(1)}, bf16[1,1,4,256,512]{4,3,2,1,0:T(8,128)(2,1)}, u32[]{:S(2)}) copy-start(bf16[1,1,4,256,512]{4,3,2,1,0:T(8,128)(2,1)} %param.10) | copy-start | bytes 3145732
  2.3 16.0 %copy-start.1 = (s32[1,1,4,2]{2,3,1,0:T(2,128)S(1)}, s32[1,1,4,2]{2,3,1,0:T(2,128)}, u32[]{:S(2)}) copy-start(s32[1,1,4,2]{2,3,1,0:T(2,128)} %param.11) | copy-start | bytes 100
  2.3 18.8 %copy-start.2 = (s32[1,2]{1,0:T(1,128)S(1)}, s32[1,2]{1,0:T(1,128)}, u32[]{:S(2)}) copy-start(s32[1,2]{1,0:T(1,128)} %param.9) | copy-start | bytes 28
  2.3 57.0 %all-to-all-start = ((bf16[32,104,256]{2,1,0:T(8,128)(2,1)}), bf16[32,104,256]{2,1,0:T(8,128)(2,1)}, u32[]{:S(2)}, u32[]{:S(2)}) async-start(bf16[32,104,256]{2,1,0:T(8,128)(2,1)} %shard_map.64), calls=%async_computation | async-start | bytes 3407872 | tf_op jit(solution)/shard_map/all_to_all | solution.py:194
  16.4 14.4 %collective-permute-start.1 = (bf16[4,256,512]{2,1,0:T(8,128)(2,1)S(1)}, bf16[4,256,512]{2,1,0:T(8,128)(2,1)S(1)}, u32[]{:S(2)}, u32[]{:S(2)}) collective-permute-start(bf16[4,256,512]{2,1,0:T(8,128)(2,1)S(1)} %bitcast.24), channel_id=1, source_target_pairs={{1,0},{2,1},{3,2},{4,3},{5,4},{6,5},{7,6},{9,8},{10,9},{11,10},{12... | collective-permute-start | bytes 3145736 | tf_op jit(solution)/shard_map/ppermute | solution.py:202
  18.3 12.3 %collective-permute-start = (s32[4,2]{0,1:T(2,128)S(1)}, s32[4,2]{0,1:T(2,128)S(1)}, u32[]{:S(2)}, u32[]{:S(2)}) collective-permute-start(s32[4,2]{0,1:T(2,128)S(1)} %bitcast.30), channel_id=1, source_target_pairs={{1,0},{2,1},{3,2},{4,3},{5,4},{6,5},{7,6},{8,7},{9,8},{10,9},{11,1... | collective-permute-start | bytes 104 | tf_op jit(solution)/shard_map/ppermute | solution.py:198
  75.3 10.7 %collective-permute-start.5 = (bf16[2,384,256]{2,1,0:T(8,128)(2,1)S(1)}, bf16[2,384,256]{2,1,0:T(8,128)(2,1)S(1)}, u32[]{:S(2)}, u32[]{:S(2)}) collective-permute-start(bf16[2,384,256]{2,1,0:T(8,128)(2,1)S(1)} %all_gather.3.refs_4_), channel_id=1, source_target_pairs={{0,112},{16,0},{32,16},{48,32},{64,48},{80,64},{96,80},{112,96},{1... | collective-permute-start | bytes 1179656 | tf_op jit(solution)/shard_map/ppermute | solution.py:214
  78.5 10.9 %collective-permute-start.2 = (bf16[2,384,256]{2,1,0:T(8,128)(2,1)S(1)}, bf16[2,384,256]{2,1,0:T(8,128)(2,1)S(1)}, u32[]{:S(2)}, u32[]{:S(2)}) collective-permute-start(bf16[2,384,256]{2,1,0:T(8,128)(2,1)S(1)} %all_gather.3.refs_4_), channel_id=1, source_target_pairs={{0,16},{16,32},{32,48},{48,64},{64,80},{80,96},{96,112},{112,0},{1... | collective-permute-start | bytes 1179656 | tf_op jit(solution)/shard_map/ppermute | solution.py:213
  81.1 29.0 %collective-permute-start.10 = (bf16[4,256,512]{2,1,0:T(8,128)(2,1)S(1)}, bf16[4,256,512]{2,1,0:T(8,128)(2,1)S(1)}, u32[]{:S(2)}, u32[]{:S(2)}) collective-permute-start(bf16[4,256,512]{2,1,0:T(8,128)(2,1)S(1)} %bitcast.25), channel_id=1, source_target_pairs={{8,7},{0,15},{24,23},{16,31},{40,39},{32,47},{56,55},{48,63},{72,7... | collective-permute-start | bytes 3145736 | tf_op jit(solution)/shard_map/ppermute | solution.py:209
  86.0 11.5 %collective-permute-start.6 = (bf16[2,384,256]{2,1,0:T(8,128)(2,1)S(1)}, bf16[2,384,256]{2,1,0:T(8,128)(2,1)S(1)}, u32[]{:S(2)}, u32[]{:S(2)}) collective-permute-start(bf16[2,384,256]{2,1,0:T(8,128)(2,1)S(1)} %collective-permute-done.5.refs_6_), channel_id=1, source_target_pairs={{0,112},{16,0},{32,16},{48,32},{64,48},{80,64},{96,80},{112,96},{1... | collective-permute-start | bytes 1179656 | tf_op jit(solution)/shard_map/ppermute | solution.py:214
  89.4 11.3 %collective-permute-start.3 = (bf16[2,384,256]{2,1,0:T(8,128)(2,1)S(1)}, bf16[2,384,256]{2,1,0:T(8,128)(2,1)S(1)}, u32[]{:S(2)}, u32[]{:S(2)}) collective-permute-start(bf16[2,384,256]{2,1,0:T(8,128)(2,1)S(1)} %collective-permute-done.2.refs_5_), channel_id=1, source_target_pairs={{0,16},{16,32},{32,48},{48,64},{64,80},{80,96},{96,112},{112,0},{1... | collective-permute-start | bytes 1179656 | tf_op jit(solution)/shard_map/ppermute | solution.py:213
  97.4 14.6 %collective-permute-start.7 = (bf16[2,384,256]{2,1,0:T(8,128)(2,1)S(1)}, bf16[2,384,256]{2,1,0:T(8,128)(2,1)S(1)}, u32[]{:S(2)}, u32[]{:S(2)}) collective-permute-start(bf16[2,384,256]{2,1,0:T(8,128)(2,1)S(1)} %collective-permute-done.6.refs_8_), channel_id=1, source_target_pairs={{0,112},{16,0},{32,16},{48,32},{64,48},{80,64},{96,80},{112,96},{1... | collective-permute-start | bytes 1179656 | tf_op jit(solution)/shard_map/ppermute | solution.py:214
  100.7 16.4 %collective-permute-start.4 = (bf16[2,384,256]{2,1,0:T(8,128)(2,1)S(1)}, bf16[2,384,256]{2,1,0:T(8,128)(2,1)S(1)}, u32[]{:S(2)}, u32[]{:S(2)}) collective-permute-start(bf16[2,384,256]{2,1,0:T(8,128)(2,1)S(1)} %collective-permute-done.3.refs_7_), channel_id=1, source_target_pairs={{0,16},{16,32},{32,48},{48,64},{64,80},{80,96},{96,112},{112,0},{1... | collective-permute-start | bytes 1179656 | tf_op jit(solution)/shard_map/ppermute | solution.py:213
  103.3 19.1 %collective-permute-start.9 = (bf16[2,192,256]{2,1,0:T(8,128)(2,1)S(1)}, bf16[2,192,256]{2,1,0:T(8,128)(2,1)S(1)}, u32[]{:S(2)}, u32[]{:S(2)}) collective-permute-start(bf16[2,192,256]{2,1,0:T(8,128)(2,1)S(1)} %slice.27), channel_id=1, source_target_pairs={{0,96},{16,112},{32,0},{48,16},{64,32},{80,48},{96,64},{112,80},{1... | collective-permute-start | bytes 589832 | tf_op jit(solution)/shard_map/ppermute | solution.py:220
  105.7 16.8 %collective-permute-start.8 = (bf16[2,192,256]{2,1,0:T(8,128)(2,1)S(1)}, bf16[2,192,256]{2,1,0:T(8,128)(2,1)S(1)}, u32[]{:S(2)}, u32[]{:S(2)}) collective-permute-start(bf16[2,192,256]{2,1,0:T(8,128)(2,1)S(1)} %slice.26), channel_id=1, source_target_pairs={{0,32},{16,48},{32,64},{48,80},{64,96},{80,112},{96,0},{112,16},{1... | collective-permute-start | bytes 589832 | tf_op jit(solution)/shard_map/ppermute | solution.py:219

commit v9 on v8

--- a/solution.py
+++ b/solution.py
@@ -93,22 +93,25 @@
     return copy
 
 
-def three_rows(*refs):
+def two_rows(*refs):
     scalars = refs[:4]
-    own, f1, b1, f2, b2, f3, b3, b_here, b_in, b_over, out, acc, o_s, sem = refs[4:]
-    b_refs = (b_here, (b_in, b_over))
-    rows = (
-        ((0, (own, b1)), (-1, (f1, own))),
-        ((-2, (f2, f1)), (1, (b1, b2))),
-        ((2, (b2, b3)), (-3, (f3, f2))),
-    )
+    own, f1, b1, f2, b2, b_here, b_in, b_over, out, acc, o_s, sem = refs[4:]
+    rows = (((0, (own, b1)), (-1, (f1, own))), ((-2, (f2, f1)), (1, (b1, b2))))
     acc[...] = jnp.zeros_like(acc)
     writes = []
     for n, (even, odd) in enumerate(rows):
-        i = on_parity(scalars, even, odd, (0, 1), b_refs, acc.at[n])
+        i = on_parity(scalars, even, odd, (0, 1), (b_here, (b_in, b_over)), acc.at[n])
         writes.append(write_row(o_s.at[n], acc.at[n], out, i, sem.at[n]))
     for c in writes:
         c.wait()
+
+
+def third_row(*refs):
+    scalars = refs[:4]
+    f2, b2, f3, b3, b_here, b_in, b_over, before, out, acc, o_s, sem = refs[4:]
+    acc[...] = jnp.zeros_like(acc)
+    i = on_parity(scalars, (2, (b2, b3)), (-3, (f3, f2)), (0, 1), (b_here, (b_in, b_over)), acc)
+    write_row(o_s, acc, out, i, sem.at[0]).wait()
 
 
 def last_row(*refs):
@@ -218,29 +221,12 @@
     shape = jax.ShapeDtypeStruct((MB, BS, NB * BS), jnp.bfloat16)
     f4 = lax.ppermute(ahead[2][:, : SPAN // 2], "z", z_route(2))
     b4 = lax.ppermute(back[2][:, SPAN // 2 :], "z", z_route(-2))
-    window = call(
-        three_rows,
-        scalars,
-        near + (ahead[3], back[3], b_here, b_in, b_over),
-        (),
-        shape,
-        [
-            pltpu.VMEM((3,) + block, jnp.float32),
-            pltpu.VMEM((3, BS, NB * BS), jnp.bfloat16),
-            pltpu.SemaphoreType.DMA((3,)),
-        ],
-        18,
-    )
-    window = call(
-        last_row,
-        scalars,
-        (ahead[3], back[3], f4, b4, b_here, b_in, b_over),
-        (window,),
-        shape,
-        [pltpu.VMEM(block, jnp.float32), pltpu.VMEM((BS, NB * BS), jnp.bfloat16), pltpu.SemaphoreType.DMA((1,))],
-        6,
-        alias=True,
-    )
+    b_all = (b_here, b_in, b_over)
+    wide = [pltpu.VMEM((2,) + block, jnp.float32), pltpu.VMEM((2, BS, NB * BS), jnp.bfloat16), pltpu.SemaphoreType.DMA((2,))]
+    slim = [pltpu.VMEM(block, jnp.float32), pltpu.VMEM((BS, NB * BS), jnp.bfloat16), pltpu.SemaphoreType.DMA((1,))]
+    window = call(two_rows, scalars, near + b_all, (), shape, wide, 12)
+    window = call(third_row, scalars, near[3:] + (ahead[3], back[3]) + b_all, (window,), shape, slim, 6, alias=True)
+    window = call(last_row, scalars, (ahead[3], back[3], f4, b4) + b_all, (window,), shape, slim, 6, alias=True)
     return window[None, None]
 
 

time: 125 us -> 125 us (level)
  waiting for transfers between devices: 50.4 us -> 42.4 us
  starting transfers between devices: 43.4 us -> 49.3 us
  Pallas kernels: 9.73 us -> 12.1 us
    ppermute x3, waiting for transfers between devices: 11.6 us -> 0.09 us  [on_device(): back.append(lax.ppermute(back[-1], 'z', z_route(-1)))]
    ppermute x3, starting transfers between devices: 9.54 us -> 15.5 us  [on_device(): back.append(lax.ppermute(back[-1], 'z', z_route(-1)))]
    ppermute x1, starting transfers between devices: 2.37 us -> 6.03 us  [on_device(): b4 = lax.ppermute(back[2][:, SPAN // 2:], 'z', z_route(-2))]
    ppermute x3, waiting for transfers between devices: 5.34 us -> 8.84 us  [on_device(): ahead.append(lax.ppermute(ahead[-1], 'z', z_route(1)))]
    ppermute x1, starting transfers between devices: 4.37 us -> 1.92 us  [on_device(): f4 = lax.ppermute(ahead[2][:, :SPAN // 2], 'z', z_route(2))]
    pallas_call x2 -> x3, Pallas kernels: 7.44 us -> 9.8 us  [call(): pl.pallas_call(kernel, out_shape=out_shape, grid_spec=pltpu.PrefetchScala...]
    ppermute x3, starting transfers between devices: 7.66 us -> 6.35 us  [on_device(): ahead.append(lax.ppermute(ahead[-1], 'z', z_route(1)))]
  transfers between devices with their start and end apart: 12 -> 12, of which waited for: 7 -> 5; matrix products, arithmetic and copies ran while one was open for 1% -> 1% of each run, Pallas kernels for 4% -> 5%
where the time goes in v9:
time: 125 us
  starting transfers between devices  49.3 us (39%)
  waiting for transfers between devices  42.4 us (34%)
  blocking collectives  15 us (12%)
  Pallas kernels  12.1 us (10%)
  between operations  3.96 us (3%)
  local copies, waits for them, and re-layouts  1.98 us (2%)
    all_to_all x1, waiting for transfers between devices, on_device(): lax.all_to_all(payload(a_columns[0].transpose(2, 0, 1), a_live[0], tile),...  28.5 us
    ppermute x3, starting transfers between devices, on_device(): back.append(lax.ppermute(back[-1], 'z', z_route(-1)))  15.5 us
    all_gather x1, blocking collectives, on_device(): own = lax.all_gather(two[:, :PIECE], 'y_lo', axis=1, tiled=True)  15 us
    all_to_all x1, starting transfers between devices, on_device(): lax.all_to_all(payload(a_columns[0].transpose(2, 0, 1), a_live[0], tile),...  14 us
    pallas_call x3, Pallas kernels, call(): pl.pallas_call(kernel, out_shape=out_shape, grid_spec=pltpu.PrefetchScala...  9.8 us
    ppermute x3, waiting for transfers between devices, on_device(): ahead.append(lax.ppermute(ahead[-1], 'z', z_route(1)))  8.84 us
    ppermute x3, starting transfers between devices, on_device(): ahead.append(lax.ppermute(ahead[-1], 'z', z_route(1)))  6.35 us
    ppermute x1, starting transfers between devices, on_device(): b4 = lax.ppermute(back[2][:, SPAN // 2:], 'z', z_route(-2))  6.03 us
  transfers between devices with their start and end apart: 12, of which 5 were waited for; matrix products, arithmetic and copies ran while one was open for 1% of the time, Pallas kernels for 5%

profile of v9, /device:TPU:6, one launch (start us, length us, event | category | flops | bytes accessed | tf_op | source)
XLA Modules:
  0.0 124.7 jit_solution(3791010677324182829)
XLA Ops:
  0.0 2.3 %shard_map.64 = bf16[32,104,256]{2,1,0:T(8,128)(2,1)} custom-call(s32[3,1,4]{2,1,0:T(1,128)} %bitcast.30, s32[1,4]{1,0:T(1,128)} %bitcast.32, bf16[32,96,256]{2,1,0:T(8,128)(2,1)} %bitcast.29), custom_call_target="tpu_custom_call" | custom-call | tf_op jit(solution)/shard_map/pallas_call | solution.py:178
  2.3 0.0 copy-start
  2.3 0.0 copy-start.1
  2.3 0.0 copy-start.2
  2.3 14.0 %all-to-all-start = ((bf16[32,104,256]{2,1,0:T(8,128)(2,1)}), bf16[32,104,256]{2,1,0:T(8,128)(2,1)}, u32[]{:S(2)}, u32[]{:S(2)}) async-start(bf16[32,104,256]{2,1,0:T(8,128)(2,1)} %shard_map.64), calls=%async_computation | async-start | bytes 3407872 | tf_op jit(solution)/shard_map/all_to_all | solution.py:197
  16.3 0.0 copy-done
  16.4 1.9 %collective-permute-start.1 = (bf16[4,256,512]{2,1,0:T(8,128)(2,1)S(1)}, bf16[4,256,512]{2,1,0:T(8,128)(2,1)S(1)}, u32[]{:S(2)}, u32[]{:S(2)}) collective-permute-start(bf16[4,256,512]{2,1,0:T(8,128)(2,1)S(1)} %bitcast.24), channel_id=1, source_target_pairs={{1,0},{2,1},{3,2},{4,3},{5,4},{6,5},{7,6},{9,8},{10,9},{11,10},{12... | collective-permute-start | bytes 3145736 | tf_op jit(solution)/shard_map/ppermute | solution.py:205
  18.3 0.0 copy-done.1
  18.3 2.8 %collective-permute-start = (s32[4,2]{0,1:T(2,128)S(1)}, s32[4,2]{0,1:T(2,128)S(1)}, u32[]{:S(2)}, u32[]{:S(2)}) collective-permute-start(s32[4,2]{0,1:T(2,128)S(1)} %bitcast.31), channel_id=1, source_target_pairs={{1,0},{2,1},{3,2},{4,3},{5,4},{6,5},{7,6},{8,7},{9,8},{10,9},{11,1... | collective-permute-start | bytes 104 | tf_op jit(solution)/shard_map/ppermute | solution.py:201
  21.1 0.0 copy-done.2
  21.2 0.6 fusion.5
  24.3 0.1 copy.11
  24.4 0.1 reshape_squeeze.3.refs_2_
  25.7 4.9 %collective-permute-done = s32[4,2]{0,1:T(2,128)S(1)} collective-permute-done((s32[4,2]{0,1:T(2,128)S(1)}, s32[4,2]{0,1:T(2,128)S(1)}, u32[]{:S(2)}, u32[]{:S(2)}) %collective-permute-start) | collective-permute-done | bytes 64 | tf_op jit(solution)/shard_map/ppermute | solution.py:201
  30.6 0.1 copy.12
  30.7 0.1 reshape.11.refs_3_
  30.8 0.0 collective-permute-done.1.refs_10_.refs_9_
  30.8 28.5 %all-to-all-done = bf16[32,104,256]{2,1,0:T(8,128)(2,1)} async-done(((bf16[32,104,256]{2,1,0:T(8,128)(2,1)}), bf16[32,104,256]{2,1,0:T(8,128)(2,1)}, u32[]{:S(2)}, u32[]{:S(2)}) %all-to-all-start) | async-done | bytes 1703968 | tf_op jit(solution)/shard_map/all_to_all | solution.py:197
  59.3 0.8 constant_dynamic-slice_fusion
  60.2 0.1 reshape.12.refs_1_
  60.3 15.0 %all_gather.3.refs_4_ = bf16[2,384,256]{2,1,0:T(8,128)(2,1)S(1)} all-gather(bf16[2,96,256]{2,1,0:T(8,128)(2,1)S(1)} %fusion), channel_id=1, replica_groups=mesh['y_lo'=4,'z'=8,'y_hi'=2,'x'=4,'core'=2] {'y_lo'}, dimensions={1}, use_global_device_ids=true | all-gather | bytes 491520 | tf_op jit(solution)/shard_map/all_gather | solution.py:210
  75.3 2.5 %collective-permute-start.2 = (bf16[2,384,256]{2,1,0:T(8,128)(2,1)S(1)}, bf16[2,384,256]{2,1,0:T(8,128)(2,1)S(1)}, u32[]{:S(2)}, u32[]{:S(2)}) collective-permute-start(bf16[2,384,256]{2,1,0:T(8,128)(2,1)S(1)} %all_gather.3.refs_4_), channel_id=1, source_target_pairs={{0,16},{16,32},{32,48},{48,64},{64,80},{80,96},{96,112},{112,0},{1... | collective-permute-start | bytes 1179656 | tf_op jit(solution)/shard_map/ppermute | solution.py:216
  77.8 4.5 %collective-permute-start.5 = (bf16[2,384,256]{2,1,0:T(8,128)(2,1)S(1)}, bf16[2,384,256]{2,1,0:T(8,128)(2,1)S(1)}, u32[]{:S(2)}, u32[]{:S(2)}) collective-permute-start(bf16[2,384,256]{2,1,0:T(8,128)(2,1)S(1)} %all_gather.3.refs_4_), channel_id=1, source_target_pairs={{0,112},{16,0},{32,16},{48,32},{64,48},{80,64},{96,80},{112,96},{1... | collective-permute-start | bytes 1179656 | tf_op jit(solution)/shard_map/ppermute | solution.py:217
  82.3 0.7 collective-permute-start.10
  83.1 3.6 %collective-permute-done.2.refs_5_ = bf16[2,384,256]{2,1,0:T(8,128)(2,1)S(1)} collective-permute-done((bf16[2,384,256]{2,1,0:T(8,128)(2,1)S(1)}, bf16[2,384,256]{2,1,0:T(8,128)(2,1)S(1)}, u32[]{:S(2)}, u32[]{:S(2)}) %collective-permute-start.2) | collective-permute-done | bytes 393248 | tf_op jit(solution)/shard_map/ppermute | solution.py:216
  86.7 1.9 %collective-permute-start.3 = (bf16[2,384,256]{2,1,0:T(8,128)(2,1)S(1)}, bf16[2,384,256]{2,1,0:T(8,128)(2,1)S(1)}, u32[]{:S(2)}, u32[]{:S(2)}) collective-permute-start(bf16[2,384,256]{2,1,0:T(8,128)(2,1)S(1)} %collective-permute-done.2.refs_5_), channel_id=1, source_target_pairs={{0,16},{16,32},{32,48},{48,64},{64,80},{80,96},{96,112},{112,0},{1... | collective-permute-start | bytes 1179656 | tf_op jit(solution)/shard_map/ppermute | solution.py:216
  88.6 0.0 collective-permute-done.5.refs_6_
  88.7 5.4 %collective-permute-start.6 = (bf16[2,384,256]{2,1,0:T(8,128)(2,1)S(1)}, bf16[2,384,256]{2,1,0:T(8,128)(2,1)S(1)}, u32[]{:S(2)}, u32[]{:S(2)}) collective-permute-start(bf16[2,384,256]{2,1,0:T(8,128)(2,1)S(1)} %collective-permute-done.5.refs_6_), channel_id=1, source_target_pairs={{0,112},{16,0},{32,16},{48,32},{64,48},{80,64},{96,80},{112,96},{1... | collective-permute-start | bytes 1179656 | tf_op jit(solution)/shard_map/ppermute | solution.py:217
  94.1 5.2 %collective-permute-done.3.refs_7_.refs_4_ = bf16[2,384,256]{2,1,0:T(8,128)(2,1)S(1)} collective-permute-done((bf16[2,384,256]{2,1,0:T(8,128)(2,1)S(1)}, bf16[2,384,256]{2,1,0:T(8,128)(2,1)S(1)}, u32[]{:S(2)}, u32[]{:S(2)}) %collective-permute-start.3) | collective-permute-done | bytes 393248 | tf_op jit(solution)/shard_map/ppermute | solution.py:216
  99.2 1.9 %collective-permute-start.4 = (bf16[2,384,256]{2,1,0:T(8,128)(2,1)S(1)}, bf16[2,384,256]{2,1,0:T(8,128)(2,1)S(1)}, u32[]{:S(2)}, u32[]{:S(2)}) collective-permute-start(bf16[2,384,256]{2,1,0:T(8,128)(2,1)S(1)} %collective-permute-done.3.refs_7_.refs_4_), channel_id=1, source_target_pairs={{0,16},{16,32},{32,48},{48,64},{64,80},{80,96},{96,112},{112,0},{1... | collective-permute-start | bytes 1179656 | tf_op jit(solution)/shard_map/ppermute | solution.py:216
  101.2 0.1 collective-permute-done.6.refs_8_.refs_5_
  101.2 5.6 %collective-permute-start.7 = (bf16[2,384,256]{2,1,0:T(8,128)(2,1)S(1)}, bf16[2,384,256]{2,1,0:T(8,128)(2,1)S(1)}, u32[]{:S(2)}, u32[]{:S(2)}) collective-permute-start(bf16[2,384,256]{2,1,0:T(8,128)(2,1)S(1)} %collective-permute-done.6.refs_8_.refs_5_), channel_id=1, source_target_pairs={{0,112},{16,0},{32,16},{48,32},{64,48},{80,64},{96,80},{112,96},{1... | collective-permute-start | bytes 1179656 | tf_op jit(solution)/shard_map/ppermute | solution.py:217
  106.9 1.9 %collective-permute-start.8 = (bf16[2,192,256]{2,1,0:T(8,128)(2,1)S(1)}, bf16[2,192,256]{2,1,0:T(8,128)(2,1)S(1)}, u32[]{:S(2)}, u32[]{:S(2)}) collective-permute-start(bf16[2,192,256]{2,1,0:T(8,128)(2,1)S(1)} %slice.26), channel_id=1, source_target_pairs={{0,32},{16,48},{32,64},{48,80},{64,96},{80,112},{96,0},{112,16},{1... | collective-permute-start | bytes 589832 | tf_op jit(solution)/shard_map/ppermute | solution.py:222
  108.8 6.0 %collective-permute-start.9 = (bf16[2,192,256]{2,1,0:T(8,128)(2,1)S(1)}, bf16[2,192,256]{2,1,0:T(8,128)(2,1)S(1)}, u32[]{:S(2)}, u32[]{:S(2)}) collective-permute-start(bf16[2,192,256]{2,1,0:T(8,128)(2,1)S(1)} %slice.27), channel_id=1, source_target_pairs={{0,96},{16,112},{32,0},{48,16},{64,32},{80,48},{96,64},{112,80},{1... | collective-permute-start | bytes 589832 | tf_op jit(solution)/shard_map/ppermute | solution.py:223
  114.9 0.0 collective-permute-done.10.refs_11_.refs_10_
  114.9 4.2 %shard_map.65.refs_11_ = bf16[4,256,1024]{2,1,0:T(8,128)(2,1)} custom-call(s32[1]{0:T(128)} %bitcast.5.refs_0_, s32[32]{0:T(128)S(1)} %reshape.12.refs_1_, s32[8]{0:T(128)S(1)} %reshape_squeeze.3.refs_2_, s32[8]{0:T(128)S(1)} %reshape.11.refs_3_, bf16[2,384,256]{2,1,0:T(8,128)(2,1)S(1)} %all_gather.3.refs_4_, ...), custom_call_target="tpu_custom_call" | custom-call | flops 805306368 | bytes 1048576 | tf_op jit(solution)/shard_map/pallas_call | solution.py:128
  119.1 0.0 collective-permute-done.4.refs_6_.refs_4_
  119.1 0.0 collective-permute-done.7.refs_7_.refs_5_
  119.1 2.6 %shard_map.66.refs_11_ = bf16[4,256,1024]{2,1,0:T(8,128)(2,1)} custom-call(s32[1]{0:T(128)} %bitcast.5.refs_0_, s32[32]{0:T(128)S(1)} %reshape.12.refs_1_, s32[8]{0:T(128)S(1)} %reshape_squeeze.3.refs_2_, s32[8]{0:T(128)S(1)} %reshape.11.refs_3_, bf16[2,384,256]{2,1,0:T(8,128)(2,1)S(1)} %collective-permute-done.3.refs_7_.refs_4_, ...), custom_call_target="tpu_custom_call", output_to_operand_aliasing={{}: (11, {})} | custom-call | flops 402653184 | bytes 1048576 | tf_op jit(solution)/shard_map/pallas_call | solution.py:128
  121.7 0.0 collective-permute-done.8.refs_6_
  121.7 0.0 collective-permute-done.9.refs_7_
  121.7 3.0 %shard_map.67 = bf16[4,256,1024]{2,1,0:T(8,128)(2,1)} custom-call(s32[1]{0:T(128)} %bitcast.5.refs_0_, s32[32]{0:T(128)S(1)} %reshape.12.refs_1_, s32[8]{0:T(128)S(1)} %reshape_squeeze.3.refs_2_, s32[8]{0:T(128)S(1)} %reshape.11.refs_3_, bf16[2,384,256]{2,1,0:T(8,128)(2,1)S(1)} %collective-permute-done.4.refs_6_.refs_4_, ...), custom_call_target="tpu_custom_call", output_to_operand_aliasing={{}: (11, {})} | custom-call | flops 402653184 | bytes 1048576 | tf_op jit(solution)/shard_map/pallas_call | solution.py:128
  (5 shorter events, 0.1 us)
Async XLA Ops:
  2.3 14.0 %copy-start = (bf16[1,1,4,256,512]{4,3,2,1,0:T(8,128)(2,1)S(1)}, bf16[1,1,4,256,512]{4,3,2,1,0:T(8,128)(2,1)}, u32[]{:S(2)}) copy-start(bf16[1,1,4,256,512]{4,3,2,1,0:T(8,128)(2,1)} %param.10) | copy-start | bytes 3145732
  2.3 16.0 %copy-start.1 = (s32[1,1,4,2]{2,3,1,0:T(2,128)S(1)}, s32[1,1,4,2]{2,3,1,0:T(2,128)}, u32[]{:S(2)}) copy-start(s32[1,1,4,2]{2,3,1,0:T(2,128)} %param.11) | copy-start | bytes 100
  2.3 18.8 %copy-start.2 = (s32[1,2]{1,0:T(1,128)S(1)}, s32[1,2]{1,0:T(1,128)}, u32[]{:S(2)}) copy-start(s32[1,2]{1,0:T(1,128)} %param.9) | copy-start | bytes 28
  2.3 57.0 %all-to-all-start = ((bf16[32,104,256]{2,1,0:T(8,128)(2,1)}), bf16[32,104,256]{2,1,0:T(8,128)(2,1)}, u32[]{:S(2)}, u32[]{:S(2)}) async-start(bf16[32,104,256]{2,1,0:T(8,128)(2,1)} %shard_map.64), calls=%async_computation | async-start | bytes 3407872 | tf_op jit(solution)/shard_map/all_to_all | solution.py:197
  16.4 14.4 %collective-permute-start.1 = (bf16[4,256,512]{2,1,0:T(8,128)(2,1)S(1)}, bf16[4,256,512]{2,1,0:T(8,128)(2,1)S(1)}, u32[]{:S(2)}, u32[]{:S(2)}) collective-permute-start(bf16[4,256,512]{2,1,0:T(8,128)(2,1)S(1)} %bitcast.24), channel_id=1, source_target_pairs={{1,0},{2,1},{3,2},{4,3},{5,4},{6,5},{7,6},{9,8},{10,9},{11,10},{12... | collective-permute-start | bytes 3145736 | tf_op jit(solution)/shard_map/ppermute | solution.py:205
  18.3 12.3 %collective-permute-start = (s32[4,2]{0,1:T(2,128)S(1)}, s32[4,2]{0,1:T(2,128)S(1)}, u32[]{:S(2)}, u32[]{:S(2)}) collective-permute-start(s32[4,2]{0,1:T(2,128)S(1)} %bitcast.31), channel_id=1, source_target_pairs={{1,0},{2,1},{3,2},{4,3},{5,4},{6,5},{7,6},{8,7},{9,8},{10,9},{11,1... | collective-permute-start | bytes 104 | tf_op jit(solution)/shard_map/ppermute | solution.py:201
  75.3 11.4 %collective-permute-start.2 = (bf16[2,384,256]{2,1,0:T(8,128)(2,1)S(1)}, bf16[2,384,256]{2,1,0:T(8,128)(2,1)S(1)}, u32[]{:S(2)}, u32[]{:S(2)}) collective-permute-start(bf16[2,384,256]{2,1,0:T(8,128)(2,1)S(1)} %all_gather.3.refs_4_), channel_id=1, source_target_pairs={{0,16},{16,32},{32,48},{48,64},{64,80},{80,96},{96,112},{112,0},{1... | collective-permute-start | bytes 1179656 | tf_op jit(solution)/shard_map/ppermute | solution.py:216
  77.8 10.8 %collective-permute-start.5 = (bf16[2,384,256]{2,1,0:T(8,128)(2,1)S(1)}, bf16[2,384,256]{2,1,0:T(8,128)(2,1)S(1)}, u32[]{:S(2)}, u32[]{:S(2)}) collective-permute-start(bf16[2,384,256]{2,1,0:T(8,128)(2,1)S(1)} %all_gather.3.refs_4_), channel_id=1, source_target_pairs={{0,112},{16,0},{32,16},{48,32},{64,48},{80,64},{96,80},{112,96},{1... | collective-permute-start | bytes 1179656 | tf_op jit(solution)/shard_map/ppermute | solution.py:217
  82.3 32.5 %collective-permute-start.10 = (bf16[4,256,512]{2,1,0:T(8,128)(2,1)S(1)}, bf16[4,256,512]{2,1,0:T(8,128)(2,1)S(1)}, u32[]{:S(2)}, u32[]{:S(2)}) collective-permute-start(bf16[4,256,512]{2,1,0:T(8,128)(2,1)S(1)} %bitcast.25), channel_id=1, source_target_pairs={{8,7},{0,15},{24,23},{16,31},{40,39},{32,47},{56,55},{48,63},{72,7... | collective-permute-start | bytes 3145736 | tf_op jit(solution)/shard_map/ppermute | solution.py:212
  86.7 12.5 %collective-permute-start.3 = (bf16[2,384,256]{2,1,0:T(8,128)(2,1)S(1)}, bf16[2,384,256]{2,1,0:T(8,128)(2,1)S(1)}, u32[]{:S(2)}, u32[]{:S(2)}) collective-permute-start(bf16[2,384,256]{2,1,0:T(8,128)(2,1)S(1)} %collective-permute-done.2.refs_5_), channel_id=1, source_target_pairs={{0,16},{16,32},{32,48},{48,64},{64,80},{80,96},{96,112},{112,0},{1... | collective-permute-start | bytes 1179656 | tf_op jit(solution)/shard_map/ppermute | solution.py:216
  88.7 12.6 %collective-permute-start.6 = (bf16[2,384,256]{2,1,0:T(8,128)(2,1)S(1)}, bf16[2,384,256]{2,1,0:T(8,128)(2,1)S(1)}, u32[]{:S(2)}, u32[]{:S(2)}) collective-permute-start(bf16[2,384,256]{2,1,0:T(8,128)(2,1)S(1)} %collective-permute-done.5.refs_6_), channel_id=1, source_target_pairs={{0,112},{16,0},{32,16},{48,32},{64,48},{80,64},{96,80},{112,96},{1... | collective-permute-start | bytes 1179656 | tf_op jit(solution)/shard_map/ppermute | solution.py:217
  99.2 19.9 %collective-permute-start.4 = (bf16[2,384,256]{2,1,0:T(8,128)(2,1)S(1)}, bf16[2,384,256]{2,1,0:T(8,128)(2,1)S(1)}, u32[]{:S(2)}, u32[]{:S(2)}) collective-permute-start(bf16[2,384,256]{2,1,0:T(8,128)(2,1)S(1)} %collective-permute-done.3.refs_7_.refs_4_), channel_id=1, source_target_pairs={{0,16},{16,32},{32,48},{48,64},{64,80},{80,96},{96,112},{112,0},{1... | collective-permute-start | bytes 1179656 | tf_op jit(solution)/shard_map/ppermute | solution.py:216
  101.2 17.9 %collective-permute-start.7 = (bf16[2,384,256]{2,1,0:T(8,128)(2,1)S(1)}, bf16[2,384,256]{2,1,0:T(8,128)(2,1)S(1)}, u32[]{:S(2)}, u32[]{:S(2)}) collective-permute-start(bf16[2,384,256]{2,1,0:T(8,128)(2,1)S(1)} %collective-permute-done.6.refs_8_.refs_5_), channel_id=1, source_target_pairs={{0,112},{16,0},{32,16},{48,32},{64,48},{80,64},{96,80},{112,96},{1... | collective-permute-start | bytes 1179656 | tf_op jit(solution)/shard_map/ppermute | solution.py:217
  106.9 14.8 %collective-permute-start.8 = (bf16[2,192,256]{2,1,0:T(8,128)(2,1)S(1)}, bf16[2,192,256]{2,1,0:T(8,128)(2,1)S(1)}, u32[]{:S(2)}, u32[]{:S(2)}) collective-permute-start(bf16[2,192,256]{2,1,0:T(8,128)(2,1)S(1)} %slice.26), channel_id=1, source_target_pairs={{0,32},{16,48},{32,64},{48,80},{64,96},{80,112},{96,0},{112,16},{1... | collective-permute-start | bytes 589832 | tf_op jit(solution)/shard_map/ppermute | solution.py:222
  108.8 12.9 %collective-permute-start.9 = (bf16[2,192,256]{2,1,0:T(8,128)(2,1)S(1)}, bf16[2,192,256]{2,1,0:T(8,128)(2,1)S(1)}, u32[]{:S(2)}, u32[]{:S(2)}) collective-permute-start(bf16[2,192,256]{2,1,0:T(8,128)(2,1)S(1)} %slice.27), channel_id=1, source_target_pairs={{0,96},{16,112},{32,0},{48,16},{64,32},{80,48},{96,64},{112,80},{1... | collective-permute-start | bytes 589832 | tf_op jit(solution)/shard_map/ppermute | solution.py:223

commit v10 on v9

--- a/solution.py
+++ b/solution.py
@@ -95,7 +95,7 @@
 
 def two_rows(*refs):
     scalars = refs[:4]
-    own, f1, b1, f2, b2, b_here, b_in, b_over, out, acc, o_s, sem = refs[4:]
+    own, b1, f1, b2, f2, b_here, b_in, b_over, out, acc, o_s, sem = refs[4:]
     rows = (((0, (own, b1)), (-1, (f1, own))), ((-2, (f2, f1)), (1, (b1, b2))))
     acc[...] = jnp.zeros_like(acc)
     writes = []
@@ -108,7 +108,7 @@
 
 def third_row(*refs):
     scalars = refs[:4]
-    f2, b2, f3, b3, b_here, b_in, b_over, before, out, acc, o_s, sem = refs[4:]
+    b2, f2, b3, f3, b_here, b_in, b_over, before, out, acc, o_s, sem = refs[4:]
     acc[...] = jnp.zeros_like(acc)
     i = on_parity(scalars, (2, (b2, b3)), (-3, (f3, f2)), (0, 1), (b_here, (b_in, b_over)), acc)
     write_row(o_s, acc, out, i, sem.at[0]).wait()
@@ -116,7 +116,7 @@
 
 def last_row(*refs):
     scalars = refs[:4]
-    f3, b3, f4, b4, b_here, b_in, b_over, before, out, acc, o_s, sem = refs[4:]
+    b3, f3, b4, f4, b_here, b_in, b_over, before, out, acc, o_s, sem = refs[4:]
     acc[...] = jnp.zeros_like(acc)
     i = on_parity(scalars, (4, (f4, b4, f3)), (3, (b3, f4, b4)), (0, 1), (b_here, (b_in, b_over)), acc)
     write_row(o_s, acc, out, i, sem.at[0]).wait()
@@ -213,20 +213,20 @@
     ahead = [own]
     back = [own]
     for step in range(3):
+        back.append(lax.ppermute(back[-1], "z", z_route(-1)))
         ahead.append(lax.ppermute(ahead[-1], "z", z_route(1)))
-        back.append(lax.ppermute(back[-1], "z", z_route(-1)))
     scalars = (place, table, bc_here, bc_next)
-    near = (own, ahead[1], back[1], ahead[2], back[2])
+    near = (own, back[1], ahead[1], back[2], ahead[2])
     block = (NB, BS, BS)
     shape = jax.ShapeDtypeStruct((MB, BS, NB * BS), jnp.bfloat16)
+    b4 = lax.ppermute(back[2][:, SPAN // 2 :], "z", z_route(-2))
     f4 = lax.ppermute(ahead[2][:, : SPAN // 2], "z", z_route(2))
-    b4 = lax.ppermute(back[2][:, SPAN // 2 :], "z", z_route(-2))
     b_all = (b_here, b_in, b_over)
     wide = [pltpu.VMEM((2,) + block, jnp.float32), pltpu.VMEM((2, BS, NB * BS), jnp.bfloat16), pltpu.SemaphoreType.DMA((2,))]
     slim = [pltpu.VMEM(block, jnp.float32), pltpu.VMEM((BS, NB * BS), jnp.bfloat16), pltpu.SemaphoreType.DMA((1,))]
     window = call(two_rows, scalars, near + b_all, (), shape, wide, 12)
-    window = call(third_row, scalars, near[3:] + (ahead[3], back[3]) + b_all, (window,), shape, slim, 6, alias=True)
-    window = call(last_row, scalars, (ahead[3], back[3], f4, b4) + b_all, (window,), shape, slim, 6, alias=True)
+    window = call(third_row, scalars, near[3:] + (back[3], ahead[3]) + b_all, (window,), shape, slim, 6, alias=True)
+    window = call(last_row, scalars, (back[3], ahead[3], b4, f4) + b_all, (window,), shape, slim, 6, alias=True)
     return window[None, None]
 
 

time: 125 us -> 123 us (0.984)
  starting transfers between devices: 49.3 us -> 43.4 us
  waiting for transfers between devices: 42.4 us -> 47.6 us
  Pallas kernels: 12.1 us -> 10.8 us
    ppermute x3, waiting for transfers between devices: 0.09 us -> 9.71 us  [on_device(): back.append(lax.ppermute(back[-1], 'z', z_route(-1)))]
    ppermute x3, starting transfers between devices: 15.5 us -> 9.54 us  [on_device(): back.append(lax.ppermute(back[-1], 'z', z_route(-1)))]
    ppermute x3, waiting for transfers between devices: 8.84 us -> 4.49 us  [on_device(): ahead.append(lax.ppermute(ahead[-1], 'z', z_route(1)))]
    ppermute x1, starting transfers between devices: 6.03 us -> 2.37 us  [on_device(): b4 = lax.ppermute(back[2][:, SPAN // 2:], 'z', z_route(-2))]
    ppermute x1, starting transfers between devices: 1.92 us -> 4.37 us  [on_device(): f4 = lax.ppermute(ahead[2][:, :SPAN // 2], 'z', z_route(2))]
    ppermute x3, starting transfers between devices: 6.35 us -> 7.66 us  [on_device(): ahead.append(lax.ppermute(ahead[-1], 'z', z_route(1)))]
    pallas_call x3, Pallas kernels: 9.8 us -> 8.55 us  [call(): pl.pallas_call(kernel, out_shape=out_shape, grid_spec=pltpu.PrefetchScala...]
  transfers between devices with their start and end apart: 12 -> 12, of which waited for: 5 -> 6; matrix products, arithmetic and copies ran while one was open for 1% -> 1% of each run, Pallas kernels for 5% -> 4%
where the time goes in v10:
time: 123 us
  waiting for transfers between devices  47.6 us (39%)
  starting transfers between devices  43.4 us (35%)
  blocking collectives  15 us (12%)
  Pallas kernels  10.8 us (9%)
  between operations  3.95 us (3%)
  local copies, waits for them, and re-layouts  1.98 us (2%)
    all_to_all x1, waiting for transfers between devices, on_device(): lax.all_to_all(payload(a_columns[0].transpose(2, 0, 1), a_live[0], tile),...  28.5 us
    all_gather x1, blocking collectives, on_device(): own = lax.all_gather(two[:, :PIECE], 'y_lo', axis=1, tiled=True)  15 us
    all_to_all x1, starting transfers between devices, on_device(): lax.all_to_all(payload(a_columns[0].transpose(2, 0, 1), a_live[0], tile),...  14 us
    ppermute x3, waiting for transfers between devices, on_device(): back.append(lax.ppermute(back[-1], 'z', z_route(-1)))  9.71 us
    ppermute x3, starting transfers between devices, on_device(): back.append(lax.ppermute(back[-1], 'z', z_route(-1)))  9.54 us
    pallas_call x3, Pallas kernels, call(): pl.pallas_call(kernel, out_shape=out_shape, grid_spec=pltpu.PrefetchScala...  8.55 us
    ppermute x3, starting transfers between devices, on_device(): ahead.append(lax.ppermute(ahead[-1], 'z', z_route(1)))  7.66 us
    ppermute x1, waiting for transfers between devices, on_device(): bc_next = lax.ppermute(bc_here, COL, col_route(cols)).reshape(-1)  4.9 us
  transfers between devices with their start and end apart: 12, of which 6 were waited for; matrix products, arithmetic and copies ran while one was open for 1% of the time, Pallas kernels for 4%

profile of v10, /device:TPU:6, one launch (start us, length us, event | category | flops | bytes accessed | tf_op | source)
XLA Modules:
  0.0 122.9 jit_solution(2147863202978583473)
XLA Ops:
  0.0 2.3 %shard_map.64 = bf16[32,104,256]{2,1,0:T(8,128)(2,1)} custom-call(s32[3,1,4]{2,1,0:T(1,128)} %bitcast.30, s32[1,4]{1,0:T(1,128)} %bitcast.32, bf16[32,96,256]{2,1,0:T(8,128)(2,1)} %bitcast.29), custom_call_target="tpu_custom_call" | custom-call | tf_op jit(solution)/shard_map/pallas_call | solution.py:178
  2.3 0.0 copy-start
  2.3 0.0 copy-start.1
  2.3 0.0 copy-start.2
  2.3 14.0 %all-to-all-start = ((bf16[32,104,256]{2,1,0:T(8,128)(2,1)}), bf16[32,104,256]{2,1,0:T(8,128)(2,1)}, u32[]{:S(2)}, u32[]{:S(2)}) async-start(bf16[32,104,256]{2,1,0:T(8,128)(2,1)} %shard_map.64), calls=%async_computation | async-start | bytes 3407872 | tf_op jit(solution)/shard_map/all_to_all | solution.py:197
  16.3 0.0 copy-done
  16.4 1.9 %collective-permute-start.1 = (bf16[4,256,512]{2,1,0:T(8,128)(2,1)S(1)}, bf16[4,256,512]{2,1,0:T(8,128)(2,1)S(1)}, u32[]{:S(2)}, u32[]{:S(2)}) collective-permute-start(bf16[4,256,512]{2,1,0:T(8,128)(2,1)S(1)} %bitcast.24), channel_id=1, source_target_pairs={{1,0},{2,1},{3,2},{4,3},{5,4},{6,5},{7,6},{9,8},{10,9},{11,10},{12... | collective-permute-start | bytes 3145736 | tf_op jit(solution)/shard_map/ppermute | solution.py:205
  18.3 0.0 copy-done.1
  18.3 2.8 %collective-permute-start = (s32[4,2]{0,1:T(2,128)S(1)}, s32[4,2]{0,1:T(2,128)S(1)}, u32[]{:S(2)}, u32[]{:S(2)}) collective-permute-start(s32[4,2]{0,1:T(2,128)S(1)} %bitcast.31), channel_id=1, source_target_pairs={{1,0},{2,1},{3,2},{4,3},{5,4},{6,5},{7,6},{8,7},{9,8},{10,9},{11,1... | collective-permute-start | bytes 104 | tf_op jit(solution)/shard_map/ppermute | solution.py:201
  21.1 0.0 copy-done.2
  21.2 0.6 fusion.5
  24.3 0.1 copy.11
  24.4 0.1 reshape_squeeze.3.refs_2_
  25.7 4.9 %collective-permute-done = s32[4,2]{0,1:T(2,128)S(1)} collective-permute-done((s32[4,2]{0,1:T(2,128)S(1)}, s32[4,2]{0,1:T(2,128)S(1)}, u32[]{:S(2)}, u32[]{:S(2)}) %collective-permute-start) | collective-permute-done | bytes 64 | tf_op jit(solution)/shard_map/ppermute | solution.py:201
  30.6 0.1 copy.12
  30.7 0.1 reshape.11.refs_3_
  30.8 0.0 collective-permute-done.1.refs_10_.refs_9_
  30.8 28.5 %all-to-all-done = bf16[32,104,256]{2,1,0:T(8,128)(2,1)} async-done(((bf16[32,104,256]{2,1,0:T(8,128)(2,1)}), bf16[32,104,256]{2,1,0:T(8,128)(2,1)}, u32[]{:S(2)}, u32[]{:S(2)}) %all-to-all-start) | async-done | bytes 1703968 | tf_op jit(solution)/shard_map/all_to_all | solution.py:197
  59.3 0.8 constant_dynamic-slice_fusion
  60.2 0.1 reshape.12.refs_1_
  60.3 15.0 %all_gather.3.refs_4_ = bf16[2,384,256]{2,1,0:T(8,128)(2,1)S(1)} all-gather(bf16[2,96,256]{2,1,0:T(8,128)(2,1)S(1)} %fusion), channel_id=1, replica_groups=mesh['y_lo'=4,'z'=8,'y_hi'=2,'x'=4,'core'=2] {'y_lo'}, dimensions={1}, use_global_device_ids=true | all-gather | bytes 491520 | tf_op jit(solution)/shard_map/all_gather | solution.py:210
  75.3 3.2 %collective-permute-start.2 = (bf16[2,384,256]{2,1,0:T(8,128)(2,1)S(1)}, bf16[2,384,256]{2,1,0:T(8,128)(2,1)S(1)}, u32[]{:S(2)}, u32[]{:S(2)}) collective-permute-start(bf16[2,384,256]{2,1,0:T(8,128)(2,1)S(1)} %all_gather.3.refs_4_), channel_id=1, source_target_pairs={{0,112},{16,0},{32,16},{48,32},{64,48},{80,64},{96,80},{112,96},{1... | collective-permute-start | bytes 1179656 | tf_op jit(solution)/shard_map/ppermute | solution.py:216
  78.5 2.6 %collective-permute-start.5 = (bf16[2,384,256]{2,1,0:T(8,128)(2,1)S(1)}, bf16[2,384,256]{2,1,0:T(8,128)(2,1)S(1)}, u32[]{:S(2)}, u32[]{:S(2)}) collective-permute-start(bf16[2,384,256]{2,1,0:T(8,128)(2,1)S(1)} %all_gather.3.refs_4_), channel_id=1, source_target_pairs={{0,16},{16,32},{32,48},{48,64},{64,80},{80,96},{96,112},{112,0},{1... | collective-permute-start | bytes 1179656 | tf_op jit(solution)/shard_map/ppermute | solution.py:217
  81.1 0.7 collective-permute-start.10
  81.9 4.1 %collective-permute-done.2.refs_5_ = bf16[2,384,256]{2,1,0:T(8,128)(2,1)S(1)} collective-permute-done((bf16[2,384,256]{2,1,0:T(8,128)(2,1)S(1)}, bf16[2,384,256]{2,1,0:T(8,128)(2,1)S(1)}, u32[]{:S(2)}, u32[]{:S(2)}) %collective-permute-start.2) | collective-permute-done | bytes 393248 | tf_op jit(solution)/shard_map/ppermute | solution.py:216
  86.0 3.4 %collective-permute-start.3 = (bf16[2,384,256]{2,1,0:T(8,128)(2,1)S(1)}, bf16[2,384,256]{2,1,0:T(8,128)(2,1)S(1)}, u32[]{:S(2)}, u32[]{:S(2)}) collective-permute-start(bf16[2,384,256]{2,1,0:T(8,128)(2,1)S(1)} %collective-permute-done.2.refs_5_), channel_id=1, source_target_pairs={{0,112},{16,0},{32,16},{48,32},{64,48},{80,64},{96,80},{112,96},{1... | collective-permute-start | bytes 1179656 | tf_op jit(solution)/shard_map/ppermute | solution.py:216
  89.4 0.0 collective-permute-done.5.refs_6_
  89.4 2.4 %collective-permute-start.6 = (bf16[2,384,256]{2,1,0:T(8,128)(2,1)S(1)}, bf16[2,384,256]{2,1,0:T(8,128)(2,1)S(1)}, u32[]{:S(2)}, u32[]{:S(2)}) collective-permute-start(bf16[2,384,256]{2,1,0:T(8,128)(2,1)S(1)} %collective-permute-done.5.refs_6_), channel_id=1, source_target_pairs={{0,16},{16,32},{32,48},{48,64},{64,80},{80,96},{96,112},{112,0},{1... | collective-permute-start | bytes 1179656 | tf_op jit(solution)/shard_map/ppermute | solution.py:217
  91.8 5.6 %collective-permute-done.3.refs_7_.refs_4_ = bf16[2,384,256]{2,1,0:T(8,128)(2,1)S(1)} collective-permute-done((bf16[2,384,256]{2,1,0:T(8,128)(2,1)S(1)}, bf16[2,384,256]{2,1,0:T(8,128)(2,1)S(1)}, u32[]{:S(2)}, u32[]{:S(2)}) %collective-permute-start.3) | collective-permute-done | bytes 393248 | tf_op jit(solution)/shard_map/ppermute | solution.py:216
  97.4 2.9 %collective-permute-start.4 = (bf16[2,384,256]{2,1,0:T(8,128)(2,1)S(1)}, bf16[2,384,256]{2,1,0:T(8,128)(2,1)S(1)}, u32[]{:S(2)}, u32[]{:S(2)}) collective-permute-start(bf16[2,384,256]{2,1,0:T(8,128)(2,1)S(1)} %collective-permute-done.3.refs_7_.refs_4_), channel_id=1, source_target_pairs={{0,112},{16,0},{32,16},{48,32},{64,48},{80,64},{96,80},{112,96},{1... | collective-permute-start | bytes 1179656 | tf_op jit(solution)/shard_map/ppermute | solution.py:216
  100.3 0.3 collective-permute-done.6.refs_8_.refs_5_
  100.7 2.6 %collective-permute-start.7 = (bf16[2,384,256]{2,1,0:T(8,128)(2,1)S(1)}, bf16[2,384,256]{2,1,0:T(8,128)(2,1)S(1)}, u32[]{:S(2)}, u32[]{:S(2)}) collective-permute-start(bf16[2,384,256]{2,1,0:T(8,128)(2,1)S(1)} %collective-permute-done.6.refs_8_.refs_5_), channel_id=1, source_target_pairs={{0,16},{16,32},{32,48},{48,64},{64,80},{80,96},{96,112},{112,0},{1... | collective-permute-start | bytes 1179656 | tf_op jit(solution)/shard_map/ppermute | solution.py:217
  103.3 2.4 %collective-permute-start.8 = (bf16[2,192,256]{2,1,0:T(8,128)(2,1)S(1)}, bf16[2,192,256]{2,1,0:T(8,128)(2,1)S(1)}, u32[]{:S(2)}, u32[]{:S(2)}) collective-permute-start(bf16[2,192,256]{2,1,0:T(8,128)(2,1)S(1)} %slice.26), channel_id=1, source_target_pairs={{0,96},{16,112},{32,0},{48,16},{64,32},{80,48},{96,64},{112,80},{1... | collective-permute-start | bytes 589832 | tf_op jit(solution)/shard_map/ppermute | solution.py:222
  105.7 4.4 %collective-permute-start.9 = (bf16[2,192,256]{2,1,0:T(8,128)(2,1)S(1)}, bf16[2,192,256]{2,1,0:T(8,128)(2,1)S(1)}, u32[]{:S(2)}, u32[]{:S(2)}) collective-permute-start(bf16[2,192,256]{2,1,0:T(8,128)(2,1)S(1)} %slice.27), channel_id=1, source_target_pairs={{0,32},{16,48},{32,64},{48,80},{64,96},{80,112},{96,0},{112,16},{1... | collective-permute-start | bytes 589832 | tf_op jit(solution)/shard_map/ppermute | solution.py:223
  110.1 0.0 collective-permute-done.10.refs_11_.refs_10_
  110.1 2.7 %shard_map.65.refs_11_ = bf16[4,256,1024]{2,1,0:T(8,128)(2,1)} custom-call(s32[1]{0:T(128)} %bitcast.5.refs_0_, s32[32]{0:T(128)S(1)} %reshape.12.refs_1_, s32[8]{0:T(128)S(1)} %reshape_squeeze.3.refs_2_, s32[8]{0:T(128)S(1)} %reshape.11.refs_3_, bf16[2,384,256]{2,1,0:T(8,128)(2,1)S(1)} %all_gather.3.refs_4_, ...), custom_call_target="tpu_custom_call" | custom-call | flops 805306368 | bytes 1048576 | tf_op jit(solution)/shard_map/pallas_call | solution.py:128
  112.9 0.0 collective-permute-done.4.refs_6_.refs_4_
  112.9 4.2 %collective-permute-done.7.refs_7_.refs_5_ = bf16[2,384,256]{2,1,0:T(8,128)(2,1)S(1)} collective-permute-done((bf16[2,384,256]{2,1,0:T(8,128)(2,1)S(1)}, bf16[2,384,256]{2,1,0:T(8,128)(2,1)S(1)}, u32[]{:S(2)}, u32[]{:S(2)}) %collective-permute-start.7) | collective-permute-done | bytes 393248 | tf_op jit(solution)/shard_map/ppermute | solution.py:217
  117.0 2.8 %shard_map.66.refs_11_ = bf16[4,256,1024]{2,1,0:T(8,128)(2,1)} custom-call(s32[1]{0:T(128)} %bitcast.5.refs_0_, s32[32]{0:T(128)S(1)} %reshape.12.refs_1_, s32[8]{0:T(128)S(1)} %reshape_squeeze.3.refs_2_, s32[8]{0:T(128)S(1)} %reshape.11.refs_3_, bf16[2,384,256]{2,1,0:T(8,128)(2,1)S(1)} %collective-permute-done.3.refs_7_.refs_4_, ...), custom_call_target="tpu_custom_call", output_to_operand_aliasing={{}: (11, {})} | custom-call | flops 402653184 | bytes 1048576 | tf_op jit(solution)/shard_map/pallas_call | solution.py:128
  119.8 0.0 collective-permute-done.8.refs_6_
  119.8 0.0 collective-permute-done.9.refs_7_
  119.9 3.0 %shard_map.67 = bf16[4,256,1024]{2,1,0:T(8,128)(2,1)} custom-call(s32[1]{0:T(128)} %bitcast.5.refs_0_, s32[32]{0:T(128)S(1)} %reshape.12.refs_1_, s32[8]{0:T(128)S(1)} %reshape_squeeze.3.refs_2_, s32[8]{0:T(128)S(1)} %reshape.11.refs_3_, bf16[2,384,256]{2,1,0:T(8,128)(2,1)S(1)} %collective-permute-done.4.refs_6_.refs_4_, ...), custom_call_target="tpu_custom_call", output_to_operand_aliasing={{}: (11, {})} | custom-call | flops 402653184 | bytes 1048576 | tf_op jit(solution)/shard_map/pallas_call | solution.py:128
  (5 shorter events, 0.1 us)
Async XLA Ops:
  2.3 14.0 %copy-start = (bf16[1,1,4,256,512]{4,3,2,1,0:T(8,128)(2,1)S(1)}, bf16[1,1,4,256,512]{4,3,2,1,0:T(8,128)(2,1)}, u32[]{:S(2)}) copy-start(bf16[1,1,4,256,512]{4,3,2,1,0:T(8,128)(2,1)} %param.10) | copy-start | bytes 3145732
  2.3 16.0 %copy-start.1 = (s32[1,1,4,2]{2,3,1,0:T(2,128)S(1)}, s32[1,1,4,2]{2,3,1,0:T(2,128)}, u32[]{:S(2)}) copy-start(s32[1,1,4,2]{2,3,1,0:T(2,128)} %param.11) | copy-start | bytes 100
  2.3 18.8 %copy-start.2 = (s32[1,2]{1,0:T(1,128)S(1)}, s32[1,2]{1,0:T(1,128)}, u32[]{:S(2)}) copy-start(s32[1,2]{1,0:T(1,128)} %param.9) | copy-start | bytes 28
  2.3 57.0 %all-to-all-start = ((bf16[32,104,256]{2,1,0:T(8,128)(2,1)}), bf16[32,104,256]{2,1,0:T(8,128)(2,1)}, u32[]{:S(2)}, u32[]{:S(2)}) async-start(bf16[32,104,256]{2,1,0:T(8,128)(2,1)} %shard_map.64), calls=%async_computation | async-start | bytes 3407872 | tf_op jit(solution)/shard_map/all_to_all | solution.py:197
  16.4 14.4 %collective-permute-start.1 = (bf16[4,256,512]{2,1,0:T(8,128)(2,1)S(1)}, bf16[4,256,512]{2,1,0:T(8,128)(2,1)S(1)}, u32[]{:S(2)}, u32[]{:S(2)}) collective-permute-start(bf16[4,256,512]{2,1,0:T(8,128)(2,1)S(1)} %bitcast.24), channel_id=1, source_target_pairs={{1,0},{2,1},{3,2},{4,3},{5,4},{6,5},{7,6},{9,8},{10,9},{11,10},{12... | collective-permute-start | bytes 3145736 | tf_op jit(solution)/shard_map/ppermute | solution.py:205
  18.3 12.3 %collective-permute-start = (s32[4,2]{0,1:T(2,128)S(1)}, s32[4,2]{0,1:T(2,128)S(1)}, u32[]{:S(2)}, u32[]{:S(2)}) collective-permute-start(s32[4,2]{0,1:T(2,128)S(1)} %bitcast.31), channel_id=1, source_target_pairs={{1,0},{2,1},{3,2},{4,3},{5,4},{6,5},{7,6},{8,7},{9,8},{10,9},{11,1... | collective-permute-start | bytes 104 | tf_op jit(solution)/shard_map/ppermute | solution.py:201
  75.3 10.7 %collective-permute-start.2 = (bf16[2,384,256]{2,1,0:T(8,128)(2,1)S(1)}, bf16[2,384,256]{2,1,0:T(8,128)(2,1)S(1)}, u32[]{:S(2)}, u32[]{:S(2)}) collective-permute-start(bf16[2,384,256]{2,1,0:T(8,128)(2,1)S(1)} %all_gather.3.refs_4_), channel_id=1, source_target_pairs={{0,112},{16,0},{32,16},{48,32},{64,48},{80,64},{96,80},{112,96},{1... | collective-permute-start | bytes 1179656 | tf_op jit(solution)/shard_map/ppermute | solution.py:216
  78.5 10.9 %collective-permute-start.5 = (bf16[2,384,256]{2,1,0:T(8,128)(2,1)S(1)}, bf16[2,384,256]{2,1,0:T(8,128)(2,1)S(1)}, u32[]{:S(2)}, u32[]{:S(2)}) collective-permute-start(bf16[2,384,256]{2,1,0:T(8,128)(2,1)S(1)} %all_gather.3.refs_4_), channel_id=1, source_target_pairs={{0,16},{16,32},{32,48},{48,64},{64,80},{80,96},{96,112},{112,0},{1... | collective-permute-start | bytes 1179656 | tf_op jit(solution)/shard_map/ppermute | solution.py:217
  81.1 29.0 %collective-permute-start.10 = (bf16[4,256,512]{2,1,0:T(8,128)(2,1)S(1)}, bf16[4,256,512]{2,1,0:T(8,128)(2,1)S(1)}, u32[]{:S(2)}, u32[]{:S(2)}) collective-permute-start(bf16[4,256,512]{2,1,0:T(8,128)(2,1)S(1)} %bitcast.25), channel_id=1, source_target_pairs={{8,7},{0,15},{24,23},{16,31},{40,39},{32,47},{56,55},{48,63},{72,7... | collective-permute-start | bytes 3145736 | tf_op jit(solution)/shard_map/ppermute | solution.py:212
  86.0 11.5 %collective-permute-start.3 = (bf16[2,384,256]{2,1,0:T(8,128)(2,1)S(1)}, bf16[2,384,256]{2,1,0:T(8,128)(2,1)S(1)}, u32[]{:S(2)}, u32[]{:S(2)}) collective-permute-start(bf16[2,384,256]{2,1,0:T(8,128)(2,1)S(1)} %collective-permute-done.2.refs_5_), channel_id=1, source_target_pairs={{0,112},{16,0},{32,16},{48,32},{64,48},{80,64},{96,80},{112,96},{1... | collective-permute-start | bytes 1179656 | tf_op jit(solution)/shard_map/ppermute | solution.py:216
  89.4 11.3 %collective-permute-start.6 = (bf16[2,384,256]{2,1,0:T(8,128)(2,1)S(1)}, bf16[2,384,256]{2,1,0:T(8,128)(2,1)S(1)}, u32[]{:S(2)}, u32[]{:S(2)}) collective-permute-start(bf16[2,384,256]{2,1,0:T(8,128)(2,1)S(1)} %collective-permute-done.5.refs_6_), channel_id=1, source_target_pairs={{0,16},{16,32},{32,48},{48,64},{64,80},{80,96},{96,112},{112,0},{1... | collective-permute-start | bytes 1179656 | tf_op jit(solution)/shard_map/ppermute | solution.py:217
  97.4 15.4 %collective-permute-start.4 = (bf16[2,384,256]{2,1,0:T(8,128)(2,1)S(1)}, bf16[2,384,256]{2,1,0:T(8,128)(2,1)S(1)}, u32[]{:S(2)}, u32[]{:S(2)}) collective-permute-start(bf16[2,384,256]{2,1,0:T(8,128)(2,1)S(1)} %collective-permute-done.3.refs_7_.refs_4_), channel_id=1, source_target_pairs={{0,112},{16,0},{32,16},{48,32},{64,48},{80,64},{96,80},{112,96},{1... | collective-permute-start | bytes 1179656 | tf_op jit(solution)/shard_map/ppermute | solution.py:216
  100.7 16.4 %collective-permute-start.7 = (bf16[2,384,256]{2,1,0:T(8,128)(2,1)S(1)}, bf16[2,384,256]{2,1,0:T(8,128)(2,1)S(1)}, u32[]{:S(2)}, u32[]{:S(2)}) collective-permute-start(bf16[2,384,256]{2,1,0:T(8,128)(2,1)S(1)} %collective-permute-done.6.refs_8_.refs_5_), channel_id=1, source_target_pairs={{0,16},{16,32},{32,48},{48,64},{64,80},{80,96},{96,112},{112,0},{1... | collective-permute-start | bytes 1179656 | tf_op jit(solution)/shard_map/ppermute | solution.py:217
  103.3 16.5 %collective-permute-start.8 = (bf16[2,192,256]{2,1,0:T(8,128)(2,1)S(1)}, bf16[2,192,256]{2,1,0:T(8,128)(2,1)S(1)}, u32[]{:S(2)}, u32[]{:S(2)}) collective-permute-start(bf16[2,192,256]{2,1,0:T(8,128)(2,1)S(1)} %slice.26), channel_id=1, source_target_pairs={{0,96},{16,112},{32,0},{48,16},{64,32},{80,48},{96,64},{112,80},{1... | collective-permute-start | bytes 589832 | tf_op jit(solution)/shard_map/ppermute | solution.py:222
  105.7 14.1 %collective-permute-start.9 = (bf16[2,192,256]{2,1,0:T(8,128)(2,1)S(1)}, bf16[2,192,256]{2,1,0:T(8,128)(2,1)S(1)}, u32[]{:S(2)}, u32[]{:S(2)}) collective-permute-start(bf16[2,192,256]{2,1,0:T(8,128)(2,1)S(1)} %slice.27), channel_id=1, source_target_pairs={{0,32},{16,48},{32,64},{48,80},{64,96},{80,112},{96,0},{112,16},{1... | collective-permute-start | bytes 589832 | tf_op jit(solution)/shard_map/ppermute | solution.py:223

commit v11 on v10

--- a/solution.py
+++ b/solution.py
@@ -106,20 +106,20 @@
         c.wait()
 
 
-def third_row(*refs):
+def last_rows(*refs):
     scalars = refs[:4]
-    b2, f2, b3, f3, b_here, b_in, b_over, before, out, acc, o_s, sem = refs[4:]
+    b2, f2, b3, f3, b4, f4, b_here, b_in, b_over, before, out, acc, o_s, sem = refs[4:]
+    rows = (
+        ((2, (b2, b3)), (-3, (f3, f2))),
+        ((4, (f4, b4, f3)), (3, (b3, f4, b4))),
+    )
     acc[...] = jnp.zeros_like(acc)
-    i = on_parity(scalars, (2, (b2, b3)), (-3, (f3, f2)), (0, 1), (b_here, (b_in, b_over)), acc)
-    write_row(o_s, acc, out, i, sem.at[0]).wait()
-
-
-def last_row(*refs):
-    scalars = refs[:4]
-    b3, f3, b4, f4, b_here, b_in, b_over, before, out, acc, o_s, sem = refs[4:]
-    acc[...] = jnp.zeros_like(acc)
-    i = on_parity(scalars, (4, (f4, b4, f3)), (3, (b3, f4, b4)), (0, 1), (b_here, (b_in, b_over)), acc)
-    write_row(o_s, acc, out, i, sem.at[0]).wait()
+    writes = []
+    for n, (even, odd) in enumerate(rows):
+        i = on_parity(scalars, even, odd, (0, 1), (b_here, (b_in, b_over)), acc.at[n])
+        writes.append(write_row(o_s.at[n], acc.at[n], out, i, sem.at[n]))
+    for c in writes:
+        c.wait()
 
 
 def call(kernel, scalars, held, left, out_shape, scratch, products, alias=False):
@@ -223,10 +223,9 @@
     f4 = lax.ppermute(ahead[2][:, : SPAN // 2], "z", z_route(2))
     b_all = (b_here, b_in, b_over)
     wide = [pltpu.VMEM((2,) + block, jnp.float32), pltpu.VMEM((2, BS, NB * BS), jnp.bfloat16), pltpu.SemaphoreType.DMA((2,))]
-    slim = [pltpu.VMEM(block, jnp.float32), pltpu.VMEM((BS, NB * BS), jnp.bfloat16), pltpu.SemaphoreType.DMA((1,))]
     window = call(two_rows, scalars, near + b_all, (), shape, wide, 12)
-    window = call(third_row, scalars, near[3:] + (back[3], ahead[3]) + b_all, (window,), shape, slim, 6, alias=True)
-    window = call(last_row, scalars, (back[3], ahead[3], b4, f4) + b_all, (window,), shape, slim, 6, alias=True)
+    far = near[3:] + (back[3], ahead[3], b4, f4)
+    window = call(last_rows, scalars, far + b_all, (window,), shape, wide, 12, alias=True)
     return window[None, None]
 
 

time: 123 us -> 124 us (level); the launches traced: 123 us -> 123 us
  starting transfers between devices: 43.4 us -> 49.3 us
  waiting for transfers between devices: 47.6 us -> 42.4 us
    ppermute x3, waiting for transfers between devices: 9.71 us -> 0.09 us  [on_device(): back.append(lax.ppermute(back[-1], 'z', z_route(-1)))]
    ppermute x3, starting transfers between devices: 9.54 us -> 15.5 us  [on_device(): back.append(lax.ppermute(back[-1], 'z', z_route(-1)))]
    ppermute x3, waiting for transfers between devices: 4.49 us -> 8.84 us  [on_device(): ahead.append(lax.ppermute(ahead[-1], 'z', z_route(1)))]
    ppermute x1, starting transfers between devices: 2.37 us -> 6.03 us  [on_device(): b4 = lax.ppermute(back[2][:, SPAN // 2:], 'z', z_route(-2))]
    ppermute x1, starting transfers between devices: 4.37 us -> 1.92 us  [on_device(): f4 = lax.ppermute(ahead[2][:, :SPAN // 2], 'z', z_route(2))]
    ppermute x3, starting transfers between devices: 7.66 us -> 6.35 us  [on_device(): ahead.append(lax.ppermute(ahead[-1], 'z', z_route(1)))]
    pallas_call x3 -> x2, Pallas kernels: 8.55 us -> 7.68 us  [call(): pl.pallas_call(kernel, out_shape=out_shape, grid_spec=pltpu.PrefetchScala...]
  transfers between devices with their start and end apart: 12 -> 12, of which waited for: 6 -> 5; matrix products, arithmetic and copies ran while one was open for 1% -> 1% of each run, Pallas kernels for 4% -> 3%
where the time goes in v11:
time: 124 us; the launch traced here: 123 us
  starting transfers between devices  49.3 us (40%)
  waiting for transfers between devices  42.4 us (34%)
  blocking collectives  15 us (12%)
  Pallas kernels  9.97 us (8%)
  between operations  3.96 us (3%)
  local copies, waits for them, and re-layouts  1.98 us (2%)
    all_to_all x1, waiting for transfers between devices, on_device(): lax.all_to_all(payload(a_columns[0].transpose(2, 0, 1), a_live[0], tile),...  28.5 us
    ppermute x3, starting transfers between devices, on_device(): back.append(lax.ppermute(back[-1], 'z', z_route(-1)))  15.5 us
    all_gather x1, blocking collectives, on_device(): own = lax.all_gather(two[:, :PIECE], 'y_lo', axis=1, tiled=True)  15 us
    all_to_all x1, starting transfers between devices, on_device(): lax.all_to_all(payload(a_columns[0].transpose(2, 0, 1), a_live[0], tile),...  14 us
    ppermute x3, waiting for transfers between devices, on_device(): ahead.append(lax.ppermute(ahead[-1], 'z', z_route(1)))  8.84 us
    pallas_call x2, Pallas kernels, call(): pl.pallas_call(kernel, out_shape=out_shape, grid_spec=pltpu.PrefetchScala...  7.68 us
    ppermute x3, starting transfers between devices, on_device(): ahead.append(lax.ppermute(ahead[-1], 'z', z_route(1)))  6.35 us
    ppermute x1, starting transfers between devices, on_device(): b4 = lax.ppermute(back[2][:, SPAN // 2:], 'z', z_route(-2))  6.03 us
  transfers between devices with their start and end apart: 12, of which 5 were waited for; matrix products, arithmetic and copies ran while one was open for 1% of the time, Pallas kernels for 3%

profile of v11, /device:TPU:6, one launch (start us, length us, event | category | flops | bytes accessed | tf_op | source)
XLA Modules:
  0.0 122.6 jit_solution(4886472039365478389)
XLA Ops:
  0.0 2.3 %shard_map.64 = bf16[32,104,256]{2,1,0:T(8,128)(2,1)} custom-call(s32[3,1,4]{2,1,0:T(1,128)} %bitcast.29, s32[1,4]{1,0:T(1,128)} %bitcast.31, bf16[32,96,256]{2,1,0:T(8,128)(2,1)} %bitcast.28), custom_call_target="tpu_custom_call" | custom-call | tf_op jit(solution)/shard_map/pallas_call | solution.py:178
  2.3 0.0 copy-start
  2.3 0.0 copy-start.1
  2.3 0.0 copy-start.2
  2.3 14.0 %all-to-all-start = ((bf16[32,104,256]{2,1,0:T(8,128)(2,1)}), bf16[32,104,256]{2,1,0:T(8,128)(2,1)}, u32[]{:S(2)}, u32[]{:S(2)}) async-start(bf16[32,104,256]{2,1,0:T(8,128)(2,1)} %shard_map.64), calls=%async_computation | async-start | bytes 3407872 | tf_op jit(solution)/shard_map/all_to_all | solution.py:197
  16.3 0.0 copy-done
  16.4 1.9 %collective-permute-start.1 = (bf16[4,256,512]{2,1,0:T(8,128)(2,1)S(1)}, bf16[4,256,512]{2,1,0:T(8,128)(2,1)S(1)}, u32[]{:S(2)}, u32[]{:S(2)}) collective-permute-start(bf16[4,256,512]{2,1,0:T(8,128)(2,1)S(1)} %bitcast.24), channel_id=1, source_target_pairs={{1,0},{2,1},{3,2},{4,3},{5,4},{6,5},{7,6},{9,8},{10,9},{11,10},{12... | collective-permute-start | bytes 3145736 | tf_op jit(solution)/shard_map/ppermute | solution.py:205
  18.3 0.0 copy-done.1
  18.3 2.8 %collective-permute-start = (s32[4,2]{0,1:T(2,128)S(1)}, s32[4,2]{0,1:T(2,128)S(1)}, u32[]{:S(2)}, u32[]{:S(2)}) collective-permute-start(s32[4,2]{0,1:T(2,128)S(1)} %bitcast.30), channel_id=1, source_target_pairs={{1,0},{2,1},{3,2},{4,3},{5,4},{6,5},{7,6},{8,7},{9,8},{10,9},{11,1... | collective-permute-start | bytes 104 | tf_op jit(solution)/shard_map/ppermute | solution.py:201
  21.1 0.0 copy-done.2
  21.2 0.6 fusion.5
  24.3 0.1 copy.10
  24.4 0.1 reshape_squeeze.3.refs_2_
  25.7 4.9 %collective-permute-done = s32[4,2]{0,1:T(2,128)S(1)} collective-permute-done((s32[4,2]{0,1:T(2,128)S(1)}, s32[4,2]{0,1:T(2,128)S(1)}, u32[]{:S(2)}, u32[]{:S(2)}) %collective-permute-start) | collective-permute-done | bytes 64 | tf_op jit(solution)/shard_map/ppermute | solution.py:201
  30.6 0.1 copy.11
  30.7 0.1 reshape.11.refs_3_
  30.8 0.0 collective-permute-done.1.refs_10_.refs_11_
  30.8 28.5 %all-to-all-done = bf16[32,104,256]{2,1,0:T(8,128)(2,1)} async-done(((bf16[32,104,256]{2,1,0:T(8,128)(2,1)}), bf16[32,104,256]{2,1,0:T(8,128)(2,1)}, u32[]{:S(2)}, u32[]{:S(2)}) %all-to-all-start) | async-done | bytes 1703968 | tf_op jit(solution)/shard_map/all_to_all | solution.py:197
  59.3 0.8 constant_dynamic-slice_fusion
  60.2 0.1 reshape.12.refs_1_
  60.3 15.0 %all_gather.3.refs_4_ = bf16[2,384,256]{2,1,0:T(8,128)(2,1)S(1)} all-gather(bf16[2,96,256]{2,1,0:T(8,128)(2,1)S(1)} %fusion), channel_id=1, replica_groups=mesh['y_lo'=4,'z'=8,'y_hi'=2,'x'=4,'core'=2] {'y_lo'}, dimensions={1}, use_global_device_ids=true | all-gather | bytes 491520 | tf_op jit(solution)/shard_map/all_gather | solution.py:210
  75.3 2.5 %collective-permute-start.4 = (bf16[2,384,256]{2,1,0:T(8,128)(2,1)S(1)}, bf16[2,384,256]{2,1,0:T(8,128)(2,1)S(1)}, u32[]{:S(2)}, u32[]{:S(2)}) collective-permute-start(bf16[2,384,256]{2,1,0:T(8,128)(2,1)S(1)} %all_gather.3.refs_4_), channel_id=1, source_target_pairs={{0,16},{16,32},{32,48},{48,64},{64,80},{80,96},{96,112},{112,0},{1... | collective-permute-start | bytes 1179656 | tf_op jit(solution)/shard_map/ppermute | solution.py:217
  77.8 4.5 %collective-permute-start.2 = (bf16[2,384,256]{2,1,0:T(8,128)(2,1)S(1)}, bf16[2,384,256]{2,1,0:T(8,128)(2,1)S(1)}, u32[]{:S(2)}, u32[]{:S(2)}) collective-permute-start(bf16[2,384,256]{2,1,0:T(8,128)(2,1)S(1)} %all_gather.3.refs_4_), channel_id=1, source_target_pairs={{0,112},{16,0},{32,16},{48,32},{64,48},{80,64},{96,80},{112,96},{1... | collective-permute-start | bytes 1179656 | tf_op jit(solution)/shard_map/ppermute | solution.py:216
  82.3 0.7 collective-permute-start.10
  83.1 3.6 %collective-permute-done.4.refs_6_ = bf16[2,384,256]{2,1,0:T(8,128)(2,1)S(1)} collective-permute-done((bf16[2,384,256]{2,1,0:T(8,128)(2,1)S(1)}, bf16[2,384,256]{2,1,0:T(8,128)(2,1)S(1)}, u32[]{:S(2)}, u32[]{:S(2)}) %collective-permute-start.4) | collective-permute-done | bytes 393248 | tf_op jit(solution)/shard_map/ppermute | solution.py:217
  86.7 1.9 %collective-permute-start.5 = (bf16[2,384,256]{2,1,0:T(8,128)(2,1)S(1)}, bf16[2,384,256]{2,1,0:T(8,128)(2,1)S(1)}, u32[]{:S(2)}, u32[]{:S(2)}) collective-permute-start(bf16[2,384,256]{2,1,0:T(8,128)(2,1)S(1)} %collective-permute-done.4.refs_6_), channel_id=1, source_target_pairs={{0,16},{16,32},{32,48},{48,64},{64,80},{80,96},{96,112},{112,0},{1... | collective-permute-start | bytes 1179656 | tf_op jit(solution)/shard_map/ppermute | solution.py:217
  88.6 0.0 collective-permute-done.2.refs_5_
  88.7 5.4 %collective-permute-start.3 = (bf16[2,384,256]{2,1,0:T(8,128)(2,1)S(1)}, bf16[2,384,256]{2,1,0:T(8,128)(2,1)S(1)}, u32[]{:S(2)}, u32[]{:S(2)}) collective-permute-start(bf16[2,384,256]{2,1,0:T(8,128)(2,1)S(1)} %collective-permute-done.2.refs_5_), channel_id=1, source_target_pairs={{0,112},{16,0},{32,16},{48,32},{64,48},{80,64},{96,80},{112,96},{1... | collective-permute-start | bytes 1179656 | tf_op jit(solution)/shard_map/ppermute | solution.py:216
  94.1 5.2 %collective-permute-done.5.refs_8_.refs_5_ = bf16[2,384,256]{2,1,0:T(8,128)(2,1)S(1)} collective-permute-done((bf16[2,384,256]{2,1,0:T(8,128)(2,1)S(1)}, bf16[2,384,256]{2,1,0:T(8,128)(2,1)S(1)}, u32[]{:S(2)}, u32[]{:S(2)}) %collective-permute-start.5) | collective-permute-done | bytes 393248 | tf_op jit(solution)/shard_map/ppermute | solution.py:217
  99.2 1.9 %collective-permute-start.7 = (bf16[2,384,256]{2,1,0:T(8,128)(2,1)S(1)}, bf16[2,384,256]{2,1,0:T(8,128)(2,1)S(1)}, u32[]{:S(2)}, u32[]{:S(2)}) collective-permute-start(bf16[2,384,256]{2,1,0:T(8,128)(2,1)S(1)} %collective-permute-done.5.refs_8_.refs_5_), channel_id=1, source_target_pairs={{0,16},{16,32},{32,48},{48,64},{64,80},{80,96},{96,112},{112,0},{1... | collective-permute-start | bytes 1179656 | tf_op jit(solution)/shard_map/ppermute | solution.py:217
  101.2 0.1 collective-permute-done.3.refs_7_.refs_4_
  101.2 5.6 %collective-permute-start.6 = (bf16[2,384,256]{2,1,0:T(8,128)(2,1)S(1)}, bf16[2,384,256]{2,1,0:T(8,128)(2,1)S(1)}, u32[]{:S(2)}, u32[]{:S(2)}) collective-permute-start(bf16[2,384,256]{2,1,0:T(8,128)(2,1)S(1)} %collective-permute-done.3.refs_7_.refs_4_), channel_id=1, source_target_pairs={{0,112},{16,0},{32,16},{48,32},{64,48},{80,64},{96,80},{112,96},{1... | collective-permute-start | bytes 1179656 | tf_op jit(solution)/shard_map/ppermute | solution.py:216
  106.9 1.9 %collective-permute-start.9 = (bf16[2,192,256]{2,1,0:T(8,128)(2,1)S(1)}, bf16[2,192,256]{2,1,0:T(8,128)(2,1)S(1)}, u32[]{:S(2)}, u32[]{:S(2)}) collective-permute-start(bf16[2,192,256]{2,1,0:T(8,128)(2,1)S(1)} %slice.27), channel_id=1, source_target_pairs={{0,32},{16,48},{32,64},{48,80},{64,96},{80,112},{96,0},{112,16},{1... | collective-permute-start | bytes 589832 | tf_op jit(solution)/shard_map/ppermute | solution.py:223
  108.8 6.0 %collective-permute-start.8 = (bf16[2,192,256]{2,1,0:T(8,128)(2,1)S(1)}, bf16[2,192,256]{2,1,0:T(8,128)(2,1)S(1)}, u32[]{:S(2)}, u32[]{:S(2)}) collective-permute-start(bf16[2,192,256]{2,1,0:T(8,128)(2,1)S(1)} %slice.26), channel_id=1, source_target_pairs={{0,96},{16,112},{32,0},{48,16},{64,32},{80,48},{96,64},{112,80},{1... | collective-permute-start | bytes 589832 | tf_op jit(solution)/shard_map/ppermute | solution.py:222
  114.9 0.0 collective-permute-done.10.refs_11_.refs_12_
  114.9 4.2 %shard_map.65.refs_13_ = bf16[4,256,1024]{2,1,0:T(8,128)(2,1)} custom-call(s32[1]{0:T(128)} %bitcast.5.refs_0_, s32[32]{0:T(128)S(1)} %reshape.12.refs_1_, s32[8]{0:T(128)S(1)} %reshape_squeeze.3.refs_2_, s32[8]{0:T(128)S(1)} %reshape.11.refs_3_, bf16[2,384,256]{2,1,0:T(8,128)(2,1)S(1)} %all_gather.3.refs_4_, ...), custom_call_target="tpu_custom_call" | custom-call | flops 805306368 | bytes 1048576 | tf_op jit(solution)/shard_map/pallas_call | solution.py:128
  119.1 0.0 collective-permute-done.9.refs_9_
  119.1 0.0 collective-permute-done.8.refs_8_
  119.1 0.0 collective-permute-done.7.refs_7_
  119.1 0.0 collective-permute-done.6.refs_6_
  119.1 3.5 %shard_map.66 = bf16[4,256,1024]{2,1,0:T(8,128)(2,1)} custom-call(s32[1]{0:T(128)} %bitcast.5.refs_0_, s32[32]{0:T(128)S(1)} %reshape.12.refs_1_, s32[8]{0:T(128)S(1)} %reshape_squeeze.3.refs_2_, s32[8]{0:T(128)S(1)} %reshape.11.refs_3_, bf16[2,384,256]{2,1,0:T(8,128)(2,1)S(1)} %collective-permute-done.3.refs_7_.refs_4_, ...), custom_call_target="tpu_custom_call", output_to_operand_aliasing={{}: (13, {})} | custom-call | flops 805306368 | bytes 1048576 | tf_op jit(solution)/shard_map/pallas_call | solution.py:128
  (5 shorter events, 0.1 us)
Async XLA Ops:
  2.3 14.0 %copy-start = (bf16[1,1,4,256,512]{4,3,2,1,0:T(8,128)(2,1)S(1)}, bf16[1,1,4,256,512]{4,3,2,1,0:T(8,128)(2,1)}, u32[]{:S(2)}) copy-start(bf16[1,1,4,256,512]{4,3,2,1,0:T(8,128)(2,1)} %param.10) | copy-start | bytes 3145732
  2.3 16.0 %copy-start.1 = (s32[1,1,4,2]{2,3,1,0:T(2,128)S(1)}, s32[1,1,4,2]{2,3,1,0:T(2,128)}, u32[]{:S(2)}) copy-start(s32[1,1,4,2]{2,3,1,0:T(2,128)} %param.11) | copy-start | bytes 100
  2.3 18.8 %copy-start.2 = (s32[1,2]{1,0:T(1,128)S(1)}, s32[1,2]{1,0:T(1,128)}, u32[]{:S(2)}) copy-start(s32[1,2]{1,0:T(1,128)} %param.9) | copy-start | bytes 28
  2.3 57.0 %all-to-all-start = ((bf16[32,104,256]{2,1,0:T(8,128)(2,1)}), bf16[32,104,256]{2,1,0:T(8,128)(2,1)}, u32[]{:S(2)}, u32[]{:S(2)}) async-start(bf16[32,104,256]{2,1,0:T(8,128)(2,1)} %shard_map.64), calls=%async_computation | async-start | bytes 3407872 | tf_op jit(solution)/shard_map/all_to_all | solution.py:197
  16.4 14.4 %collective-permute-start.1 = (bf16[4,256,512]{2,1,0:T(8,128)(2,1)S(1)}, bf16[4,256,512]{2,1,0:T(8,128)(2,1)S(1)}, u32[]{:S(2)}, u32[]{:S(2)}) collective-permute-start(bf16[4,256,512]{2,1,0:T(8,128)(2,1)S(1)} %bitcast.24), channel_id=1, source_target_pairs={{1,0},{2,1},{3,2},{4,3},{5,4},{6,5},{7,6},{9,8},{10,9},{11,10},{12... | collective-permute-start | bytes 3145736 | tf_op jit(solution)/shard_map/ppermute | solution.py:205
  18.3 12.3 %collective-permute-start = (s32[4,2]{0,1:T(2,128)S(1)}, s32[4,2]{0,1:T(2,128)S(1)}, u32[]{:S(2)}, u32[]{:S(2)}) collective-permute-start(s32[4,2]{0,1:T(2,128)S(1)} %bitcast.30), channel_id=1, source_target_pairs={{1,0},{2,1},{3,2},{4,3},{5,4},{6,5},{7,6},{8,7},{9,8},{10,9},{11,1... | collective-permute-start | bytes 104 | tf_op jit(solution)/shard_map/ppermute | solution.py:201
  75.3 11.4 %collective-permute-start.4 = (bf16[2,384,256]{2,1,0:T(8,128)(2,1)S(1)}, bf16[2,384,256]{2,1,0:T(8,128)(2,1)S(1)}, u32[]{:S(2)}, u32[]{:S(2)}) collective-permute-start(bf16[2,384,256]{2,1,0:T(8,128)(2,1)S(1)} %all_gather.3.refs_4_), channel_id=1, source_target_pairs={{0,16},{16,32},{32,48},{48,64},{64,80},{80,96},{96,112},{112,0},{1... | collective-permute-start | bytes 1179656 | tf_op jit(solution)/shard_map/ppermute | solution.py:217
  77.8 10.8 %collective-permute-start.2 = (bf16[2,384,256]{2,1,0:T(8,128)(2,1)S(1)}, bf16[2,384,256]{2,1,0:T(8,128)(2,1)S(1)}, u32[]{:S(2)}, u32[]{:S(2)}) collective-permute-start(bf16[2,384,256]{2,1,0:T(8,128)(2,1)S(1)} %all_gather.3.refs_4_), channel_id=1, source_target_pairs={{0,112},{16,0},{32,16},{48,32},{64,48},{80,64},{96,80},{112,96},{1... | collective-permute-start | bytes 1179656 | tf_op jit(solution)/shard_map/ppermute | solution.py:216
  82.3 32.5 %collective-permute-start.10 = (bf16[4,256,512]{2,1,0:T(8,128)(2,1)S(1)}, bf16[4,256,512]{2,1,0:T(8,128)(2,1)S(1)}, u32[]{:S(2)}, u32[]{:S(2)}) collective-permute-start(bf16[4,256,512]{2,1,0:T(8,128)(2,1)S(1)} %bitcast.25), channel_id=1, source_target_pairs={{8,7},{0,15},{24,23},{16,31},{40,39},{32,47},{56,55},{48,63},{72,7... | collective-permute-start | bytes 3145736 | tf_op jit(solution)/shard_map/ppermute | solution.py:212
  86.7 12.5 %collective-permute-start.5 = (bf16[2,384,256]{2,1,0:T(8,128)(2,1)S(1)}, bf16[2,384,256]{2,1,0:T(8,128)(2,1)S(1)}, u32[]{:S(2)}, u32[]{:S(2)}) collective-permute-start(bf16[2,384,256]{2,1,0:T(8,128)(2,1)S(1)} %collective-permute-done.4.refs_6_), channel_id=1, source_target_pairs={{0,16},{16,32},{32,48},{48,64},{64,80},{80,96},{96,112},{112,0},{1... | collective-permute-start | bytes 1179656 | tf_op jit(solution)/shard_map/ppermute | solution.py:217
  88.7 12.6 %collective-permute-start.3 = (bf16[2,384,256]{2,1,0:T(8,128)(2,1)S(1)}, bf16[2,384,256]{2,1,0:T(8,128)(2,1)S(1)}, u32[]{:S(2)}, u32[]{:S(2)}) collective-permute-start(bf16[2,384,256]{2,1,0:T(8,128)(2,1)S(1)} %collective-permute-done.2.refs_5_), channel_id=1, source_target_pairs={{0,112},{16,0},{32,16},{48,32},{64,48},{80,64},{96,80},{112,96},{1... | collective-permute-start | bytes 1179656 | tf_op jit(solution)/shard_map/ppermute | solution.py:216
  99.2 19.9 %collective-permute-start.7 = (bf16[2,384,256]{2,1,0:T(8,128)(2,1)S(1)}, bf16[2,384,256]{2,1,0:T(8,128)(2,1)S(1)}, u32[]{:S(2)}, u32[]{:S(2)}) collective-permute-start(bf16[2,384,256]{2,1,0:T(8,128)(2,1)S(1)} %collective-permute-done.5.refs_8_.refs_5_), channel_id=1, source_target_pairs={{0,16},{16,32},{32,48},{48,64},{64,80},{80,96},{96,112},{112,0},{1... | collective-permute-start | bytes 1179656 | tf_op jit(solution)/shard_map/ppermute | solution.py:217
  101.2 17.9 %collective-permute-start.6 = (bf16[2,384,256]{2,1,0:T(8,128)(2,1)S(1)}, bf16[2,384,256]{2,1,0:T(8,128)(2,1)S(1)}, u32[]{:S(2)}, u32[]{:S(2)}) collective-permute-start(bf16[2,384,256]{2,1,0:T(8,128)(2,1)S(1)} %collective-permute-done.3.refs_7_.refs_4_), channel_id=1, source_target_pairs={{0,112},{16,0},{32,16},{48,32},{64,48},{80,64},{96,80},{112,96},{1... | collective-permute-start | bytes 1179656 | tf_op jit(solution)/shard_map/ppermute | solution.py:216
  106.9 12.2 %collective-permute-start.9 = (bf16[2,192,256]{2,1,0:T(8,128)(2,1)S(1)}, bf16[2,192,256]{2,1,0:T(8,128)(2,1)S(1)}, u32[]{:S(2)}, u32[]{:S(2)}) collective-permute-start(bf16[2,192,256]{2,1,0:T(8,128)(2,1)S(1)} %slice.27), channel_id=1, source_target_pairs={{0,32},{16,48},{32,64},{48,80},{64,96},{80,112},{96,0},{112,16},{1... | collective-permute-start | bytes 589832 | tf_op jit(solution)/shard_map/ppermute | solution.py:223
  108.8 10.3 %collective-permute-start.8 = (bf16[2,192,256]{2,1,0:T(8,128)(2,1)S(1)}, bf16[2,192,256]{2,1,0:T(8,128)(2,1)S(1)}, u32[]{:S(2)}, u32[]{:S(2)}) collective-permute-start(bf16[2,192,256]{2,1,0:T(8,128)(2,1)S(1)} %slice.26), channel_id=1, source_target_pairs={{0,96},{16,112},{32,0},{48,16},{64,32},{80,48},{96,64},{112,80},{1... | collective-permute-start | bytes 589832 | tf_op jit(solution)/shard_map/ppermute | solution.py:222

commit v12 on v11

--- a/solution.py
+++ b/solution.py
@@ -108,7 +108,7 @@
 
 def last_rows(*refs):
     scalars = refs[:4]
-    b2, f2, b3, f3, b4, f4, b_here, b_in, b_over, before, out, acc, o_s, sem = refs[4:]
+    f2, b2, f3, b3, f4, b4, b_here, b_in, b_over, before, out, acc, o_s, sem = refs[4:]
     rows = (
         ((2, (b2, b3)), (-3, (f3, f2))),
         ((4, (f4, b4, f3)), (3, (b3, f4, b4))),
@@ -224,7 +224,7 @@
     b_all = (b_here, b_in, b_over)
     wide = [pltpu.VMEM((2,) + block, jnp.float32), pltpu.VMEM((2, BS, NB * BS), jnp.bfloat16), pltpu.SemaphoreType.DMA((2,))]
     window = call(two_rows, scalars, near + b_all, (), shape, wide, 12)
-    far = near[3:] + (back[3], ahead[3], b4, f4)
+    far = (ahead[2], back[2], ahead[3], back[3], f4, b4)
     window = call(last_rows, scalars, far + b_all, (window,), shape, wide, 12, alias=True)
     return window[None, None]
 

time: 124 us -> 123 us (level)
  the two profiles are of different devices: /device:TPU:6 before, /device:TPU:66 now
where the time goes in v12:
time: 123 us; the launch traced here: 122 us
  starting transfers between devices  45.1 us (37%)
  waiting for transfers between devices  44.8 us (36%)
  blocking collectives  15.4 us (13%)
  Pallas kernels  11 us (9%)
  between operations  3.94 us (3%)
  local copies, waits for them, and re-layouts  1.98 us (2%)
    all_to_all x1, waiting for transfers between devices, on_device(): lax.all_to_all(payload(a_columns[0].transpose(2, 0, 1), a_live[0], tile),...  27.1 us
    all_gather x1, blocking collectives, on_device(): own = lax.all_gather(two[:, :PIECE], 'y_lo', axis=1, tiled=True)  15.4 us
    all_to_all x1, starting transfers between devices, on_device(): lax.all_to_all(payload(a_columns[0].transpose(2, 0, 1), a_live[0], tile),...  13.4 us
    ppermute x3, starting transfers between devices, on_device(): back.append(lax.ppermute(back[-1], 'z', z_route(-1)))  11.9 us
    pallas_call x2, Pallas kernels, call(): pl.pallas_call(kernel, out_shape=out_shape, grid_spec=pltpu.PrefetchScala...  8.7 us
    ppermute x3, waiting for transfers between devices, on_device(): back.append(lax.ppermute(back[-1], 'z', z_route(-1)))  8.27 us
    ppermute x3, starting transfers between devices, on_device(): ahead.append(lax.ppermute(ahead[-1], 'z', z_route(1)))  6.39 us
    ppermute x1, starting transfers between devices, on_device(): b4 = lax.ppermute(back[2][:, SPAN // 2:], 'z', z_route(-2))  5.86 us
  transfers between devices with their start and end apart: 12, of which 5 were waited for; matrix products, arithmetic and copies ran while one was open for 1% of the time, Pallas kernels for 4%

profile of v12, /device:TPU:66, one launch (start us, length us, event | category | flops | bytes accessed | tf_op | source)
XLA Modules:
  0.0 122.2 jit_solution(1159909831798314054)
XLA Ops:
  0.0 2.3 %shard_map.64 = bf16[32,104,256]{2,1,0:T(8,128)(2,1)} custom-call(s32[3,1,4]{2,1,0:T(1,128)} %bitcast.29, s32[1,4]{1,0:T(1,128)} %bitcast.31, bf16[32,96,256]{2,1,0:T(8,128)(2,1)} %bitcast.28), custom_call_target="tpu_custom_call" | custom-call | tf_op jit(solution)/shard_map/pallas_call | solution.py:178
  2.3 0.0 copy-start
  2.3 0.0 copy-start.1
  2.3 0.0 copy-start.2
  2.3 13.4 %all-to-all-start = ((bf16[32,104,256]{2,1,0:T(8,128)(2,1)}), bf16[32,104,256]{2,1,0:T(8,128)(2,1)}, u32[]{:S(2)}, u32[]{:S(2)}) async-start(bf16[32,104,256]{2,1,0:T(8,128)(2,1)} %shard_map.64), calls=%async_computation | async-start | bytes 3407872 | tf_op jit(solution)/shard_map/all_to_all | solution.py:197
  15.7 0.0 copy-done
  15.7 1.9 %collective-permute-start.1 = (bf16[4,256,512]{2,1,0:T(8,128)(2,1)S(1)}, bf16[4,256,512]{2,1,0:T(8,128)(2,1)S(1)}, u32[]{:S(2)}, u32[]{:S(2)}) collective-permute-start(bf16[4,256,512]{2,1,0:T(8,128)(2,1)S(1)} %bitcast.24), channel_id=1, source_target_pairs={{1,0},{2,1},{3,2},{4,3},{5,4},{6,5},{7,6},{9,8},{10,9},{11,10},{12... | collective-permute-start | bytes 3145736 | tf_op jit(solution)/shard_map/ppermute | solution.py:205
  17.6 0.0 copy-done.1
  17.6 2.5 %collective-permute-start = (s32[4,2]{0,1:T(2,128)S(1)}, s32[4,2]{0,1:T(2,128)S(1)}, u32[]{:S(2)}, u32[]{:S(2)}) collective-permute-start(s32[4,2]{0,1:T(2,128)S(1)} %bitcast.30), channel_id=1, source_target_pairs={{1,0},{2,1},{3,2},{4,3},{5,4},{6,5},{7,6},{8,7},{9,8},{10,9},{11,1... | collective-permute-start | bytes 104 | tf_op jit(solution)/shard_map/ppermute | solution.py:201
  20.2 0.0 copy-done.2
  20.2 0.6 fusion.5
  23.4 0.1 copy.10
  23.4 0.1 reshape_squeeze.3.refs_2_
  24.8 5.2 %collective-permute-done = s32[4,2]{0,1:T(2,128)S(1)} collective-permute-done((s32[4,2]{0,1:T(2,128)S(1)}, s32[4,2]{0,1:T(2,128)S(1)}, u32[]{:S(2)}, u32[]{:S(2)}) %collective-permute-start) | collective-permute-done | bytes 64 | tf_op jit(solution)/shard_map/ppermute | solution.py:201
  30.0 0.1 copy.11
  30.1 0.1 reshape.11.refs_3_
  30.1 0.0 collective-permute-done.1.refs_10_.refs_11_
  30.1 27.1 %all-to-all-done = bf16[32,104,256]{2,1,0:T(8,128)(2,1)} async-done(((bf16[32,104,256]{2,1,0:T(8,128)(2,1)}), bf16[32,104,256]{2,1,0:T(8,128)(2,1)}, u32[]{:S(2)}, u32[]{:S(2)}) %all-to-all-start) | async-done | bytes 1703968 | tf_op jit(solution)/shard_map/all_to_all | solution.py:197
  57.2 0.8 constant_dynamic-slice_fusion
  58.1 0.1 reshape.12.refs_1_
  58.2 15.4 %all_gather.3.refs_4_ = bf16[2,384,256]{2,1,0:T(8,128)(2,1)S(1)} all-gather(bf16[2,96,256]{2,1,0:T(8,128)(2,1)S(1)} %fusion), channel_id=1, replica_groups=mesh['y_lo'=4,'z'=8,'y_hi'=2,'x'=4,'core'=2] {'y_lo'}, dimensions={1}, use_global_device_ids=true | all-gather | bytes 491520 | tf_op jit(solution)/shard_map/all_gather | solution.py:210
  73.6 3.3 %collective-permute-start.4 = (bf16[2,384,256]{2,1,0:T(8,128)(2,1)S(1)}, bf16[2,384,256]{2,1,0:T(8,128)(2,1)S(1)}, u32[]{:S(2)}, u32[]{:S(2)}) collective-permute-start(bf16[2,384,256]{2,1,0:T(8,128)(2,1)S(1)} %all_gather.3.refs_4_), channel_id=1, source_target_pairs={{0,112},{16,0},{32,16},{48,32},{64,48},{80,64},{96,80},{112,96},{1... | collective-permute-start | bytes 1179656 | tf_op jit(solution)/shard_map/ppermute | solution.py:216
  76.8 2.5 %collective-permute-start.2 = (bf16[2,384,256]{2,1,0:T(8,128)(2,1)S(1)}, bf16[2,384,256]{2,1,0:T(8,128)(2,1)S(1)}, u32[]{:S(2)}, u32[]{:S(2)}) collective-permute-start(bf16[2,384,256]{2,1,0:T(8,128)(2,1)S(1)} %all_gather.3.refs_4_), channel_id=1, source_target_pairs={{0,16},{16,32},{32,48},{48,64},{64,80},{80,96},{96,112},{112,0},{1... | collective-permute-start | bytes 1179656 | tf_op jit(solution)/shard_map/ppermute | solution.py:217
  79.4 0.7 collective-permute-start.10
  80.1 3.1 %collective-permute-done.4.refs_5_ = bf16[2,384,256]{2,1,0:T(8,128)(2,1)S(1)} collective-permute-done((bf16[2,384,256]{2,1,0:T(8,128)(2,1)S(1)}, bf16[2,384,256]{2,1,0:T(8,128)(2,1)S(1)}, u32[]{:S(2)}, u32[]{:S(2)}) %collective-permute-start.4) | collective-permute-done | bytes 393248 | tf_op jit(solution)/shard_map/ppermute | solution.py:216
  83.3 4.3 %collective-permute-start.5 = (bf16[2,384,256]{2,1,0:T(8,128)(2,1)S(1)}, bf16[2,384,256]{2,1,0:T(8,128)(2,1)S(1)}, u32[]{:S(2)}, u32[]{:S(2)}) collective-permute-start(bf16[2,384,256]{2,1,0:T(8,128)(2,1)S(1)} %collective-permute-done.4.refs_5_), channel_id=1, source_target_pairs={{0,112},{16,0},{32,16},{48,32},{64,48},{80,64},{96,80},{112,96},{1... | collective-permute-start | bytes 1179656 | tf_op jit(solution)/shard_map/ppermute | solution.py:216
  87.5 0.0 collective-permute-done.2.refs_6_
  87.5 1.9 %collective-permute-start.3 = (bf16[2,384,256]{2,1,0:T(8,128)(2,1)S(1)}, bf16[2,384,256]{2,1,0:T(8,128)(2,1)S(1)}, u32[]{:S(2)}, u32[]{:S(2)}) collective-permute-start(bf16[2,384,256]{2,1,0:T(8,128)(2,1)S(1)} %collective-permute-done.2.refs_6_), channel_id=1, source_target_pairs={{0,16},{16,32},{32,48},{48,64},{64,80},{80,96},{96,112},{112,0},{1... | collective-permute-start | bytes 1179656 | tf_op jit(solution)/shard_map/ppermute | solution.py:217
  89.5 5.1 %collective-permute-done.5.refs_7_.refs_5_ = bf16[2,384,256]{2,1,0:T(8,128)(2,1)S(1)} collective-permute-done((bf16[2,384,256]{2,1,0:T(8,128)(2,1)S(1)}, bf16[2,384,256]{2,1,0:T(8,128)(2,1)S(1)}, u32[]{:S(2)}, u32[]{:S(2)}) %collective-permute-start.5) | collective-permute-done | bytes 393248 | tf_op jit(solution)/shard_map/ppermute | solution.py:216
  94.6 4.4 %collective-permute-start.7 = (bf16[2,384,256]{2,1,0:T(8,128)(2,1)S(1)}, bf16[2,384,256]{2,1,0:T(8,128)(2,1)S(1)}, u32[]{:S(2)}, u32[]{:S(2)}) collective-permute-start(bf16[2,384,256]{2,1,0:T(8,128)(2,1)S(1)} %collective-permute-done.5.refs_7_.refs_5_), channel_id=1, source_target_pairs={{0,112},{16,0},{32,16},{48,32},{64,48},{80,64},{96,80},{112,96},{1... | collective-permute-start | bytes 1179656 | tf_op jit(solution)/shard_map/ppermute | solution.py:216
  99.0 0.0 collective-permute-done.3.refs_8_.refs_4_
  99.0 1.9 %collective-permute-start.6 = (bf16[2,384,256]{2,1,0:T(8,128)(2,1)S(1)}, bf16[2,384,256]{2,1,0:T(8,128)(2,1)S(1)}, u32[]{:S(2)}, u32[]{:S(2)}) collective-permute-start(bf16[2,384,256]{2,1,0:T(8,128)(2,1)S(1)} %collective-permute-done.3.refs_8_.refs_4_), channel_id=1, source_target_pairs={{0,16},{16,32},{32,48},{48,64},{64,80},{80,96},{96,112},{112,0},{1... | collective-permute-start | bytes 1179656 | tf_op jit(solution)/shard_map/ppermute | solution.py:217
  101.0 5.9 %collective-permute-start.9 = (bf16[2,192,256]{2,1,0:T(8,128)(2,1)S(1)}, bf16[2,192,256]{2,1,0:T(8,128)(2,1)S(1)}, u32[]{:S(2)}, u32[]{:S(2)}) collective-permute-start(bf16[2,192,256]{2,1,0:T(8,128)(2,1)S(1)} %slice.27), channel_id=1, source_target_pairs={{0,96},{16,112},{32,0},{48,16},{64,32},{80,48},{96,64},{112,80},{1... | collective-permute-start | bytes 589832 | tf_op jit(solution)/shard_map/ppermute | solution.py:222
  106.8 2.4 %collective-permute-start.8 = (bf16[2,192,256]{2,1,0:T(8,128)(2,1)S(1)}, bf16[2,192,256]{2,1,0:T(8,128)(2,1)S(1)}, u32[]{:S(2)}, u32[]{:S(2)}) collective-permute-start(bf16[2,192,256]{2,1,0:T(8,128)(2,1)S(1)} %slice.26), channel_id=1, source_target_pairs={{0,32},{16,48},{32,64},{48,80},{64,96},{80,112},{96,0},{112,16},{1... | collective-permute-start | bytes 589832 | tf_op jit(solution)/shard_map/ppermute | solution.py:223
  109.2 0.0 collective-permute-done.10.refs_11_.refs_12_
  109.2 4.7 %shard_map.65.refs_13_ = bf16[4,256,1024]{2,1,0:T(8,128)(2,1)} custom-call(s32[1]{0:T(128)} %bitcast.5.refs_0_, s32[32]{0:T(128)S(1)} %reshape.12.refs_1_, s32[8]{0:T(128)S(1)} %reshape_squeeze.3.refs_2_, s32[8]{0:T(128)S(1)} %reshape.11.refs_3_, bf16[2,384,256]{2,1,0:T(8,128)(2,1)S(1)} %all_gather.3.refs_4_, ...), custom_call_target="tpu_custom_call" | custom-call | flops 805306368 | bytes 1048576 | tf_op jit(solution)/shard_map/pallas_call | solution.py:128
  113.9 0.0 collective-permute-done.9.refs_9_
  114.0 4.3 %collective-permute-done.8.refs_8_ = bf16[2,192,256]{2,1,0:T(8,128)(2,1)S(1)} collective-permute-done((bf16[2,192,256]{2,1,0:T(8,128)(2,1)S(1)}, bf16[2,192,256]{2,1,0:T(8,128)(2,1)S(1)}, u32[]{:S(2)}, u32[]{:S(2)}) %collective-permute-start.8) | collective-permute-done | bytes 196640 | tf_op jit(solution)/shard_map/ppermute | solution.py:223
  118.2 0.0 collective-permute-done.7.refs_7_
  118.2 0.0 collective-permute-done.6.refs_6_
  118.2 4.0 %shard_map.66 = bf16[4,256,1024]{2,1,0:T(8,128)(2,1)} custom-call(s32[1]{0:T(128)} %bitcast.5.refs_0_, s32[32]{0:T(128)S(1)} %reshape.12.refs_1_, s32[8]{0:T(128)S(1)} %reshape_squeeze.3.refs_2_, s32[8]{0:T(128)S(1)} %reshape.11.refs_3_, bf16[2,384,256]{2,1,0:T(8,128)(2,1)S(1)} %collective-permute-done.3.refs_8_.refs_4_, ...), custom_call_target="tpu_custom_call", output_to_operand_aliasing={{}: (13, {})} | custom-call | flops 805306368 | bytes 1048576 | tf_op jit(solution)/shard_map/pallas_call | solution.py:128
  (5 shorter events, 0.1 us)
Async XLA Ops:
  2.3 13.4 %copy-start = (bf16[1,1,4,256,512]{4,3,2,1,0:T(8,128)(2,1)S(1)}, bf16[1,1,4,256,512]{4,3,2,1,0:T(8,128)(2,1)}, u32[]{:S(2)}) copy-start(bf16[1,1,4,256,512]{4,3,2,1,0:T(8,128)(2,1)} %param.10) | copy-start | bytes 3145732
  2.3 15.3 %copy-start.1 = (s32[1,1,4,2]{2,3,1,0:T(2,128)S(1)}, s32[1,1,4,2]{2,3,1,0:T(2,128)}, u32[]{:S(2)}) copy-start(s32[1,1,4,2]{2,3,1,0:T(2,128)} %param.11) | copy-start | bytes 100
  2.3 17.9 %copy-start.2 = (s32[1,2]{1,0:T(1,128)S(1)}, s32[1,2]{1,0:T(1,128)}, u32[]{:S(2)}) copy-start(s32[1,2]{1,0:T(1,128)} %param.9) | copy-start | bytes 28
  2.3 54.9 %all-to-all-start = ((bf16[32,104,256]{2,1,0:T(8,128)(2,1)}), bf16[32,104,256]{2,1,0:T(8,128)(2,1)}, u32[]{:S(2)}, u32[]{:S(2)}) async-start(bf16[32,104,256]{2,1,0:T(8,128)(2,1)} %shard_map.64), calls=%async_computation | async-start | bytes 3407872 | tf_op jit(solution)/shard_map/all_to_all | solution.py:197
  15.7 14.4 %collective-permute-start.1 = (bf16[4,256,512]{2,1,0:T(8,128)(2,1)S(1)}, bf16[4,256,512]{2,1,0:T(8,128)(2,1)S(1)}, u32[]{:S(2)}, u32[]{:S(2)}) collective-permute-start(bf16[4,256,512]{2,1,0:T(8,128)(2,1)S(1)} %bitcast.24), channel_id=1, source_target_pairs={{1,0},{2,1},{3,2},{4,3},{5,4},{6,5},{7,6},{9,8},{10,9},{11,10},{12... | collective-permute-start | bytes 3145736 | tf_op jit(solution)/shard_map/ppermute | solution.py:205
  17.6 12.3 %collective-permute-start = (s32[4,2]{0,1:T(2,128)S(1)}, s32[4,2]{0,1:T(2,128)S(1)}, u32[]{:S(2)}, u32[]{:S(2)}) collective-permute-start(s32[4,2]{0,1:T(2,128)S(1)} %bitcast.30), channel_id=1, source_target_pairs={{1,0},{2,1},{3,2},{4,3},{5,4},{6,5},{7,6},{8,7},{9,8},{10,9},{11,1... | collective-permute-start | bytes 104 | tf_op jit(solution)/shard_map/ppermute | solution.py:201
  73.6 9.7 %collective-permute-start.4 = (bf16[2,384,256]{2,1,0:T(8,128)(2,1)S(1)}, bf16[2,384,256]{2,1,0:T(8,128)(2,1)S(1)}, u32[]{:S(2)}, u32[]{:S(2)}) collective-permute-start(bf16[2,384,256]{2,1,0:T(8,128)(2,1)S(1)} %all_gather.3.refs_4_), channel_id=1, source_target_pairs={{0,112},{16,0},{32,16},{48,32},{64,48},{80,64},{96,80},{112,96},{1... | collective-permute-start | bytes 1179656 | tf_op jit(solution)/shard_map/ppermute | solution.py:216
  76.8 10.7 %collective-permute-start.2 = (bf16[2,384,256]{2,1,0:T(8,128)(2,1)S(1)}, bf16[2,384,256]{2,1,0:T(8,128)(2,1)S(1)}, u32[]{:S(2)}, u32[]{:S(2)}) collective-permute-start(bf16[2,384,256]{2,1,0:T(8,128)(2,1)S(1)} %all_gather.3.refs_4_), channel_id=1, source_target_pairs={{0,16},{16,32},{32,48},{48,64},{64,80},{80,96},{96,112},{112,0},{1... | collective-permute-start | bytes 1179656 | tf_op jit(solution)/shard_map/ppermute | solution.py:217
  79.4 29.8 %collective-permute-start.10 = (bf16[4,256,512]{2,1,0:T(8,128)(2,1)S(1)}, bf16[4,256,512]{2,1,0:T(8,128)(2,1)S(1)}, u32[]{:S(2)}, u32[]{:S(2)}) collective-permute-start(bf16[4,256,512]{2,1,0:T(8,128)(2,1)S(1)} %bitcast.25), channel_id=1, source_target_pairs={{8,7},{0,15},{24,23},{16,31},{40,39},{32,47},{56,55},{48,63},{72,7... | collective-permute-start | bytes 3145736 | tf_op jit(solution)/shard_map/ppermute | solution.py:212
  83.3 11.3 %collective-permute-start.5 = (bf16[2,384,256]{2,1,0:T(8,128)(2,1)S(1)}, bf16[2,384,256]{2,1,0:T(8,128)(2,1)S(1)}, u32[]{:S(2)}, u32[]{:S(2)}) collective-permute-start(bf16[2,384,256]{2,1,0:T(8,128)(2,1)S(1)} %collective-permute-done.4.refs_5_), channel_id=1, source_target_pairs={{0,112},{16,0},{32,16},{48,32},{64,48},{80,64},{96,80},{112,96},{1... | collective-permute-start | bytes 1179656 | tf_op jit(solution)/shard_map/ppermute | solution.py:216
  87.5 11.5 %collective-permute-start.3 = (bf16[2,384,256]{2,1,0:T(8,128)(2,1)S(1)}, bf16[2,384,256]{2,1,0:T(8,128)(2,1)S(1)}, u32[]{:S(2)}, u32[]{:S(2)}) collective-permute-start(bf16[2,384,256]{2,1,0:T(8,128)(2,1)S(1)} %collective-permute-done.2.refs_6_), channel_id=1, source_target_pairs={{0,16},{16,32},{32,48},{48,64},{64,80},{80,96},{96,112},{112,0},{1... | collective-permute-start | bytes 1179656 | tf_op jit(solution)/shard_map/ppermute | solution.py:217
  94.6 23.6 %collective-permute-start.7 = (bf16[2,384,256]{2,1,0:T(8,128)(2,1)S(1)}, bf16[2,384,256]{2,1,0:T(8,128)(2,1)S(1)}, u32[]{:S(2)}, u32[]{:S(2)}) collective-permute-start(bf16[2,384,256]{2,1,0:T(8,128)(2,1)S(1)} %collective-permute-done.5.refs_7_.refs_5_), channel_id=1, source_target_pairs={{0,112},{16,0},{32,16},{48,32},{64,48},{80,64},{96,80},{112,96},{1... | collective-permute-start | bytes 1179656 | tf_op jit(solution)/shard_map/ppermute | solution.py:216
  99.0 19.2 %collective-permute-start.6 = (bf16[2,384,256]{2,1,0:T(8,128)(2,1)S(1)}, bf16[2,384,256]{2,1,0:T(8,128)(2,1)S(1)}, u32[]{:S(2)}, u32[]{:S(2)}) collective-permute-start(bf16[2,384,256]{2,1,0:T(8,128)(2,1)S(1)} %collective-permute-done.3.refs_8_.refs_4_), channel_id=1, source_target_pairs={{0,16},{16,32},{32,48},{48,64},{64,80},{80,96},{96,112},{112,0},{1... | collective-permute-start | bytes 1179656 | tf_op jit(solution)/shard_map/ppermute | solution.py:217
  101.0 13.0 %collective-permute-start.9 = (bf16[2,192,256]{2,1,0:T(8,128)(2,1)S(1)}, bf16[2,192,256]{2,1,0:T(8,128)(2,1)S(1)}, u32[]{:S(2)}, u32[]{:S(2)}) collective-permute-start(bf16[2,192,256]{2,1,0:T(8,128)(2,1)S(1)} %slice.27), channel_id=1, source_target_pairs={{0,96},{16,112},{32,0},{48,16},{64,32},{80,48},{96,64},{112,80},{1... | collective-permute-start | bytes 589832 | tf_op jit(solution)/shard_map/ppermute | solution.py:222
  106.8 11.4 %collective-permute-start.8 = (bf16[2,192,256]{2,1,0:T(8,128)(2,1)S(1)}, bf16[2,192,256]{2,1,0:T(8,128)(2,1)S(1)}, u32[]{:S(2)}, u32[]{:S(2)}) collective-permute-start(bf16[2,192,256]{2,1,0:T(8,128)(2,1)S(1)} %slice.26), channel_id=1, source_target_pairs={{0,32},{16,48},{32,64},{48,80},{64,96},{80,112},{96,0},{112,16},{1... | collective-permute-start | bytes 589832 | tf_op jit(solution)/shard_map/ppermute | solution.py:223
